TPU v7x, 512 devices: a whole 4x8x8 slice. The times are simulated.
512 devices in a mesh: wide: 64 (over x, y, core), narrow: 8 (over z).
Axes of the slice: x: 4, y: 8, z: 8, core: 2. Of those that a mesh axis runs over, the one named last changes fastest.
Arguments:
- kernel: float32 [32768, 64, 128], P(('wide', 'narrow')), may hold values from 0 to 0.015625
- volume: float32 [32768, 64], P(('wide', 'narrow')), may hold values from 0.5 to 4
- velocity: float32 [32768, 3, 64], P(('wide', 'narrow')), may hold values from -6 to 6
- block_brick: int32 [32768, 1], P(('wide', 'narrow')), may hold values from 0 to 63; in each aligned block of 64 rows (0 to 63, 64 to 127, ...) at most 2 rows name the same one
- block_tile: int32 [32768], P(('wide', 'narrow')), may hold values from 0 to 127
- fluid_velocity: float32 [3, 256, 64, 512], P(None, 'wide', 'narrow'), may hold values from -6 to 6
Outputs:
- particle_drag: float32 [32768, 3, 64], P(('wide', 'narrow'))
- pressure: float32 [256, 64, 512], P('wide', 'narrow')
- fluid_next: float32 [3, 256, 64, 512], P(None, 'wide', 'narrow')
Inputs may be any that keep to these rules, and one draw needn't show every extreme that they name: `block_brick`: among the 64 blocks of one device, at most 2 name the same brick, a bound that some block reaches.
All inputs are finite; a program needn't handle non-finite values.
Results may differ from a plain program's by a relative error of at most 0.00007.
Values sent between devices are 32-bit elements; how exact they have to be, the bound alone decides.
No kernel may reach another device: no remote copies, remote signals or barrier semaphores. Data moves between devices by JAX's collectives and lax.ppermute only.
A program may use at most 64 MiB of HBM per device.

v0:
```python
import jax
import jax.numpy as jnp
from jax import lax
from jax.sharding import PartitionSpec as P

SWEEPS = 6


highest = lax.Precision.HIGHEST


def with_halo(block, sides, width):
    for axis, dim in sides:
        count = lax.axis_size(axis)
        forward = [(i, i + 1) for i in range(count - 1)]
        backward = [(target, source) for source, target in forward]
        low = lax.ppermute(
            lax.slice_in_dim(block, block.shape[dim] - width, None, axis=dim), axis, forward
        )
        high = lax.ppermute(lax.slice_in_dim(block, 0, width, axis=dim), axis, backward)
        block = jnp.concatenate([low, block, high], axis=dim)
    return block


def neighbours(padded):
    return [
        padded[..., 2:, 1:-1, 1:-1],
        padded[..., :-2, 1:-1, 1:-1],
        padded[..., 1:-1, 2:, 1:-1],
        padded[..., 1:-1, :-2, 1:-1],
        padded[..., 1:-1, 1:-1, 2:],
        padded[..., 1:-1, 1:-1, :-2],
    ]


def pad_third(field):
    return jnp.pad(field, ((0, 0), (0, 0), (0, 0), (1, 1)))


def pressure_sides(pressure):
    ghosted = with_halo(pressure[None], (("wide", 1), ("narrow", 2)), 1)
    return [side[0] for side in neighbours(pad_third(ghosted))]


def local(kernel, volume, velocity, block_brick, block_tile, fluid_velocity):
    n_wide = lax.axis_size("wide")
    blocks = kernel.shape[0]
    cells_tile = kernel.shape[2]
    capacity = max(2, (2 * blocks + n_wide - 1) // n_wide)
    slot_count = n_wide * capacity
    extent = fluid_velocity.shape[1:]
    tile_count = extent[0] * extent[1] * extent[2] // cells_tile
    target = block_brick[:, 0]
    matches = (target[:, None] == jnp.arange(n_wide, dtype=jnp.int32)[None, :]).astype(jnp.int32)
    position = jnp.sum((jnp.cumsum(matches, axis=0) - 1) * matches, axis=1)
    placed = target * capacity + position
    carried = jnp.concatenate([volume[:, None, :], volume[:, None, :] * velocity], axis=1)
    tile_number = block_tile.astype(jnp.float32)
    tile_range = jnp.arange(tile_count, dtype=jnp.float32)
    own_sums = jnp.einsum("bkp,bpc->bkc", carried, kernel, precision=highest)
    own_sums = jnp.concatenate(
        [own_sums, jnp.broadcast_to(tile_number[:, None, None], (blocks, 1, cells_tile))], axis=1
    )
    send_sums = jnp.zeros((slot_count, 5, cells_tile), jnp.float32).at[placed].set(own_sums)
    received = lax.all_to_all(
        send_sums.reshape(n_wide, capacity, 5, cells_tile),
        "wide",
        split_axis=0,
        concat_axis=0,
        tiled=True,
    )
    received = received.reshape(slot_count, 5, cells_tile)
    slot_sums = received[:, :4]
    slot_tiles = received[:, 4, 0]
    selector = (slot_tiles[:, None] == tile_range[None, :]).astype(jnp.float32)
    spread = jnp.einsum("st,skc->ktc", selector, slot_sums, precision=highest).reshape(
        (4,) + extent
    )
    solid_share = spread[0]
    momentum = spread[1:]
    growth = (1.0 + solid_share) ** 2
    provisional = (fluid_velocity + growth * momentum) / (1.0 + growth * solid_share)
    void_share = 1.0 / (1.0 + solid_share)
    stacked = jnp.concatenate([void_share * provisional, void_share[None]], axis=0)
    ghosted = with_halo(stacked, (("wide", 1), ("narrow", 2)), 1)
    sides = neighbours(pad_third(ghosted))
    source = -0.5 * (
        sides[0][0] - sides[1][0] + sides[2][1] - sides[3][1] + sides[4][2] - sides[5][2]
    )
    weights = [0.5 * (void_share + side[3]) for side in sides]
    diagonal = weights[0] + weights[1] + weights[2] + weights[3] + weights[4] + weights[5]
    pressure = source / diagonal
    for sweep_index in range(SWEEPS - 1):
        beside_all = pressure_sides(pressure)
        total = source
        for which in range(6):
            total = total + weights[which] * beside_all[which]
        pressure = total / diagonal
    beside_all = pressure_sides(pressure)
    fluid_next = provisional - 0.5 * jnp.stack(
        [
            beside_all[0] - beside_all[1],
            beside_all[2] - beside_all[3],
            beside_all[4] - beside_all[5],
        ]
    )
    coupled = jnp.concatenate([growth * fluid_next, growth[None]], axis=0).reshape(
        4, tile_count, cells_tile
    )
    picked = jnp.einsum("st,ktc->skc", selector, coupled, precision=highest)
    returned = lax.all_to_all(
        picked.reshape(n_wide, capacity, 4, cells_tile),
        "wide",
        split_axis=0,
        concat_axis=0,
        tiled=True,
    )
    block_fields = returned.reshape(slot_count, 4, cells_tile)[placed]
    sampled = jnp.einsum("bkc,bpc->bkp", block_fields, kernel, precision=highest)
    particle_drag = volume[:, None, :] * sampled[:, :3] - carried[:, 1:] * sampled[:, 3:4]
    return (particle_drag, pressure, fluid_next)


def solution(mesh):
    return jax.shard_map(
        local,
        mesh=mesh,
        in_specs=(
            P(("wide", "narrow"), None, None),
            P(("wide", "narrow"), None),
            P(("wide", "narrow"), None, None),
            P(("wide", "narrow"), None),
            P(("wide", "narrow")),
            P(None, "wide", "narrow", None),
        ),
        out_specs=(
            P(("wide", "narrow"), None, None),
            P("wide", "narrow", None),
            P(None, "wide", "narrow", None),
        ),
        check_vma=False,
    )
```

profile of v0, /device:TPU:193, one launch (start us, length us, event | category | flops | bytes accessed | tf_op | source)
XLA Modules:
  0.0 204.0 jit_solution(11152389675427395725)
XLA Ops:
  3.8 1.0 copy_multiply_fusion
  4.8 2.5 %fusion.7 = f32[64,4,128]{2,1,0:T(4,128)S(1)} fusion(f32[64,64,128]{2,1,0:T(8,128)S(1)} %copy-done, f32[64,3,64]{2,1,0:T(4,128)S(1)} %copy_multiply_fusion, f32[64,1,64]{2,1,0:T(1,128)} %bitcast.108), kind=kOutput, calls=%fused_computation.48 | convolution fusion | flops 25182208 | bytes 2293760 | tf_op jit(solution)/shard_map/bkp,bpc->bkc/dot_general | solution.py:60
  7.6 2.4 %scatter_fusion = f32[128,5,128]{2,1,0:T(8,128)S(1)} fusion(f32[128,5,128]{2,1,0:T(8,128)S(1)} %broadcast_in_dim.6, s32[64]{0:T(128)S(1)} %fusion.79, f32[64,5,128]{2,1,0:T(8,128)S(1)} %pad_maximum_fusion), kind=kCustom, calls=%fused_computation.1 | custom fusion | bytes 491776 | tf_op jit(solution)/shard_map/scatter | solution.py:64
  10.2 23.9 %all_to_all.10 = f32[64,2,5,128]{3,1,2,0:T(2,128)S(1)} all-to-all(f32[64,2,5,128]{3,1,2,0:T(2,128)S(1)} %copy.37), channel_id=1, replica_groups=mesh['wide'=64,'narrow'=8] {'wide'}, dimensions={0} | all-to-all | bytes 655360 | tf_op jit(solution)/shard_map/all_to_all | solution.py:65
  37.0 2.3 %collective-permute-start = (f32[4,1,8,512]{3,2,1,0:T(8,128)S(1)}, f32[4,1,8,512]{3,2,1,0:T(8,128)S(1)}, u32[]{:S(2)}, u32[]{:S(2)}) collective-permute-start(f32[4,1,8,512]{3,2,1,0:T(8,128)S(1)} %get-tuple-element.32), channel_id=1, source_target_pairs={{8,0},{16,8},{24,16},{32,24},{40,32},{48,40},{56,48},{64,56},{72,6... | collective-permute-start | bytes 196616 | tf_op jit(solution)/shard_map/ppermute | solution.py:20
  39.3 3.3 %collective-permute-start.1 = (f32[4,1,8,512]{3,2,1,0:T(8,128)S(1)}, f32[4,1,8,512]{3,2,1,0:T(8,128)S(1)}, u32[]{:S(2)}, u32[]{:S(2)}) collective-permute-start(f32[4,1,8,512]{3,2,1,0:T(8,128)S(1)} %get-tuple-element.31), channel_id=1, source_target_pairs={{0,8},{8,16},{16,24},{24,32},{32,40},{40,48},{48,56},{56,64},{64,7... | collective-permute-start | bytes 196616 | tf_op jit(solution)/shard_map/ppermute | solution.py:17
  42.6 1.3 collective-permute-done.1
  43.9 1.9 collective-permute-start.2
  45.8 5.2 %collective-permute-start.3 = (f32[4,6,1,512]{3,2,1,0:T(1,128)S(1)}, f32[4,6,1,512]{3,2,1,0:T(1,128)S(1)}, u32[]{:S(2)}, u32[]{:S(2)}) collective-permute-start(f32[4,6,1,512]{3,2,1,0:T(1,128)S(1)} %get-tuple-element.29), channel_id=1, source_target_pairs={{0,1},{1,2},{2,3},{3,4},{4,5},{5,6},{6,7},{8,9},{9,10},{10,11},{11... | collective-permute-start | bytes 147464 | tf_op jit(solution)/shard_map/ppermute | solution.py:17
  51.1 1.1 collective-permute-done.3
  53.6 1.9 collective-permute-start.4
  55.5 5.1 %collective-permute-start.5 = (f32[1,1,8,512]{3,2,1,0:T(8,128)S(1)}, f32[1,1,8,512]{3,2,1,0:T(8,128)S(1)}, u32[]{:S(2)}, u32[]{:S(2)}) collective-permute-start(f32[1,1,8,512]{3,2,1,0:T(8,128)S(1)} %get-tuple-element.60), channel_id=1, source_target_pairs={{0,8},{8,16},{16,24},{24,32},{32,40},{40,48},{48,56},{56,64},{64,7... | collective-permute-start | bytes 49160 | tf_op jit(solution)/shard_map/ppermute | solution.py:17
  61.5 1.9 collective-permute-start.6
  63.4 5.2 %collective-permute-start.7 = (f32[1,6,1,512]{3,2,1,0:T(1,128)S(1)}, f32[1,6,1,512]{3,2,1,0:T(1,128)S(1)}, u32[]{:S(2)}, u32[]{:S(2)}) collective-permute-start(f32[1,6,1,512]{3,2,1,0:T(1,128)S(1)} %get-tuple-element.48), channel_id=1, source_target_pairs={{0,1},{1,2},{2,3},{3,4},{4,5},{5,6},{6,7},{8,9},{9,10},{10,11},{11... | collective-permute-start | bytes 36872 | tf_op jit(solution)/shard_map/ppermute | solution.py:17
  69.8 1.9 collective-permute-start.8
  71.7 5.1 %collective-permute-start.9 = (f32[1,1,8,512]{3,2,1,0:T(8,128)S(1)}, f32[1,1,8,512]{3,2,1,0:T(8,128)S(1)}, u32[]{:S(2)}, u32[]{:S(2)}) collective-permute-start(f32[1,1,8,512]{3,2,1,0:T(8,128)S(1)} %get-tuple-element.58), channel_id=1, source_target_pairs={{0,8},{8,16},{16,24},{24,32},{32,40},{40,48},{48,56},{56,64},{64,7... | collective-permute-start | bytes 49160 | tf_op jit(solution)/shard_map/ppermute | solution.py:17
  77.6 1.9 collective-permute-start.10
  79.5 5.1 %collective-permute-start.11 = (f32[1,6,1,512]{3,2,1,0:T(1,128)S(1)}, f32[1,6,1,512]{3,2,1,0:T(1,128)S(1)}, u32[]{:S(2)}, u32[]{:S(2)}) collective-permute-start(f32[1,6,1,512]{3,2,1,0:T(1,128)S(1)} %get-tuple-element.46), channel_id=1, source_target_pairs={{0,1},{1,2},{2,3},{3,4},{4,5},{5,6},{6,7},{8,9},{9,10},{10,11},{11... | collective-permute-start | bytes 36872 | tf_op jit(solution)/shard_map/ppermute | solution.py:17
  85.8 1.9 collective-permute-start.12
  87.7 5.1 %collective-permute-start.13 = (f32[1,1,8,512]{3,2,1,0:T(8,128)S(1)}, f32[1,1,8,512]{3,2,1,0:T(8,128)S(1)}, u32[]{:S(2)}, u32[]{:S(2)}) collective-permute-start(f32[1,1,8,512]{3,2,1,0:T(8,128)S(1)} %get-tuple-element.56), channel_id=1, source_target_pairs={{0,8},{8,16},{16,24},{24,32},{32,40},{40,48},{48,56},{56,64},{64,7... | collective-permute-start | bytes 49160 | tf_op jit(solution)/shard_map/ppermute | solution.py:17
  93.7 1.9 collective-permute-start.14
  95.6 5.1 %collective-permute-start.15 = (f32[1,6,1,512]{3,2,1,0:T(1,128)S(1)}, f32[1,6,1,512]{3,2,1,0:T(1,128)S(1)}, u32[]{:S(2)}, u32[]{:S(2)}) collective-permute-start(f32[1,6,1,512]{3,2,1,0:T(1,128)S(1)} %get-tuple-element.44), channel_id=1, source_target_pairs={{0,1},{1,2},{2,3},{3,4},{4,5},{5,6},{6,7},{8,9},{9,10},{10,11},{11... | collective-permute-start | bytes 36872 | tf_op jit(solution)/shard_map/ppermute | solution.py:17
  101.8 1.9 collective-permute-start.16
  103.8 5.1 %collective-permute-start.17 = (f32[1,1,8,512]{3,2,1,0:T(8,128)S(1)}, f32[1,1,8,512]{3,2,1,0:T(8,128)S(1)}, u32[]{:S(2)}, u32[]{:S(2)}) collective-permute-start(f32[1,1,8,512]{3,2,1,0:T(8,128)S(1)} %get-tuple-element.54), channel_id=1, source_target_pairs={{0,8},{8,16},{16,24},{24,32},{32,40},{40,48},{48,56},{56,64},{64,7... | collective-permute-start | bytes 49160 | tf_op jit(solution)/shard_map/ppermute | solution.py:17
  109.7 1.9 collective-permute-start.18
  111.6 5.1 %collective-permute-start.19 = (f32[1,6,1,512]{3,2,1,0:T(1,128)S(1)}, f32[1,6,1,512]{3,2,1,0:T(1,128)S(1)}, u32[]{:S(2)}, u32[]{:S(2)}) collective-permute-start(f32[1,6,1,512]{3,2,1,0:T(1,128)S(1)} %get-tuple-element.42), channel_id=1, source_target_pairs={{0,1},{1,2},{2,3},{3,4},{4,5},{5,6},{6,7},{8,9},{9,10},{10,11},{11... | collective-permute-start | bytes 36872 | tf_op jit(solution)/shard_map/ppermute | solution.py:17
  117.9 1.9 collective-permute-start.20
  119.8 5.1 %collective-permute-start.21 = (f32[1,1,8,512]{3,2,1,0:T(8,128)S(1)}, f32[1,1,8,512]{3,2,1,0:T(8,128)S(1)}, u32[]{:S(2)}, u32[]{:S(2)}) collective-permute-start(f32[1,1,8,512]{3,2,1,0:T(8,128)S(1)} %get-tuple-element.52), channel_id=1, source_target_pairs={{0,8},{8,16},{16,24},{24,32},{32,40},{40,48},{48,56},{56,64},{64,7... | collective-permute-start | bytes 49160 | tf_op jit(solution)/shard_map/ppermute | solution.py:17
  125.8 1.9 collective-permute-start.22
  127.7 5.1 %collective-permute-start.23 = (f32[1,6,1,512]{3,2,1,0:T(1,128)S(1)}, f32[1,6,1,512]{3,2,1,0:T(1,128)S(1)}, u32[]{:S(2)}, u32[]{:S(2)}) collective-permute-start(f32[1,6,1,512]{3,2,1,0:T(1,128)S(1)} %get-tuple-element.40), channel_id=1, source_target_pairs={{0,1},{1,2},{2,3},{3,4},{4,5},{5,6},{6,7},{8,9},{9,10},{10,11},{11... | collective-permute-start | bytes 36872 | tf_op jit(solution)/shard_map/ppermute | solution.py:17
  134.6 5.0 %collective-permute-start.25 = (f32[1,1,8,512]{3,2,1,0:T(8,128)S(1)}, f32[1,1,8,512]{3,2,1,0:T(8,128)S(1)}, u32[]{:S(2)}, u32[]{:S(2)}) collective-permute-start(f32[1,1,8,512]{3,2,1,0:T(8,128)S(1)} %get-tuple-element.50), channel_id=1, source_target_pairs={{0,8},{8,16},{16,24},{24,32},{32,40},{40,48},{48,56},{56,64},{64,7... | collective-permute-start | bytes 49160 | tf_op jit(solution)/shard_map/ppermute | solution.py:17
  139.6 1.9 collective-permute-start.24
  141.6 3.1 %collective-permute-done.24 = f32[1,1,8,512]{3,2,1,0:T(8,128)S(1)} collective-permute-done((f32[1,1,8,512]{3,2,1,0:T(8,128)S(1)}, f32[1,1,8,512]{3,2,1,0:T(8,128)S(1)}, u32[]{:S(2)}, u32[]{:S(2)}) %collective-permute-start.24) | collective-permute-done | bytes 16416 | tf_op jit(solution)/shard_map/ppermute | solution.py:20
  145.3 5.1 %collective-permute-start.27 = (f32[1,6,1,512]{3,2,1,0:T(1,128)}, f32[1,6,1,512]{3,2,1,0:T(1,128)}, u32[]{:S(2)}, u32[]{:S(2)}) collective-permute-start(f32[1,6,1,512]{3,2,1,0:T(1,128)} %get-tuple-element.38), channel_id=1, source_target_pairs={{0,1},{1,2},{2,3},{3,4},{4,5},{5,6},{6,7},{8,9},{9,10},{10,11},{11... | collective-permute-start | bytes 36872 | tf_op jit(solution)/shard_map/ppermute | solution.py:17
  150.5 1.9 collective-permute-start.26
  152.4 1.4 eq.43
  153.8 1.6 copy.44
  155.4 1.4 copy.39
  156.8 1.0 select_maximum_fusion.5
  158.6 1.8 broadcast_multiply_fusion.1
  160.4 0.9 concatenate.190
  161.3 1.2 fusion.1
  163.4 22.1 %all-to-all-start.1 = ((f32[64,2,4,128]{3,2,1,0:T(4,128)}), f32[64,2,4,128]{3,2,1,0:T(4,128)}, u32[]{:S(2)}, u32[]{:S(2)}) async-start(f32[64,2,4,128]{3,2,1,0:T(4,128)} %copy.45), calls=%async_computation.1 | async-start | bytes 524288 | tf_op jit(solution)/shard_map/all_to_all | solution.py:111
  186.2 1.9 fusion.59
  188.0 9.3 %all-to-all-done.1 = f32[64,2,4,128]{3,2,1,0:T(4,128)} async-done(((f32[64,2,4,128]{3,2,1,0:T(4,128)}), f32[64,2,4,128]{3,2,1,0:T(4,128)}, u32[]{:S(2)}, u32[]{:S(2)}) %all-to-all-start.1) | async-done | bytes 262176 | tf_op jit(solution)/shard_map/all_to_all | solution.py:111
  197.3 1.6 gather_fusion
  199.0 3.4 %fusion.90 = f32[64,4,64]{2,1,0:T(4,128)S(1)} fusion(f32[64,4,128]{2,1,0:T(4,128)S(1)} %gather_fusion, f32[64,64,128]{2,1,0:T(8,128)S(1)} %copy-done), kind=kOutput, calls=%fused_computation.261 | convolution fusion | flops 25165824 | bytes 2293760 | tf_op jit(solution)/shard_map/bkc,bpc->bkp/dot_general | solution.py:119
  202.4 1.0 fusion.6
  (106 shorter events, 21.9 us)
Async XLA Ops:
  0.6 4.1 %copy-start = (f32[64,64,128]{2,1,0:T(8,128)S(1)}, f32[64,64,128]{2,1,0:T(8,128)}, u32[]{:S(2)}) copy-start(f32[64,64,128]{2,1,0:T(8,128)} %param.6) | copy-start | bytes 6291460
  3.1 6.9 %copy-start.13 = (s32[64]{0:T(128)}, s32[64]{0:T(128)S(1)}, u32[]{:S(2)}) copy-start(s32[64]{0:T(128)S(1)} %fusion.79) | copy-start | bytes 772
  34.0 2.9 %copy-start.2 = (f32[3,4,8,512]{3,2,1,0:T(8,128)S(1)}, f32[3,4,8,512]{3,2,1,0:T(8,128)}, u32[]{:S(2)}) copy-start(f32[3,4,8,512]{3,2,1,0:T(8,128)} %param.11) | copy-start | bytes 589828
  34.3 0.5 copy-start.12
  36.0 0.6 copy-start.4
  36.0 16.8 %copy-start.3 = (f32[4,8,512]{2,1,0:T(8,128)}, f32[4,8,512]{2,1,0:T(8,128)S(1)}, u32[]{:S(2)}) copy-start(f32[4,8,512]{2,1,0:T(8,128)S(1)} %get-tuple-element.64) | copy-start | bytes 196612
  37.0 5.6 %collective-permute-start = (f32[4,1,8,512]{3,2,1,0:T(8,128)S(1)}, f32[4,1,8,512]{3,2,1,0:T(8,128)S(1)}, u32[]{:S(2)}, u32[]{:S(2)}) collective-permute-start(f32[4,1,8,512]{3,2,1,0:T(8,128)S(1)} %get-tuple-element.32), channel_id=1, source_target_pairs={{8,0},{16,8},{24,16},{32,24},{40,32},{48,40},{56,48},{64,56},{72,6... | collective-permute-start | bytes 196616 | tf_op jit(solution)/shard_map/ppermute | solution.py:20
  39.3 4.6 %collective-permute-start.1 = (f32[4,1,8,512]{3,2,1,0:T(8,128)S(1)}, f32[4,1,8,512]{3,2,1,0:T(8,128)S(1)}, u32[]{:S(2)}, u32[]{:S(2)}) collective-permute-start(f32[4,1,8,512]{3,2,1,0:T(8,128)S(1)} %get-tuple-element.31), channel_id=1, source_target_pairs={{0,8},{8,16},{16,24},{24,32},{32,40},{40,48},{48,56},{56,64},{64,7... | collective-permute-start | bytes 196616 | tf_op jit(solution)/shard_map/ppermute | solution.py:17
  43.9 7.2 %collective-permute-start.2 = (f32[4,6,1,512]{3,2,1,0:T(1,128)S(1)}, f32[4,6,1,512]{3,2,1,0:T(1,128)S(1)}, u32[]{:S(2)}, u32[]{:S(2)}) collective-permute-start(f32[4,6,1,512]{3,2,1,0:T(1,128)S(1)} %get-tuple-element.30), channel_id=1, source_target_pairs={{1,0},{2,1},{3,2},{4,3},{5,4},{6,5},{7,6},{9,8},{10,9},{11,10},{12... | collective-permute-start | bytes 147464 | tf_op jit(solution)/shard_map/ppermute | solution.py:20
  45.8 6.4 %collective-permute-start.3 = (f32[4,6,1,512]{3,2,1,0:T(1,128)S(1)}, f32[4,6,1,512]{3,2,1,0:T(1,128)S(1)}, u32[]{:S(2)}, u32[]{:S(2)}) collective-permute-start(f32[4,6,1,512]{3,2,1,0:T(1,128)S(1)} %get-tuple-element.29), channel_id=1, source_target_pairs={{0,1},{1,2},{2,3},{3,4},{4,5},{5,6},{6,7},{8,9},{9,10},{10,11},{11... | collective-permute-start | bytes 147464 | tf_op jit(solution)/shard_map/ppermute | solution.py:17
  53.6 7.0 %collective-permute-start.4 = (f32[1,1,8,512]{3,2,1,0:T(8,128)S(1)}, f32[1,1,8,512]{3,2,1,0:T(8,128)S(1)}, u32[]{:S(2)}, u32[]{:S(2)}) collective-permute-start(f32[1,1,8,512]{3,2,1,0:T(8,128)S(1)} %get-tuple-element.61), channel_id=1, source_target_pairs={{8,0},{16,8},{24,16},{32,24},{40,32},{48,40},{56,48},{64,56},{72,6... | collective-permute-start | bytes 49160 | tf_op jit(solution)/shard_map/ppermute | solution.py:20
  55.5 6.0 %collective-permute-start.5 = (f32[1,1,8,512]{3,2,1,0:T(8,128)S(1)}, f32[1,1,8,512]{3,2,1,0:T(8,128)S(1)}, u32[]{:S(2)}, u32[]{:S(2)}) collective-permute-start(f32[1,1,8,512]{3,2,1,0:T(8,128)S(1)} %get-tuple-element.60), channel_id=1, source_target_pairs={{0,8},{8,16},{16,24},{24,32},{32,40},{40,48},{48,56},{56,64},{64,7... | collective-permute-start | bytes 49160 | tf_op jit(solution)/shard_map/ppermute | solution.py:17
  61.5 7.1 %collective-permute-start.6 = (f32[1,6,1,512]{3,2,1,0:T(1,128)S(1)}, f32[1,6,1,512]{3,2,1,0:T(1,128)S(1)}, u32[]{:S(2)}, u32[]{:S(2)}) collective-permute-start(f32[1,6,1,512]{3,2,1,0:T(1,128)S(1)} %get-tuple-element.49), channel_id=1, source_target_pairs={{1,0},{2,1},{3,2},{4,3},{5,4},{6,5},{7,6},{9,8},{10,9},{11,10},{12... | collective-permute-start | bytes 36872 | tf_op jit(solution)/shard_map/ppermute | solution.py:20
  63.4 6.0 %collective-permute-start.7 = (f32[1,6,1,512]{3,2,1,0:T(1,128)S(1)}, f32[1,6,1,512]{3,2,1,0:T(1,128)S(1)}, u32[]{:S(2)}, u32[]{:S(2)}) collective-permute-start(f32[1,6,1,512]{3,2,1,0:T(1,128)S(1)} %get-tuple-element.48), channel_id=1, source_target_pairs={{0,1},{1,2},{2,3},{3,4},{4,5},{5,6},{6,7},{8,9},{9,10},{10,11},{11... | collective-permute-start | bytes 36872 | tf_op jit(solution)/shard_map/ppermute | solution.py:17
  69.8 7.0 %collective-permute-start.8 = (f32[1,1,8,512]{3,2,1,0:T(8,128)S(1)}, f32[1,1,8,512]{3,2,1,0:T(8,128)S(1)}, u32[]{:S(2)}, u32[]{:S(2)}) collective-permute-start(f32[1,1,8,512]{3,2,1,0:T(8,128)S(1)} %get-tuple-element.59), channel_id=1, source_target_pairs={{8,0},{16,8},{24,16},{32,24},{40,32},{48,40},{56,48},{64,56},{72,6... | collective-permute-start | bytes 49160 | tf_op jit(solution)/shard_map/ppermute | solution.py:20
  71.7 5.9 %collective-permute-start.9 = (f32[1,1,8,512]{3,2,1,0:T(8,128)S(1)}, f32[1,1,8,512]{3,2,1,0:T(8,128)S(1)}, u32[]{:S(2)}, u32[]{:S(2)}) collective-permute-start(f32[1,1,8,512]{3,2,1,0:T(8,128)S(1)} %get-tuple-element.58), channel_id=1, source_target_pairs={{0,8},{8,16},{16,24},{24,32},{32,40},{40,48},{48,56},{56,64},{64,7... | collective-permute-start | bytes 49160 | tf_op jit(solution)/shard_map/ppermute | solution.py:17
  77.6 7.1 %collective-permute-start.10 = (f32[1,6,1,512]{3,2,1,0:T(1,128)S(1)}, f32[1,6,1,512]{3,2,1,0:T(1,128)S(1)}, u32[]{:S(2)}, u32[]{:S(2)}) collective-permute-start(f32[1,6,1,512]{3,2,1,0:T(1,128)S(1)} %get-tuple-element.47), channel_id=1, source_target_pairs={{1,0},{2,1},{3,2},{4,3},{5,4},{6,5},{7,6},{9,8},{10,9},{11,10},{12... | collective-permute-start | bytes 36872 | tf_op jit(solution)/shard_map/ppermute | solution.py:20
  79.5 5.9 %collective-permute-start.11 = (f32[1,6,1,512]{3,2,1,0:T(1,128)S(1)}, f32[1,6,1,512]{3,2,1,0:T(1,128)S(1)}, u32[]{:S(2)}, u32[]{:S(2)}) collective-permute-start(f32[1,6,1,512]{3,2,1,0:T(1,128)S(1)} %get-tuple-element.46), channel_id=1, source_target_pairs={{0,1},{1,2},{2,3},{3,4},{4,5},{5,6},{6,7},{8,9},{9,10},{10,11},{11... | collective-permute-start | bytes 36872 | tf_op jit(solution)/shard_map/ppermute | solution.py:17
  85.8 7.0 %collective-permute-start.12 = (f32[1,1,8,512]{3,2,1,0:T(8,128)S(1)}, f32[1,1,8,512]{3,2,1,0:T(8,128)S(1)}, u32[]{:S(2)}, u32[]{:S(2)}) collective-permute-start(f32[1,1,8,512]{3,2,1,0:T(8,128)S(1)} %get-tuple-element.57), channel_id=1, source_target_pairs={{8,0},{16,8},{24,16},{32,24},{40,32},{48,40},{56,48},{64,56},{72,6... | collective-permute-start | bytes 49160 | tf_op jit(solution)/shard_map/ppermute | solution.py:20
  87.7 5.9 %collective-permute-start.13 = (f32[1,1,8,512]{3,2,1,0:T(8,128)S(1)}, f32[1,1,8,512]{3,2,1,0:T(8,128)S(1)}, u32[]{:S(2)}, u32[]{:S(2)}) collective-permute-start(f32[1,1,8,512]{3,2,1,0:T(8,128)S(1)} %get-tuple-element.56), channel_id=1, source_target_pairs={{0,8},{8,16},{16,24},{24,32},{32,40},{40,48},{48,56},{56,64},{64,7... | collective-permute-start | bytes 49160 | tf_op jit(solution)/shard_map/ppermute | solution.py:17
  93.7 7.1 %collective-permute-start.14 = (f32[1,6,1,512]{3,2,1,0:T(1,128)S(1)}, f32[1,6,1,512]{3,2,1,0:T(1,128)S(1)}, u32[]{:S(2)}, u32[]{:S(2)}) collective-permute-start(f32[1,6,1,512]{3,2,1,0:T(1,128)S(1)} %get-tuple-element.45), channel_id=1, source_target_pairs={{1,0},{2,1},{3,2},{4,3},{5,4},{6,5},{7,6},{9,8},{10,9},{11,10},{12... | collective-permute-start | bytes 36872 | tf_op jit(solution)/shard_map/ppermute | solution.py:20
  95.6 5.9 %collective-permute-start.15 = (f32[1,6,1,512]{3,2,1,0:T(1,128)S(1)}, f32[1,6,1,512]{3,2,1,0:T(1,128)S(1)}, u32[]{:S(2)}, u32[]{:S(2)}) collective-permute-start(f32[1,6,1,512]{3,2,1,0:T(1,128)S(1)} %get-tuple-element.44), channel_id=1, source_target_pairs={{0,1},{1,2},{2,3},{3,4},{4,5},{5,6},{6,7},{8,9},{9,10},{10,11},{11... | collective-permute-start | bytes 36872 | tf_op jit(solution)/shard_map/ppermute | solution.py:17
  101.8 7.0 %collective-permute-start.16 = (f32[1,1,8,512]{3,2,1,0:T(8,128)S(1)}, f32[1,1,8,512]{3,2,1,0:T(8,128)S(1)}, u32[]{:S(2)}, u32[]{:S(2)}) collective-permute-start(f32[1,1,8,512]{3,2,1,0:T(8,128)S(1)} %get-tuple-element.55), channel_id=1, source_target_pairs={{8,0},{16,8},{24,16},{32,24},{40,32},{48,40},{56,48},{64,56},{72,6... | collective-permute-start | bytes 49160 | tf_op jit(solution)/shard_map/ppermute | solution.py:20
  103.8 5.9 %collective-permute-start.17 = (f32[1,1,8,512]{3,2,1,0:T(8,128)S(1)}, f32[1,1,8,512]{3,2,1,0:T(8,128)S(1)}, u32[]{:S(2)}, u32[]{:S(2)}) collective-permute-start(f32[1,1,8,512]{3,2,1,0:T(8,128)S(1)} %get-tuple-element.54), channel_id=1, source_target_pairs={{0,8},{8,16},{16,24},{24,32},{32,40},{40,48},{48,56},{56,64},{64,7... | collective-permute-start | bytes 49160 | tf_op jit(solution)/shard_map/ppermute | solution.py:17
  109.7 7.1 %collective-permute-start.18 = (f32[1,6,1,512]{3,2,1,0:T(1,128)S(1)}, f32[1,6,1,512]{3,2,1,0:T(1,128)S(1)}, u32[]{:S(2)}, u32[]{:S(2)}) collective-permute-start(f32[1,6,1,512]{3,2,1,0:T(1,128)S(1)} %get-tuple-element.43), channel_id=1, source_target_pairs={{1,0},{2,1},{3,2},{4,3},{5,4},{6,5},{7,6},{9,8},{10,9},{11,10},{12... | collective-permute-start | bytes 36872 | tf_op jit(solution)/shard_map/ppermute | solution.py:20
  111.6 5.9 %collective-permute-start.19 = (f32[1,6,1,512]{3,2,1,0:T(1,128)S(1)}, f32[1,6,1,512]{3,2,1,0:T(1,128)S(1)}, u32[]{:S(2)}, u32[]{:S(2)}) collective-permute-start(f32[1,6,1,512]{3,2,1,0:T(1,128)S(1)} %get-tuple-element.42), channel_id=1, source_target_pairs={{0,1},{1,2},{2,3},{3,4},{4,5},{5,6},{6,7},{8,9},{9,10},{10,11},{11... | collective-permute-start | bytes 36872 | tf_op jit(solution)/shard_map/ppermute | solution.py:17
  117.9 7.0 %collective-permute-start.20 = (f32[1,1,8,512]{3,2,1,0:T(8,128)S(1)}, f32[1,1,8,512]{3,2,1,0:T(8,128)S(1)}, u32[]{:S(2)}, u32[]{:S(2)}) collective-permute-start(f32[1,1,8,512]{3,2,1,0:T(8,128)S(1)} %get-tuple-element.53), channel_id=1, source_target_pairs={{8,0},{16,8},{24,16},{32,24},{40,32},{48,40},{56,48},{64,56},{72,6... | collective-permute-start | bytes 49160 | tf_op jit(solution)/shard_map/ppermute | solution.py:20
  119.8 5.9 %collective-permute-start.21 = (f32[1,1,8,512]{3,2,1,0:T(8,128)S(1)}, f32[1,1,8,512]{3,2,1,0:T(8,128)S(1)}, u32[]{:S(2)}, u32[]{:S(2)}) collective-permute-start(f32[1,1,8,512]{3,2,1,0:T(8,128)S(1)} %get-tuple-element.52), channel_id=1, source_target_pairs={{0,8},{8,16},{16,24},{24,32},{32,40},{40,48},{48,56},{56,64},{64,7... | collective-permute-start | bytes 49160 | tf_op jit(solution)/shard_map/ppermute | solution.py:17
  125.7 8.8 %copy-start.7 = (f32[1,1,8,512]{3,2,1,0:T(8,128)}, f32[1,1,8,512]{3,2,1,0:T(8,128)S(1)}, u32[]{:S(2)}) copy-start(f32[1,1,8,512]{3,2,1,0:T(8,128)S(1)} %collective-permute-done.21) | copy-start | bytes 49156
  125.8 7.1 %collective-permute-start.22 = (f32[1,6,1,512]{3,2,1,0:T(1,128)S(1)}, f32[1,6,1,512]{3,2,1,0:T(1,128)S(1)}, u32[]{:S(2)}, u32[]{:S(2)}) collective-permute-start(f32[1,6,1,512]{3,2,1,0:T(1,128)S(1)} %get-tuple-element.41), channel_id=1, source_target_pairs={{1,0},{2,1},{3,2},{4,3},{5,4},{6,5},{7,6},{9,8},{10,9},{11,10},{12... | collective-permute-start | bytes 36872 | tf_op jit(solution)/shard_map/ppermute | solution.py:20
  127.7 5.9 %collective-permute-start.23 = (f32[1,6,1,512]{3,2,1,0:T(1,128)S(1)}, f32[1,6,1,512]{3,2,1,0:T(1,128)S(1)}, u32[]{:S(2)}, u32[]{:S(2)}) collective-permute-start(f32[1,6,1,512]{3,2,1,0:T(1,128)S(1)} %get-tuple-element.40), channel_id=1, source_target_pairs={{0,1},{1,2},{2,3},{3,4},{4,5},{5,6},{6,7},{8,9},{9,10},{10,11},{11... | collective-permute-start | bytes 36872 | tf_op jit(solution)/shard_map/ppermute | solution.py:17
  132.8 12.5 %copy-start.10 = (f32[1,6,1,512]{3,2,1,0:T(1,128)}, f32[1,6,1,512]{3,2,1,0:T(1,128)S(1)}, u32[]{:S(2)}) copy-start(f32[1,6,1,512]{3,2,1,0:T(1,128)S(1)} %collective-permute-done.22) | copy-start | bytes 36868
  133.6 16.8 %copy-start.11 = (f32[1,6,1,512]{3,2,1,0:T(1,128)}, f32[1,6,1,512]{3,2,1,0:T(1,128)S(1)}, u32[]{:S(2)}) copy-start(f32[1,6,1,512]{3,2,1,0:T(1,128)S(1)} %collective-permute-done.23) | copy-start | bytes 36868
  133.8 0.7 copy-start.1
  134.6 7.0 %collective-permute-start.25 = (f32[1,1,8,512]{3,2,1,0:T(8,128)S(1)}, f32[1,1,8,512]{3,2,1,0:T(8,128)S(1)}, u32[]{:S(2)}, u32[]{:S(2)}) collective-permute-start(f32[1,1,8,512]{3,2,1,0:T(8,128)S(1)} %get-tuple-element.50), channel_id=1, source_target_pairs={{0,8},{8,16},{16,24},{24,32},{32,40},{40,48},{48,56},{56,64},{64,7... | collective-permute-start | bytes 49160 | tf_op jit(solution)/shard_map/ppermute | solution.py:17
  139.6 5.1 %collective-permute-start.24 = (f32[1,1,8,512]{3,2,1,0:T(8,128)S(1)}, f32[1,1,8,512]{3,2,1,0:T(8,128)S(1)}, u32[]{:S(2)}, u32[]{:S(2)}) collective-permute-start(f32[1,1,8,512]{3,2,1,0:T(8,128)S(1)} %get-tuple-element.51), channel_id=1, source_target_pairs={{8,0},{16,8},{24,16},{32,24},{40,32},{48,40},{56,48},{64,56},{72,6... | collective-permute-start | bytes 49160 | tf_op jit(solution)/shard_map/ppermute | solution.py:20
  141.6 3.1 %copy-start.8 = (f32[1,1,8,512]{3,2,1,0:T(8,128)}, f32[1,1,8,512]{3,2,1,0:T(8,128)S(1)}, u32[]{:S(2)}) copy-start(f32[1,1,8,512]{3,2,1,0:T(8,128)S(1)} %collective-permute-done.25) | copy-start | bytes 49156
  144.7 0.6 copy-start.9
  145.3 11.4 %collective-permute-start.27 = (f32[1,6,1,512]{3,2,1,0:T(1,128)}, f32[1,6,1,512]{3,2,1,0:T(1,128)}, u32[]{:S(2)}, u32[]{:S(2)}) collective-permute-start(f32[1,6,1,512]{3,2,1,0:T(1,128)} %get-tuple-element.38), channel_id=1, source_target_pairs={{0,1},{1,2},{2,3},{3,4},{4,5},{5,6},{6,7},{8,9},{9,10},{10,11},{11... | collective-permute-start | bytes 36872 | tf_op jit(solution)/shard_map/ppermute | solution.py:17
  150.5 6.3 %collective-permute-start.26 = (f32[1,6,1,512]{3,2,1,0:T(1,128)}, f32[1,6,1,512]{3,2,1,0:T(1,128)}, u32[]{:S(2)}, u32[]{:S(2)}) collective-permute-start(f32[1,6,1,512]{3,2,1,0:T(1,128)} %get-tuple-element.39), channel_id=1, source_target_pairs={{1,0},{2,1},{3,2},{4,3},{5,4},{6,5},{7,6},{9,8},{10,9},{11,10},{12... | collective-permute-start | bytes 36872 | tf_op jit(solution)/shard_map/ppermute | solution.py:20
  158.6 27.6 %copy-start.5 = (f32[4,8,512]{2,1,0:T(8,128)S(1)}, f32[4,8,512]{2,1,0:T(8,128)}, u32[]{:S(2)}) copy-start(f32[4,8,512]{2,1,0:T(8,128)} %copy-done.4) | copy-start | bytes 196612
  163.4 39.0 %copy-start.6 = (f32[64,64]{1,0:T(8,128)S(1)}, f32[64,64]{1,0:T(8,128)}, u32[]{:S(2)}) copy-start(f32[64,64]{1,0:T(8,128)} %param.7) | copy-start | bytes 49156
  163.4 34.0 %all-to-all-start.1 = ((f32[64,2,4,128]{3,2,1,0:T(4,128)}), f32[64,2,4,128]{3,2,1,0:T(4,128)}, u32[]{:S(2)}, u32[]{:S(2)}) async-start(f32[64,2,4,128]{3,2,1,0:T(4,128)} %copy.45), calls=%async_computation.1 | async-start | bytes 524288 | tf_op jit(solution)/shard_map/all_to_all | solution.py:111
where the time goes:
time: 206 us; the launch traced here: 204 us
  starting transfers between devices  119 us (58%)
  blocking collectives  23.9 us (12%)
  waiting for transfers between devices  23.1 us (11%)
  other arithmetic  15.7 us (8%)
  local copies, waits for them, and re-layouts  13.6 us (7%)
  matrix products  7.47 us (4%)
    ppermute x14, starting transfers between devices, with_halo(): lax.ppermute(lax.slice_in_dim(block, block.shape[dim] - width, None, axis...  69.7 us
    ppermute x14, starting transfers between devices, with_halo(): lax.ppermute(lax.slice_in_dim(block, 0, width, axis=dim), axis, backward)  27.3 us
    all_to_all x1, blocking collectives, local(): lax.all_to_all(send_sums.reshape(n_wide, capacity, 5, cells_tile), 'wide'...  23.9 us
    all_to_all x1, starting transfers between devices, local(): lax.all_to_all(picked.reshape(n_wide, capacity, 4, cells_tile), 'wide', s...  22.1 us
    ppermute x14, waiting for transfers between devices, with_halo(): lax.ppermute(lax.slice_in_dim(block, block.shape[dim] - width, None, axis...  10.6 us
    all_to_all x1, waiting for transfers between devices, local(): lax.all_to_all(picked.reshape(n_wide, capacity, 4, cells_tile), 'wide', s...  9.3 us
  transfers between devices with their start and end apart: 29, of which 14 were waited for; matrix products, arithmetic and copies ran while one was open for 3% of the time, Pallas kernels for 0%

commit v1 on v0

v1 whole, which is shorter than its diff:
```python
import functools

import jax
import jax.numpy as jnp
from jax import lax
from jax.experimental import pallas as pl
from jax.experimental.pallas import tpu as pltpu
from jax.sharding import PartitionSpec as P

SWEEPS = 6
DEPTH = SWEEPS + 1
CX, CZ, NY = 4, 8, 512
XS = 2 * CX
XE = XS + 2 * DEPTH
CELLS = 128
SLOTS = 4
KEYS = 4 * SLOTS + 1

highest = lax.Precision.HIGHEST
f32 = jnp.float32


def iota(shape, dim):
    return lax.broadcasted_iota(jnp.int32, shape, dim)


def split3(x):
    hi = x.astype(jnp.bfloat16)
    rest = x - hi.astype(f32)
    mid = rest.astype(jnp.bfloat16)
    low = (rest - mid.astype(f32)).astype(jnp.bfloat16)
    return hi, mid, low


def prev_y(x):
    return jnp.where(iota(x.shape, x.ndim - 1) == 0, 0.0, pltpu.roll(x, 1, x.ndim - 1))


def next_y(x):
    return jnp.where(iota(x.shape, x.ndim - 1) == NY - 1, 0.0, pltpu.roll(x, NY - 1, x.ndim - 1))


def pack_kernel(brick_ref, tile_ref, sums_ref, send_ref, placed_ref, count_ref):
    blocks = sums_ref.shape[0]
    send_ref[...] = jnp.zeros_like(send_ref)

    def clear(i, _):
        count_ref[i] = 0
        return 0

    lax.fori_loop(0, count_ref.shape[0], clear, 0)
    lane = iota((1, CELLS), 1)

    def body(b, _):
        brick = brick_ref[b]
        position = count_ref[brick]
        count_ref[brick] = position + 1
        chip = brick // 2
        slot = (brick % 2) * 2 + position
        placed_ref[b] = chip * SLOTS + slot
        row = chip * KEYS + slot * 4
        for k in range(4):
            send_ref[pl.ds(row + k, 1), :] = sums_ref[b, pl.ds(k, 1), :]
        keys = pl.ds(chip * KEYS + 4 * SLOTS, 1)
        send_ref[keys, :] = jnp.where(lane == slot, tile_ref[b].astype(f32), send_ref[keys, :])
        return 0

    lax.fori_loop(0, blocks, body, 0)


def spread_kernel(recv_ref, fluid_ref, out_ref, pick_ref):
    chips = recv_ref.shape[0] // KEYS
    tiles = recv_ref[pl.ds(4 * SLOTS, chips, stride=KEYS), :].astype(jnp.int32)
    rows = (tiles >> 5) * 32 + (tiles & 3) * 8 + ((tiles >> 2) & 7)
    cells = iota((chips, XS * 32), 1)
    for j in range(SLOTS):
        mine = rows[:, j : j + 1] + (j // 2) * 128
        pick_ref[pl.ds(j * chips, chips), :] = (cells == mine).astype(f32)
    pick = pick_ref[...].astype(jnp.bfloat16)
    for k in range(4):
        sums = jnp.concatenate(
            [recv_ref[pl.ds(j * 4 + k, chips, stride=KEYS), :] for j in range(SLOTS)], axis=0
        )
        total = jnp.zeros((XS * 32, CELLS), f32)
        for part in split3(sums):
            total += lax.dot_general(
                pick, part, (((0,), (0,)), ((), ())), preferred_element_type=f32
            )
        for x in range(XS):
            for q in range(4):
                out_ref[k * XS + x, :, q * 128 : (q + 1) * 128] = total[
                    x * 32 + q * 8 : x * 32 + q * 8 + 8, :
                ]
    out_ref[4 * XS :] = fluid_ref[...].reshape(3 * CX, CZ, NY)


def fields_kernel(core_ref, own_ref, other_ref, field_ref, aux_ref, send_ref):
    core = core_ref[0]
    for x in range(XS):
        sums = [own_ref[k * XS + x] + other_ref[k * XS + x] for k in range(4)]
        mine = core == x // CX
        fluid = [
            jnp.where(
                mine, own_ref[4 * XS + a * CX + x % CX], other_ref[4 * XS + a * CX + x % CX]
            )
            for a in range(3)
        ]
        solid = sums[0]
        growth = (1.0 + solid) ** 2
        void = 1.0 / (1.0 + solid)
        scale = 1.0 / (1.0 + growth * solid)
        provisional = [(fluid[a] + growth * sums[1 + a]) * scale for a in range(3)]
        field_ref[x] = void
        for a in range(3):
            field_ref[(1 + a) * XS + x] = void * provisional[a]
            aux_ref[a * XS + x] = provisional[a]
        aux_ref[3 * XS + x] = growth
    for f in range(4):
        send_ref[f * DEPTH : (f + 1) * DEPTH] = field_ref[pl.ds(f * XS + 1 - core, DEPTH)]


ROWS_S = XE - 2


def source_kernel(core_ref, field_ref, recv_ref, swap_ref, send_ref, face_ref):
    core = core_ref[0]
    first = core == 0

    def row(f, r):
        if r < DEPTH:
            return jnp.where(first, recv_ref[f * DEPTH + r], swap_ref[f * DEPTH + r])
        if r < DEPTH + XS:
            return field_ref[f * XS + r - DEPTH]
        i = f * DEPTH + r - DEPTH - XS
        return jnp.where(first, swap_ref[i], recv_ref[i])

    for r in range(XE):
        send_ref[r] = row(0, r)
    face_ref[...] = jnp.zeros_like(face_ref)
    send_ref[XE + ROWS_S :] = jnp.zeros((3, CZ, NY), f32)
    z = iota((CZ, NY), 0)
    for i in range(ROWS_S):
        r = i + 1
        along_x = row(1, r + 1) - row(1, r - 1)
        vz = row(2, r)
        along_z = jnp.where(z == CZ - 1, 0.0, pltpu.roll(vz, CZ - 1, 0)) - jnp.where(
            z == 0, 0.0, pltpu.roll(vz, 1, 0)
        )
        vy = row(3, r)
        along_y = next_y(vy) - prev_y(vy)
        send_ref[XE + i] = -0.5 * (along_x + along_z + along_y)
        low, high = vz[0:1], vz[CZ - 1 : CZ]
        face_ref[i // 8, i % 8 : i % 8 + 1, :] = low
        face_ref[3 + i // 8, i % 8 : i % 8 + 1, :] = high
        send_ref[XE + ROWS_S + i // 8, i % 8 : i % 8 + 1, :] = jnp.where(first, high, low)


def solve_kernel(
    core_ref, own_ref, face_ref, recv_ref, swap_ref, aux_ref, pick_ref,
    pressure_ref, next_ref, send_ref,
    v, s, wx, wy, wz, inv, pa, pb, coupled,
):
    core = core_ref[0]
    first = core == 0
    mid = pl.ds(CZ, CZ)

    def assemble(r, _):
        here, there = recv_ref[r], swap_ref[r]
        v[r, 0:CZ] = jnp.where(first, here, there)
        v[r, CZ : 2 * CZ] = own_ref[r]
        v[r, 2 * CZ :] = jnp.where(first, there, here)
        return 0

    lax.fori_loop(0, XE, assemble, 0)

    for i in range(ROWS_S):
        r = i + 1
        here, there = recv_ref[XE + i], swap_ref[XE + i]
        s[r, 0:CZ] = jnp.where(first, here, there)
        s[r, CZ : 2 * CZ] = own_ref[XE + i]
        s[r, 2 * CZ :] = jnp.where(first, there, here)
        tile, sub = i // 8, i % 8
        line = slice(sub, sub + 1)
        one = recv_ref[XE + ROWS_S + tile, line, :]
        two = swap_ref[XE + ROWS_S + tile, line, :]
        below, above = jnp.where(first, one, two), jnp.where(first, two, one)
        own_low, own_high = face_ref[tile, line, :], face_ref[3 + tile, line, :]
        s[r, CZ - 1 : CZ] += -0.5 * own_low
        s[r, CZ : CZ + 1] += 0.5 * below
        s[r, 2 * CZ - 1 : 2 * CZ] += -0.5 * above
        s[r, 2 * CZ : 2 * CZ + 1] += 0.5 * own_high

    last = iota((3 * CZ, NY), 1) == NY - 1

    def weights(r, _):
        c = v[r]
        up = next_y(c)
        over = pltpu.roll(c, 3 * CZ - 1, 0)
        diagonal = 3.0 * c + 0.5 * (
            (v[r + 1] + v[r - 1]) + (up + prev_y(c)) + (over + pltpu.roll(c, 1, 0))
        )
        i = jnp.where(c > 0.0, 1.0 / jnp.where(c > 0.0, diagonal, 1.0), 0.0)
        wx[r] = 0.5 * (c + v[r + 1])
        wy[r] = jnp.where(last, 0.0, 0.5 * (c + up))
        wz[r] = 0.5 * (c + over)
        inv[r] = i
        p = s[r] * i
        s[r] = p
        pa[r] = p
        return 0

    lax.fori_loop(1, XE - 1, weights, 0)

    def sweep(src, dst, reach):
        def body(r, _):
            p = src[r]
            y = wy[r]
            z = wz[r]
            acc = wx[r] * src[r + 1] + wx[r - 1] * src[r - 1]
            acc += y * pltpu.roll(p, NY - 1, 1) + pltpu.roll(y * p, 1, 1)
            acc += z * pltpu.roll(p, 3 * CZ - 1, 0) + pltpu.roll(z * p, 1, 0)
            dst[r] = s[r] + inv[r] * acc
            return 0

        lax.fori_loop(DEPTH - reach, DEPTH + XS + reach, body, 0)

    src, dst = pa, pb
    for k in range(1, SWEEPS):
        sweep(src, dst, SWEEPS - k)
        src, dst = dst, src

    for i in range(CX):
        pressure_ref[i] = src[DEPTH + core * CX + i, mid, :]

    for x in range(XS):
        r = DEPTH + x
        p = src[r]
        growth = aux_ref[3 * XS + x]
        diffs = [
            src[r + 1, mid, :] - src[r - 1, mid, :],
            (pltpu.roll(p, 3 * CZ - 1, 0) - pltpu.roll(p, 1, 0))[CZ : 2 * CZ],
            next_y(p[CZ : 2 * CZ]) - prev_y(p[CZ : 2 * CZ]),
        ]
        for a in range(3):
            value = aux_ref[a * XS + x] - 0.5 * diffs[a]
            out = growth * value

            @pl.when(core == x // CX)
            def _(a=a, x=x, value=value):
                next_ref[a, x % CX] = value

            for q in range(4):
                coupled[pl.ds(x * 32 + q * 8, 8), a * 128 : (a + 1) * 128] = out[
                    :, q * 128 : (q + 1) * 128
                ]
        for q in range(4):
            coupled[pl.ds(x * 32 + q * 8, 8), 3 * 128 : 4 * 128] = growth[
                :, q * 128 : (q + 1) * 128
            ]

    pick = pick_ref[...].astype(jnp.bfloat16)
    chips = pick.shape[0] // SLOTS
    for k in range(4):
        total = jnp.zeros((pick.shape[0], CELLS), f32)
        for part in split3(coupled[:, k * 128 : (k + 1) * 128]):
            total += jnp.dot(pick, part, preferred_element_type=f32)
        for j in range(SLOTS):
            send_ref[pl.ds(j * 4 + k, chips, stride=4 * SLOTS), :] = total[
                j * chips : (j + 1) * chips, :
            ]


def gather_kernel(placed_ref, back_ref, out_ref):
    def body(b, _):
        row = placed_ref[b] * 4
        for k in range(4):
            out_ref[b, pl.ds(k, 1), :] = back_ref[pl.ds(row + k, 1), :]
        return 0

    lax.fori_loop(0, out_ref.shape[0], body, 0)


VMEM = pl.BlockSpec(memory_space=pltpu.VMEM)
SMEM = pl.BlockSpec(memory_space=pltpu.SMEM)


def call(kernel, ins, outs, *args, scratch=(), name=None):
    return pl.pallas_call(
        kernel,
        out_shape=[shape for shape, _ in outs],
        in_specs=ins,
        out_specs=[spec for _, spec in outs],
        scratch_shapes=scratch,
        name=name,
        compiler_params=pltpu.CompilerParams(vmem_limit_bytes=40 * 1024 * 1024),
    )(*args)


def arr(*shape):
    return jax.ShapeDtypeStruct(shape, f32)


def local(n_wide, n_narrow, kernel, volume, velocity, block_brick, block_tile, fluid_velocity):
    blocks = kernel.shape[0]
    chips = n_wide // 2
    swap = [(w, w ^ 1) for w in range(n_wide)]
    along_wide = [(w, w + 2) for w in range(0, n_wide - 2, 2)] + [
        (w, w - 2) for w in range(3, n_wide, 2)
    ]
    along_narrow = [
        (w * n_narrow + n, w * n_narrow + t)
        for w in range(n_wide)
        for n in range(n_narrow)
        for t in (n + 1 - 2 * (w % 2),)
        if 0 <= t < n_narrow
    ]
    groups = [list(range(c, n_wide, 2)) for c in range(2)]

    def exchange(x):
        return lax.all_to_all(
            x, "wide", split_axis=0, concat_axis=0, tiled=True, axis_index_groups=groups
        )

    core = (lax.axis_index("wide") % 2).astype(jnp.int32).reshape(1)
    carried = jnp.concatenate([volume[:, None, :], volume[:, None, :] * velocity], axis=1)
    own_sums = jnp.einsum("bkp,bpc->bkc", carried, kernel, precision=highest)
    send, placed = call(
        pack_kernel,
        [SMEM, SMEM, VMEM],
        [(arr(chips * KEYS, CELLS), VMEM), (jax.ShapeDtypeStruct((blocks,), jnp.int32), SMEM)],
        block_brick.reshape(blocks),
        block_tile,
        own_sums,
        scratch=[pltpu.SMEM((n_wide,), jnp.int32)],
        name="pack",
    )
    recv = exchange(send.reshape(chips * KEYS, 1, CELLS)).reshape(chips * KEYS, CELLS)
    part, pick = call(
        spread_kernel,
        [VMEM, VMEM],
        [(arr(4 * XS + 3 * CX, CZ, NY), VMEM), (arr(SLOTS * chips, XS * 32), VMEM)],
        recv,
        fluid_velocity,
        name="spread",
    )
    other = lax.ppermute(part, "wide", swap)
    fields, aux, send_x = call(
        fields_kernel,
        [SMEM, VMEM, VMEM],
        [
            (arr(4 * XS, CZ, NY), VMEM),
            (arr(4 * XS, CZ, NY), VMEM),
            (arr(4 * DEPTH, CZ, NY), VMEM),
        ],
        core,
        part,
        other,
        name="fields",
    )
    recv_x = lax.ppermute(send_x, "wide", along_wide)
    swap_x = lax.ppermute(recv_x, "wide", swap)
    rows_z = XE + ROWS_S + 3
    send_z, faces = call(
        source_kernel,
        [SMEM, VMEM, VMEM, VMEM],
        [(arr(rows_z, CZ, NY), VMEM), (arr(6, CZ, NY), VMEM)],
        core,
        fields,
        recv_x,
        swap_x,
        name="source",
    )
    recv_z = lax.ppermute(send_z, ("wide", "narrow"), along_narrow)
    swap_z = lax.ppermute(recv_z, "wide", swap)
    region = pltpu.VMEM((XE, 3 * CZ, NY), f32)
    pressure, fluid_next, send_back = call(
        solve_kernel,
        [SMEM] + [VMEM] * 6,
        [
            (arr(CX, CZ, NY), VMEM),
            (arr(3, CX, CZ, NY), VMEM),
            (arr(chips * 4 * SLOTS, CELLS), VMEM),
        ],
        core,
        send_z,
        faces,
        recv_z,
        swap_z,
        aux,
        pick,
        scratch=[region] * 8 + [pltpu.VMEM((XS * 32, 4 * CELLS), f32)],
        name="solve",
    )
    back = exchange(send_back.reshape(chips, 4 * SLOTS, CELLS)).reshape(chips * 4 * SLOTS, CELLS)
    (block_fields,) = call(
        gather_kernel,
        [SMEM, VMEM],
        [(arr(blocks, 4, CELLS), VMEM)],
        placed,
        back,
        name="gather",
    )
    sampled = jnp.einsum("bkc,bpc->bkp", block_fields, kernel, precision=highest)
    particle_drag = volume[:, None, :] * sampled[:, :3] - carried[:, 1:] * sampled[:, 3:4]
    return (particle_drag, pressure, fluid_next)


def solution(mesh):
    return jax.shard_map(
        functools.partial(local, mesh.shape["wide"], mesh.shape["narrow"]),
        mesh=mesh,
        in_specs=(
            P(("wide", "narrow"), None, None),
            P(("wide", "narrow"), None),
            P(("wide", "narrow"), None, None),
            P(("wide", "narrow"), None),
            P(("wide", "narrow")),
            P(None, "wide", "narrow", None),
        ),
        out_specs=(
            P(("wide", "narrow"), None, None),
            P("wide", "narrow", None),
            P(None, "wide", "narrow", None),
        ),
        check_vma=False,
    )
```

time: 206 us -> 103 us (0.50)
  the two profiles are of different devices: /device:TPU:193 before, /device:TPU:264 now
where the time goes in v1:
time: 103 us
  blocking collectives  40.8 us (40%)
  waiting for transfers between devices  24.9 us (24%)
  Pallas kernels  15.4 us (15%)
  starting transfers between devices  11.8 us (11%)
  matrix products  5.9 us (6%)
  local copies, waits for them, and re-layouts  1.85 us (2%)
  other arithmetic  1.25 us (1%)
    all_to_all x2, blocking collectives, exchange(): lax.all_to_all(x, 'wide', split_axis=0, concat_axis=0, tiled=True, axis_i...  40.8 us
    pallas_call x6, Pallas kernels, call(): pl.pallas_call(kernel, out_shape=[shape for shape, _ in outs], in_specs=i...  15.4 us
    ppermute x1, waiting for transfers between devices, local(): recv_z = lax.ppermute(send_z, ('wide', 'narrow'), along_narrow)  11.2 us
    ppermute x1, waiting for transfers between devices, local(): recv_x = lax.ppermute(send_x, 'wide', along_wide)  7.67 us
    ppermute x1, starting transfers between devices, local(): recv_z = lax.ppermute(send_z, ('wide', 'narrow'), along_narrow)  3.38 us
    dot_general x1, matrix products, local(): jnp.einsum('bkc,bpc->bkp', block_fields, kernel, precision=highest)  3.36 us
    ppermute x1, starting transfers between devices, local(): recv_x = lax.ppermute(send_x, 'wide', along_wide)  2.69 us
    dot_general x1, matrix products, local(): own_sums = jnp.einsum('bkp,bpc->bkc', carried, kernel, precision=highest)  2.54 us
  transfers between devices with their start and end apart: 5, of which 5 were waited for; matrix products, arithmetic and copies ran while one was open for 0% of the time, Pallas kernels for 0%

profile of v1, /device:TPU:264, one launch (start us, length us, event | category | flops | bytes accessed | tf_op | source)
XLA Modules:
  0.0 102.7 jit_solution(350318877158542920)
XLA Ops:
  0.6 0.0 copy-start
  0.6 0.0 copy-start.5
  0.7 0.0 copy-start.4
  0.7 0.0 copy-start.1
  0.7 1.1 %copy_multiply_fusion = f32[64,3,64]{2,1,0:T(4,128)S(1)} fusion(f32[64,3,64]{2,0,1:T(8,128)} %param.8, f32[64,64]{1,0:T(8,128)} %param.7), kind=kLoop, calls=%fused_computation.6 | loop fusion | flops 12288 | bytes 114688 | tf_op jit(solution)/shard_map/mul | solution.py:325
  1.8 0.5 copy-done
  2.3 2.5 %fusion.1.sums_ref = f32[64,4,128]{2,1,0:T(4,128)S(1)} fusion(f32[64,64,128]{2,1,0:T(8,128)S(1)} %copy-done, f32[64,3,64]{2,1,0:T(4,128)S(1)} %copy_multiply_fusion, f32[64,1,64]{2,1,0:T(1,128)} %bitcast.18), kind=kOutput, calls=%fused_computation.2 | convolution fusion | flops 25182208 | bytes 2293760 | tf_op jit(solution)/shard_map/bkp,bpc->bkc/dot_general | solution.py:326
  4.8 0.0 copy-done.5
  4.8 0.0 copy-done.4
  4.8 2.6 %pack.1 = (f32[544,128]{1,0:T(8,128)S(1)}, s32[64]{0:T(128)S(1)}) custom-call(s32[64]{0:T(128)S(1)} %bitcast.17, s32[64]{0:T(128)S(1)} %copy-done.5, f32[64,4,128]{2,1,0:T(4,128)S(1)} %fusion.1.sums_ref), custom_call_target="tpu_custom_call" | custom-call | tf_op jit(solution)/shard_map/pack/pallas_call | solution.py:288
  7.5 22.6 %all_to_all.10 = f32[544,1,128]{2,1,0:T(1,128)S(1)} all-to-all(f32[544,1,128]{2,1,0:T(1,128)S(1)} %bitcast.15), channel_id=1, replica_groups={{0,16,32,48,64,80,96,112,128,144,160,176,192,208,224,240,256,272,288,30..., dimensions={0} | all-to-all | bytes 557056 | tf_op jit(solution)/shard_map/all_to_all | solution.py:320
  30.1 0.0 copy-done.1
  30.1 0.5 spread.1
  30.5 0.0 copy-start.2
  30.5 0.6 copy-done.2
  31.2 1.9 %collective-permute-start = (f32[44,8,512]{2,1,0:T(8,128)S(1)}, f32[44,8,512]{2,1,0:T(8,128)S(1)}, u32[]{:S(2)}, u32[]{:S(2)}) collective-permute-start(f32[44,8,512]{2,1,0:T(8,128)S(1)} %get-tuple-element.17.own_ref), channel_id=1, source_target_pairs={{0,8},{8,0},{16,24},{24,16},{32,40},{40,32},{48,56},{56,48},{64,72... | collective-permute-start | bytes 2162696 | tf_op jit(solution)/shard_map/ppermute | solution.py:346
  33.1 0.0 copy-start.3
  33.1 2.1 %collective-permute-done.other_ref = f32[44,8,512]{2,1,0:T(8,128)S(1)} collective-permute-done((f32[44,8,512]{2,1,0:T(8,128)S(1)}, f32[44,8,512]{2,1,0:T(8,128)S(1)}, u32[]{:S(2)}, u32[]{:S(2)}) %collective-permute-start) | collective-permute-done | bytes 720928 | tf_op jit(solution)/shard_map/ppermute | solution.py:346
  35.3 0.1 fields.1
  35.4 2.7 %collective-permute-start.1 = (f32[28,8,512]{2,1,0:T(8,128)S(1)}, f32[28,8,512]{2,1,0:T(8,128)S(1)}, u32[]{:S(2)}, u32[]{:S(2)}) collective-permute-start(f32[28,8,512]{2,1,0:T(8,128)S(1)} %get-tuple-element.19), channel_id=1, source_target_pairs={{0,16},{16,32},{32,48},{48,64},{64,80},{80,96},{96,112},{112,128},... | collective-permute-start | bytes 1376264 | tf_op jit(solution)/shard_map/ppermute | solution.py:360
  38.1 7.7 %collective-permute-done.1.recv_ref = f32[28,8,512]{2,1,0:T(8,128)S(1)} collective-permute-done((f32[28,8,512]{2,1,0:T(8,128)S(1)}, f32[28,8,512]{2,1,0:T(8,128)S(1)}, u32[]{:S(2)}, u32[]{:S(2)}) %collective-permute-start.1) | collective-permute-done | bytes 458784 | tf_op jit(solution)/shard_map/ppermute | solution.py:360
  45.8 1.9 %collective-permute-start.2 = (f32[28,8,512]{2,1,0:T(8,128)S(1)}, f32[28,8,512]{2,1,0:T(8,128)S(1)}, u32[]{:S(2)}, u32[]{:S(2)}) collective-permute-start(f32[28,8,512]{2,1,0:T(8,128)S(1)} %collective-permute-done.1.recv_ref), channel_id=1, source_target_pairs={{0,8},{8,0},{16,24},{24,16},{32,40},{40,32},{48,56},{56,48},{64,72... | collective-permute-start | bytes 1376264 | tf_op jit(solution)/shard_map/ppermute | solution.py:361
  47.7 1.8 %collective-permute-done.2.swap_ref = f32[28,8,512]{2,1,0:T(8,128)S(1)} collective-permute-done((f32[28,8,512]{2,1,0:T(8,128)S(1)}, f32[28,8,512]{2,1,0:T(8,128)S(1)}, u32[]{:S(2)}, u32[]{:S(2)}) %collective-permute-start.2) | collective-permute-done | bytes 458784 | tf_op jit(solution)/shard_map/ppermute | solution.py:361
  49.5 0.3 source.1
  49.8 3.4 %collective-permute-start.3 = (f32[45,8,512]{2,1,0:T(8,128)S(1)}, f32[45,8,512]{2,1,0:T(8,128)S(1)}, u32[]{:S(2)}, u32[]{:S(2)}) collective-permute-start(f32[45,8,512]{2,1,0:T(8,128)S(1)} %get-tuple-element.20.own_ref), channel_id=1, source_target_pairs={{0,1},{1,2},{2,3},{3,4},{4,5},{5,6},{6,7},{9,8},{10,9},{11,10},{12... | collective-permute-start | bytes 2211848 | tf_op jit(solution)/shard_map/ppermute | solution.py:373
  53.2 11.2 %collective-permute-done.3.recv_ref = f32[45,8,512]{2,1,0:T(8,128)S(1)} collective-permute-done((f32[45,8,512]{2,1,0:T(8,128)S(1)}, f32[45,8,512]{2,1,0:T(8,128)S(1)}, u32[]{:S(2)}, u32[]{:S(2)}) %collective-permute-start.3) | collective-permute-done | bytes 737312 | tf_op jit(solution)/shard_map/ppermute | solution.py:373
  64.3 1.9 %collective-permute-start.4 = (f32[45,8,512]{2,1,0:T(8,128)S(1)}, f32[45,8,512]{2,1,0:T(8,128)S(1)}, u32[]{:S(2)}, u32[]{:S(2)}) collective-permute-start(f32[45,8,512]{2,1,0:T(8,128)S(1)} %collective-permute-done.3.recv_ref), channel_id=1, source_target_pairs={{0,8},{8,0},{16,24},{24,16},{32,40},{40,32},{48,56},{56,48},{64,72... | collective-permute-start | bytes 2211848 | tf_op jit(solution)/shard_map/ppermute | solution.py:374
  66.3 2.2 %collective-permute-done.4.swap_ref = f32[45,8,512]{2,1,0:T(8,128)S(1)} collective-permute-done((f32[45,8,512]{2,1,0:T(8,128)S(1)}, f32[45,8,512]{2,1,0:T(8,128)S(1)}, u32[]{:S(2)}, u32[]{:S(2)}) %collective-permute-start.4) | collective-permute-done | bytes 737312 | tf_op jit(solution)/shard_map/ppermute | solution.py:374
  68.4 0.0 copy-done.3
  68.4 11.0 %solve.1 = (f32[4,8,512]{2,1,0:T(8,128)}, f32[3,4,8,512]{3,2,1,0:T(8,128)}, f32[512,128]{1,0:T(8,128)S(1)}) custom-call(s32[1]{0:T(128)} %bitcast.2.core_ref, f32[45,8,512]{2,1,0:T(8,128)S(1)} %get-tuple-element.20.own_ref, f32[6,8,512]{2,1,0:T(8,128)S(1)} %get-tuple-element.21.face_ref, f32[45,8,512]{2,1,0:T(8,128)S(1)} %collective-permute-done.3.recv_ref, ...), custom_call_target="tpu_custom_call" | custom-call | tf_op jit(solution)/shard_map/solve/pallas_call | solution.py:288
  79.4 0.0 copy-start.6
  79.4 0.0 copy-start.7
  79.4 18.2 %all_to_all.11 = f32[32,16,128]{2,1,0:T(8,128)S(1)} all-to-all(f32[32,16,128]{2,1,0:T(8,128)S(1)} %bitcast.16), channel_id=1, replica_groups={{0,16,32,48,64,80,96,112,128,144,160,176,192,208,224,240,256,272,288,30..., dimensions={0} | all-to-all | bytes 524288 | tf_op jit(solution)/shard_map/all_to_all | solution.py:320
  97.6 0.9 gather.1
  98.5 3.4 %fusion.6 = f32[64,4,64]{2,1,0:T(4,128)S(1)} fusion(f32[64,4,128]{2,1,0:T(4,128)S(1)} %gather.1, f32[64,64,128]{2,1,0:T(8,128)S(1)} %copy-done), kind=kOutput, calls=%fused_computation.8 | convolution fusion | flops 25165824 | bytes 2293760 | tf_op jit(solution)/shard_map/bkc,bpc->bkp/dot_general | solution.py:403
  102.0 0.0 copy-done.6
  102.0 0.0 copy-done.7
  102.0 0.1 fusion
  102.1 0.6 copy.13
  (1 shorter events, 0.0 us)
Async XLA Ops:
  0.6 1.7 %copy-start = (f32[64,64,128]{2,1,0:T(8,128)S(1)}, f32[64,64,128]{2,1,0:T(8,128)}, u32[]{:S(2)}) copy-start(f32[64,64,128]{2,1,0:T(8,128)} %param.6) | copy-start | bytes 6291460
  0.6 4.2 %copy-start.5 = (s32[64]{0:T(128)S(1)}, s32[64]{0:T(128)}, u32[]{:S(2)}) copy-start(s32[64]{0:T(128)} %tile_ref.1) | copy-start | bytes 772
  0.7 4.2 %copy-start.4 = (s32[64,1]{0,1:T(1,128)S(1)}, s32[64,1]{0,1:T(1,128)}, u32[]{:S(2)}) copy-start(s32[64,1]{0,1:T(1,128)} %param.9) | copy-start | bytes 772
  0.7 29.4 %copy-start.1 = (f32[3,4,8,512]{3,2,1,0:T(8,128)S(1)}, f32[3,4,8,512]{3,2,1,0:T(8,128)}, u32[]{:S(2)}) copy-start(f32[3,4,8,512]{3,2,1,0:T(8,128)} %fluid_ref.1) | copy-start | bytes 589828
  30.5 0.7 copy-start.2
  31.2 4.1 %collective-permute-start = (f32[44,8,512]{2,1,0:T(8,128)S(1)}, f32[44,8,512]{2,1,0:T(8,128)S(1)}, u32[]{:S(2)}, u32[]{:S(2)}) collective-permute-start(f32[44,8,512]{2,1,0:T(8,128)S(1)} %get-tuple-element.17.own_ref), channel_id=1, source_target_pairs={{0,8},{8,0},{16,24},{24,16},{32,40},{40,32},{48,56},{56,48},{64,72... | collective-permute-start | bytes 2162696 | tf_op jit(solution)/shard_map/ppermute | solution.py:346
  33.1 35.3 %copy-start.3 = (f32[128,256]{1,0:T(8,128)S(1)}, f32[128,256]{1,0:T(8,128)}, u32[]{:S(2)}) copy-start(f32[128,256]{1,0:T(8,128)} %copy-done.2) | copy-start | bytes 393220
  35.4 10.4 %collective-permute-start.1 = (f32[28,8,512]{2,1,0:T(8,128)S(1)}, f32[28,8,512]{2,1,0:T(8,128)S(1)}, u32[]{:S(2)}, u32[]{:S(2)}) collective-permute-start(f32[28,8,512]{2,1,0:T(8,128)S(1)} %get-tuple-element.19), channel_id=1, source_target_pairs={{0,16},{16,32},{32,48},{48,64},{64,80},{80,96},{96,112},{112,128},... | collective-permute-start | bytes 1376264 | tf_op jit(solution)/shard_map/ppermute | solution.py:360
  45.8 3.7 %collective-permute-start.2 = (f32[28,8,512]{2,1,0:T(8,128)S(1)}, f32[28,8,512]{2,1,0:T(8,128)S(1)}, u32[]{:S(2)}, u32[]{:S(2)}) collective-permute-start(f32[28,8,512]{2,1,0:T(8,128)S(1)} %collective-permute-done.1.recv_ref), channel_id=1, source_target_pairs={{0,8},{8,0},{16,24},{24,16},{32,40},{40,32},{48,56},{56,48},{64,72... | collective-permute-start | bytes 1376264 | tf_op jit(solution)/shard_map/ppermute | solution.py:361
  49.8 14.6 %collective-permute-start.3 = (f32[45,8,512]{2,1,0:T(8,128)S(1)}, f32[45,8,512]{2,1,0:T(8,128)S(1)}, u32[]{:S(2)}, u32[]{:S(2)}) collective-permute-start(f32[45,8,512]{2,1,0:T(8,128)S(1)} %get-tuple-element.20.own_ref), channel_id=1, source_target_pairs={{0,1},{1,2},{2,3},{3,4},{4,5},{5,6},{6,7},{9,8},{10,9},{11,10},{12... | collective-permute-start | bytes 2211848 | tf_op jit(solution)/shard_map/ppermute | solution.py:373
  64.3 4.1 %collective-permute-start.4 = (f32[45,8,512]{2,1,0:T(8,128)S(1)}, f32[45,8,512]{2,1,0:T(8,128)S(1)}, u32[]{:S(2)}, u32[]{:S(2)}) collective-permute-start(f32[45,8,512]{2,1,0:T(8,128)S(1)} %collective-permute-done.3.recv_ref), channel_id=1, source_target_pairs={{0,8},{8,0},{16,24},{24,16},{32,40},{40,32},{48,56},{56,48},{64,72... | collective-permute-start | bytes 2211848 | tf_op jit(solution)/shard_map/ppermute | solution.py:374
  79.4 22.5 %copy-start.6 = (f32[64,3,64]{2,0,1:T(8,128)S(1)}, f32[64,3,64]{2,0,1:T(8,128)}, u32[]{:S(2)}) copy-start(f32[64,3,64]{2,0,1:T(8,128)} %param.8) | copy-start | bytes 147460
  79.4 22.5 %copy-start.7 = (f32[64,64]{1,0:T(8,128)S(1)}, f32[64,64]{1,0:T(8,128)}, u32[]{:S(2)}) copy-start(f32[64,64]{1,0:T(8,128)} %param.7) | copy-start | bytes 49156

commit v2 on v1

--- a/solution.py
+++ b/solution.py
@@ -16,8 +16,9 @@
 SLOTS = 4
 KEYS = 4 * SLOTS + 1
 
-highest = lax.Precision.HIGHEST
+high = lax.Precision.HIGH
 f32 = jnp.float32
+UNROLL = 8
 
 
 def iota(shape, dim):
@@ -48,24 +49,22 @@
         count_ref[i] = 0
         return 0
 
-    lax.fori_loop(0, count_ref.shape[0], clear, 0)
-    lane = iota((1, CELLS), 1)
-
-    def body(b, _):
+    lax.fori_loop(0, count_ref.shape[0], clear, 0, unroll=8)
+    chips = count_ref.shape[0] // 2
+    spot = iota((chips, CELLS), 0) * CELLS + iota((chips, CELLS), 1)
+
+    def body(b, keys):
         brick = brick_ref[b]
         position = count_ref[brick]
         count_ref[brick] = position + 1
         chip = brick // 2
         slot = (brick % 2) * 2 + position
         placed_ref[b] = chip * SLOTS + slot
-        row = chip * KEYS + slot * 4
-        for k in range(4):
-            send_ref[pl.ds(row + k, 1), :] = sums_ref[b, pl.ds(k, 1), :]
-        keys = pl.ds(chip * KEYS + 4 * SLOTS, 1)
-        send_ref[keys, :] = jnp.where(lane == slot, tile_ref[b].astype(f32), send_ref[keys, :])
-        return 0
-
-    lax.fori_loop(0, blocks, body, 0)
+        send_ref[pl.ds(chip * KEYS + slot * 4, 4), :] = sums_ref[b]
+        return jnp.where(spot == chip * CELLS + slot, tile_ref[b].astype(f32), keys)
+
+    keys = lax.fori_loop(0, blocks, body, jnp.zeros((chips, CELLS), f32), unroll=UNROLL)
+    send_ref[pl.ds(4 * SLOTS, chips, stride=KEYS), :] = keys
 
 
 def spread_kernel(recv_ref, fluid_ref, out_ref, pick_ref):
@@ -155,74 +154,128 @@
         send_ref[XE + ROWS_S + i // 8, i % 8 : i % 8 + 1, :] = jnp.where(first, high, low)
 
 
+ZE = 3 * CZ
+Q = NY // CELLS
+PAD = 8
+
+
 def solve_kernel(
     core_ref, own_ref, face_ref, recv_ref, swap_ref, aux_ref, pick_ref,
     pressure_ref, next_ref, send_ref,
-    v, s, wx, wy, wz, inv, pa, pb, coupled,
+    v, s, xp, xm, zp, zm, yp, ym, pa, pb, faces, coupled, keep,
 ):
     core = core_ref[0]
-    first = core == 0
-    mid = pl.ds(CZ, CZ)
-
-    def assemble(r, _):
-        here, there = recv_ref[r], swap_ref[r]
-        v[r, 0:CZ] = jnp.where(first, here, there)
-        v[r, CZ : 2 * CZ] = own_ref[r]
-        v[r, 2 * CZ :] = jnp.where(first, there, here)
-        return 0
-
-    lax.fori_loop(0, XE, assemble, 0)
-
-    for i in range(ROWS_S):
-        r = i + 1
-        here, there = recv_ref[XE + i], swap_ref[XE + i]
-        s[r, 0:CZ] = jnp.where(first, here, there)
-        s[r, CZ : 2 * CZ] = own_ref[XE + i]
-        s[r, 2 * CZ :] = jnp.where(first, there, here)
-        tile, sub = i // 8, i % 8
-        line = slice(sub, sub + 1)
-        one = recv_ref[XE + ROWS_S + tile, line, :]
-        two = swap_ref[XE + ROWS_S + tile, line, :]
-        below, above = jnp.where(first, one, two), jnp.where(first, two, one)
-        own_low, own_high = face_ref[tile, line, :], face_ref[3 + tile, line, :]
-        s[r, CZ - 1 : CZ] += -0.5 * own_low
-        s[r, CZ : CZ + 1] += 0.5 * below
-        s[r, 2 * CZ - 1 : 2 * CZ] += -0.5 * above
-        s[r, 2 * CZ : 2 * CZ + 1] += 0.5 * own_high
-
-    last = iota((3 * CZ, NY), 1) == NY - 1
+    lane = iota((CZ, CELLS), 1)
+    sub = iota((CZ, CELLS), 0)
+
+    def at(r, q, z=0):
+        return pl.ds((r * Q + q) * ZE + PAD + z, CZ)
+
+    def lanes(q):
+        return slice(q * CELLS, (q + 1) * CELLS)
+
+    def bring(low, high):
+        def body(r, _):
+            for q in range(Q):
+                v[at(r, q)] = low[r, :, lanes(q)]
+                v[at(r, q, CZ)] = own_ref[r, :, lanes(q)]
+                v[at(r, q, 2 * CZ)] = high[r, :, lanes(q)]
+                s[at(r, q)] = low[XE + r, :, lanes(q)]
+                s[at(r, q, CZ)] = own_ref[XE + r, :, lanes(q)]
+                s[at(r, q, 2 * CZ)] = high[XE + r, :, lanes(q)]
+            return 0
+
+        lax.fori_loop(0, ROWS_S, body, 0, unroll=2)
+        for r in range(ROWS_S, XE):
+            for q in range(Q):
+                v[at(r, q)] = low[r, :, lanes(q)]
+                v[at(r, q, CZ)] = own_ref[r, :, lanes(q)]
+                v[at(r, q, 2 * CZ)] = high[r, :, lanes(q)]
+        tail = XE + ROWS_S
+        for f, (ref, base) in enumerate(((face_ref, 0), (face_ref, 3), (low, tail), (high, tail))):
+            for t in range(3):
+                for q in range(Q):
+                    faces[(f * Q + q) * 24 + t * 8 : (f * Q + q) * 24 + t * 8 + 8] = ref[
+                        base + t, :, lanes(q)
+                    ]
+
+    @pl.when(core == 0)
+    def _():
+        bring(recv_ref, swap_ref)
+
+    @pl.when(core != 0)
+    def _():
+        bring(swap_ref, recv_ref)
+
+    def shifted(values):
+        up = [pltpu.roll(x, CELLS - 1, 1) for x in values]
+        down = [pltpu.roll(x, 1, 1) for x in values]
+        ups = [jnp.where(lane == CELLS - 1, up[q + 1], up[q]) for q in range(Q - 1)] + [up[-1]]
+        downs = [down[0]] + [jnp.where(lane == 0, down[q - 1], down[q]) for q in range(1, Q)]
+        return ups, downs
 
     def weights(r, _):
-        c = v[r]
-        up = next_y(c)
-        over = pltpu.roll(c, 3 * CZ - 1, 0)
-        diagonal = 3.0 * c + 0.5 * (
-            (v[r + 1] + v[r - 1]) + (up + prev_y(c)) + (over + pltpu.roll(c, 1, 0))
-        )
-        i = jnp.where(c > 0.0, 1.0 / jnp.where(c > 0.0, diagonal, 1.0), 0.0)
-        wx[r] = 0.5 * (c + v[r + 1])
-        wy[r] = jnp.where(last, 0.0, 0.5 * (c + up))
-        wz[r] = 0.5 * (c + over)
-        inv[r] = i
-        p = s[r] * i
-        s[r] = p
-        pa[r] = p
+        i = r - 1
+
+        def face(f, q):
+            return jnp.broadcast_to(faces[pl.ds((f * Q + q) * 24 + i, 1)], (CZ, CELLS))
+
+        for z in range(0, ZE, CZ):
+            c = [v[at(r, q, z)] for q in range(Q)]
+            ups, downs = shifted(c)
+            for q in range(Q):
+                up, down = ups[q], downs[q]
+                if q == Q - 1:
+                    up = jnp.where(lane == CELLS - 1, 0.0, up)
+                if q == 0:
+                    down = jnp.where(lane == 0, 0.0, down)
+                here = at(r, q, z)
+                t = [
+                    c[q] + v[at(r + 1, q, z)],
+                    c[q] + v[at(r - 1, q, z)],
+                    c[q] + v[at(r, q, z + 1)],
+                    c[q] + v[at(r, q, z - 1)],
+                    c[q] + up,
+                    c[q] + down,
+                ]
+                total = ((t[0] + t[1]) + (t[2] + t[3])) + (t[4] + t[5])
+                some = c[q] > 0.0
+                scale = jnp.where(some, 1.0 / jnp.where(some, total, 1.0), 0.0)
+                if q == Q - 1:
+                    t[4] = jnp.where(lane == CELLS - 1, 0.0, t[4])
+                if q == 0:
+                    t[5] = jnp.where(lane == 0, 0.0, t[5])
+                for ref, value in zip((xp, xm, zp, zm, yp, ym), t):
+                    ref[here] = value * scale
+                value = s[at(i, q, z)]
+                if z == 0:
+                    value = value - jnp.where(sub == CZ - 1, 0.5 * face(0, q), 0.0)
+                elif z == CZ:
+                    value = value + jnp.where(sub == 0, 0.5 * face(2, q), 0.0)
+                    value = value - jnp.where(sub == CZ - 1, 0.5 * face(3, q), 0.0)
+                else:
+                    value = value + jnp.where(sub == 0, 0.5 * face(1, q), 0.0)
+                value = (2.0 * value) * scale
+                s[at(i, q, z)] = value
+                pa[here] = value
         return 0
 
     lax.fori_loop(1, XE - 1, weights, 0)
 
     def sweep(src, dst, reach):
         def body(r, _):
-            p = src[r]
-            y = wy[r]
-            z = wz[r]
-            acc = wx[r] * src[r + 1] + wx[r - 1] * src[r - 1]
-            acc += y * pltpu.roll(p, NY - 1, 1) + pltpu.roll(y * p, 1, 1)
-            acc += z * pltpu.roll(p, 3 * CZ - 1, 0) + pltpu.roll(z * p, 1, 0)
-            dst[r] = s[r] + inv[r] * acc
+            for z in range(0, ZE, CZ):
+                p = [src[at(r, q, z)] for q in range(Q)]
+                ups, downs = shifted(p)
+                for q in range(Q):
+                    here = at(r, q, z)
+                    a = xp[here] * src[at(r + 1, q, z)] + xm[here] * src[at(r - 1, q, z)]
+                    b = zp[here] * src[at(r, q, z + 1)] + zm[here] * src[at(r, q, z - 1)]
+                    c = yp[here] * ups[q] + ym[here] * downs[q]
+                    dst[here] = (s[at(r - 1, q, z)] + a) + (b + c)
             return 0
 
-        lax.fori_loop(DEPTH - reach, DEPTH + XS + reach, body, 0)
+        lax.fori_loop(DEPTH - reach, DEPTH + XS + reach, body, 0, unroll=2)
 
     src, dst = pa, pb
     for k in range(1, SWEEPS):
@@ -230,39 +283,35 @@
         src, dst = dst, src
 
     for i in range(CX):
-        pressure_ref[i] = src[DEPTH + core * CX + i, mid, :]
-
+        for q in range(Q):
+            pressure_ref[i, :, lanes(q)] = src[at(DEPTH + core * CX + i, q, CZ)]
     for x in range(XS):
         r = DEPTH + x
-        p = src[r]
-        growth = aux_ref[3 * XS + x]
-        diffs = [
-            src[r + 1, mid, :] - src[r - 1, mid, :],
-            (pltpu.roll(p, 3 * CZ - 1, 0) - pltpu.roll(p, 1, 0))[CZ : 2 * CZ],
-            next_y(p[CZ : 2 * CZ]) - prev_y(p[CZ : 2 * CZ]),
-        ]
-        for a in range(3):
-            value = aux_ref[a * XS + x] - 0.5 * diffs[a]
-            out = growth * value
-
-            @pl.when(core == x // CX)
-            def _(a=a, x=x, value=value):
-                next_ref[a, x % CX] = value
-
-            for q in range(4):
-                coupled[pl.ds(x * 32 + q * 8, 8), a * 128 : (a + 1) * 128] = out[
-                    :, q * 128 : (q + 1) * 128
-                ]
-        for q in range(4):
-            coupled[pl.ds(x * 32 + q * 8, 8), 3 * 128 : 4 * 128] = growth[
-                :, q * 128 : (q + 1) * 128
+        p = [src[at(r, q, CZ)] for q in range(Q)]
+        ups, downs = shifted(p)
+        ups[-1] = jnp.where(lane == CELLS - 1, 0.0, ups[-1])
+        downs[0] = jnp.where(lane == 0, 0.0, downs[0])
+        for q in range(Q):
+            growth = aux_ref[3 * XS + x, :, lanes(q)]
+            diffs = [
+                src[at(r + 1, q, CZ)] - src[at(r - 1, q, CZ)],
+                src[at(r, q, CZ + 1)] - src[at(r, q, CZ - 1)],
+                ups[q] - downs[q],
             ]
+            put = slice(x * 32 + q * 8, x * 32 + q * 8 + 8)
+            for a in range(3):
+                value = aux_ref[a * XS + x, :, lanes(q)] - 0.5 * diffs[a]
+                coupled[put, lanes(a)] = growth * value
+                keep[a * XS + x, :, lanes(q)] = value
+            coupled[put, lanes(3)] = growth
+    for a in range(3):
+        next_ref[a] = keep[pl.ds(a * XS + core * CX, CX)]
 
     pick = pick_ref[...].astype(jnp.bfloat16)
     chips = pick.shape[0] // SLOTS
     for k in range(4):
         total = jnp.zeros((pick.shape[0], CELLS), f32)
-        for part in split3(coupled[:, k * 128 : (k + 1) * 128]):
+        for part in split3(coupled[:, lanes(k)]):
             total += jnp.dot(pick, part, preferred_element_type=f32)
         for j in range(SLOTS):
             send_ref[pl.ds(j * 4 + k, chips, stride=4 * SLOTS), :] = total[
@@ -272,19 +321,17 @@
 
 def gather_kernel(placed_ref, back_ref, out_ref):
     def body(b, _):
-        row = placed_ref[b] * 4
-        for k in range(4):
-            out_ref[b, pl.ds(k, 1), :] = back_ref[pl.ds(row + k, 1), :]
+        out_ref[b] = back_ref[pl.ds(placed_ref[b] * 4, 4), :]
         return 0
 
-    lax.fori_loop(0, out_ref.shape[0], body, 0)
+    lax.fori_loop(0, out_ref.shape[0], body, 0, unroll=UNROLL)
 
 
 VMEM = pl.BlockSpec(memory_space=pltpu.VMEM)
 SMEM = pl.BlockSpec(memory_space=pltpu.SMEM)
 
 
-def call(kernel, ins, outs, *args, scratch=(), name=None):
+def call(kernel, ins, outs, *args, scratch=(), name=None, grant=4):
     return pl.pallas_call(
         kernel,
         out_shape=[shape for shape, _ in outs],
@@ -292,7 +339,7 @@
         out_specs=[spec for _, spec in outs],
         scratch_shapes=scratch,
         name=name,
-        compiler_params=pltpu.CompilerParams(vmem_limit_bytes=40 * 1024 * 1024),
+        compiler_params=pltpu.CompilerParams(vmem_limit_bytes=grant * 1024 * 1024),
     )(*args)
 
 
@@ -323,7 +370,7 @@
 
     core = (lax.axis_index("wide") % 2).astype(jnp.int32).reshape(1)
     carried = jnp.concatenate([volume[:, None, :], volume[:, None, :] * velocity], axis=1)
-    own_sums = jnp.einsum("bkp,bpc->bkc", carried, kernel, precision=highest)
+    own_sums = jnp.einsum("bkp,bpc->bkc", carried, kernel, precision=high)
     send, placed = call(
         pack_kernel,
         [SMEM, SMEM, VMEM],
@@ -372,7 +419,7 @@
     )
     recv_z = lax.ppermute(send_z, ("wide", "narrow"), along_narrow)
     swap_z = lax.ppermute(recv_z, "wide", swap)
-    region = pltpu.VMEM((XE, 3 * CZ, NY), f32)
+    region = pltpu.VMEM((XE * Q * ZE + 2 * PAD, CELLS), f32)
     pressure, fluid_next, send_back = call(
         solve_kernel,
         [SMEM] + [VMEM] * 6,
@@ -388,8 +435,14 @@
         swap_z,
         aux,
         pick,
-        scratch=[region] * 8 + [pltpu.VMEM((XS * 32, 4 * CELLS), f32)],
+        scratch=[region] * 10
+        + [
+            pltpu.VMEM((4 * Q * 24 + PAD, CELLS), f32),
+            pltpu.VMEM((XS * 32, 4 * CELLS), f32),
+            pltpu.VMEM((3 * XS, CZ, NY), f32),
+        ],
         name="solve",
+        grant=20,
     )
     back = exchange(send_back.reshape(chips, 4 * SLOTS, CELLS)).reshape(chips * 4 * SLOTS, CELLS)
     (block_fields,) = call(
@@ -400,7 +453,7 @@
         back,
         name="gather",
     )
-    sampled = jnp.einsum("bkc,bpc->bkp", block_fields, kernel, precision=highest)
+    sampled = jnp.einsum("bkc,bpc->bkp", block_fields, kernel, precision=high)
     particle_drag = volume[:, None, :] * sampled[:, :3] - carried[:, 1:] * sampled[:, 3:4]
     return (particle_drag, pressure, fluid_next)
 

time: 103 us -> 97 us (0.942)
  Pallas kernels: 15.4 us -> 11.8 us
  matrix products: 5.9 us -> 3.41 us
    pallas_call x6, Pallas kernels: 15.4 us -> 11.8 us  [call(): pl.pallas_call(kernel, out_shape=[shape for shape, _ in outs], in_specs=i...]
    dot_general x2, matrix products: 5.9 us -> 3.41 us  [the longest x1 1.73 us: local(): sampled = jnp.einsum('bkc,bpc->bkp', block_fields, kernel, precision=high)]
where the time goes in v2:
time: 97 us; the launch traced here: 96.6 us
  blocking collectives  40.7 us (42%)
  waiting for transfers between devices  24.9 us (26%)
  Pallas kernels  11.8 us (12%)
  starting transfers between devices  11.8 us (12%)
  matrix products  3.41 us (4%)
  local copies, waits for them, and re-layouts  1.85 us (2%)
  other arithmetic  1.25 us (1%)
    all_to_all x2, blocking collectives, exchange(): lax.all_to_all(x, 'wide', split_axis=0, concat_axis=0, tiled=True, axis_i...  40.7 us
    pallas_call x6, Pallas kernels, call(): pl.pallas_call(kernel, out_shape=[shape for shape, _ in outs], in_specs=i...  11.8 us
    ppermute x1, waiting for transfers between devices, local(): recv_z = lax.ppermute(send_z, ('wide', 'narrow'), along_narrow)  11.2 us
    ppermute x1, waiting for transfers between devices, local(): recv_x = lax.ppermute(send_x, 'wide', along_wide)  7.67 us
    ppermute x1, starting transfers between devices, local(): recv_z = lax.ppermute(send_z, ('wide', 'narrow'), along_narrow)  3.38 us
    ppermute x1, starting transfers between devices, local(): recv_x = lax.ppermute(send_x, 'wide', along_wide)  2.7 us
    ppermute x1, waiting for transfers between devices, local(): swap_z = lax.ppermute(recv_z, 'wide', swap)  2.18 us
    ppermute x1, waiting for transfers between devices, local(): other = lax.ppermute(part, 'wide', swap)  2.13 us
  transfers between devices with their start and end apart: 5, of which 5 were waited for; matrix products, arithmetic and copies ran while one was open for 0% of the time, Pallas kernels for 0%

profile of v2, /device:TPU:264, one launch (start us, length us, event | category | flops | bytes accessed | tf_op | source)
XLA Modules:
  0.0 96.6 jit_solution(7809221053889022728)
XLA Ops:
  0.6 0.0 copy-start
  0.6 0.0 copy-start.5
  0.7 0.0 copy-start.4
  0.7 0.0 copy-start.1
  0.7 1.1 %copy_multiply_fusion = f32[64,3,64]{2,1,0:T(4,128)S(1)} fusion(f32[64,3,64]{2,0,1:T(8,128)} %param.8, f32[64,64]{1,0:T(8,128)} %param.7), kind=kLoop, calls=%fused_computation.6 | loop fusion | flops 12288 | bytes 114688 | tf_op jit(solution)/shard_map/mul | solution.py:372
  1.8 0.5 copy-done
  2.3 1.7 %fusion.1.sums_ref = f32[64,4,128]{2,1,0:T(4,128)S(1)} fusion(f32[64,64,128]{2,1,0:T(8,128)S(1)} %copy-done, f32[64,3,64]{2,1,0:T(4,128)S(1)} %copy_multiply_fusion, f32[64,1,64]{2,1,0:T(1,128)} %bitcast.18), kind=kOutput, calls=%fused_computation.2 | convolution fusion | flops 12599296 | bytes 2293760 | tf_op jit(solution)/shard_map/bkp,bpc->bkc/dot_general | solution.py:373
  4.0 0.0 copy-done.5
  4.0 0.0 copy-done.4
  4.0 1.9 %pack.1 = (f32[544,128]{1,0:T(8,128)S(1)}, s32[64]{0:T(128)S(1)}) custom-call(s32[64]{0:T(128)S(1)} %bitcast.17, s32[64]{0:T(128)S(1)} %copy-done.5, f32[64,4,128]{2,1,0:T(4,128)S(1)} %fusion.1.sums_ref), custom_call_target="tpu_custom_call" | custom-call | tf_op jit(solution)/shard_map/pack/pallas_call | solution.py:335
  5.9 22.6 %all_to_all.10 = f32[544,1,128]{2,1,0:T(1,128)S(1)} all-to-all(f32[544,1,128]{2,1,0:T(1,128)S(1)} %bitcast.15), channel_id=1, replica_groups={{0,16,32,48,64,80,96,112,128,144,160,176,192,208,224,240,256,272,288,30..., dimensions={0} | all-to-all | bytes 557056 | tf_op jit(solution)/shard_map/all_to_all | solution.py:367
  28.5 0.0 copy-done.1
  28.5 0.5 spread.1
  29.0 0.0 copy-start.2
  29.0 0.6 copy-done.2
  29.7 1.9 %collective-permute-start = (f32[44,8,512]{2,1,0:T(8,128)S(1)}, f32[44,8,512]{2,1,0:T(8,128)S(1)}, u32[]{:S(2)}, u32[]{:S(2)}) collective-permute-start(f32[44,8,512]{2,1,0:T(8,128)S(1)} %get-tuple-element.17.own_ref), channel_id=1, source_target_pairs={{0,8},{8,0},{16,24},{24,16},{32,40},{40,32},{48,56},{56,48},{64,72... | collective-permute-start | bytes 2162696 | tf_op jit(solution)/shard_map/ppermute | solution.py:393
  31.6 0.0 copy-start.3
  31.6 2.1 %collective-permute-done.other_ref = f32[44,8,512]{2,1,0:T(8,128)S(1)} collective-permute-done((f32[44,8,512]{2,1,0:T(8,128)S(1)}, f32[44,8,512]{2,1,0:T(8,128)S(1)}, u32[]{:S(2)}, u32[]{:S(2)}) %collective-permute-start) | collective-permute-done | bytes 720928 | tf_op jit(solution)/shard_map/ppermute | solution.py:393
  33.7 0.1 fields.1
  33.9 2.7 %collective-permute-start.1 = (f32[28,8,512]{2,1,0:T(8,128)S(1)}, f32[28,8,512]{2,1,0:T(8,128)S(1)}, u32[]{:S(2)}, u32[]{:S(2)}) collective-permute-start(f32[28,8,512]{2,1,0:T(8,128)S(1)} %get-tuple-element.19), channel_id=1, source_target_pairs={{0,16},{16,32},{32,48},{48,64},{64,80},{80,96},{96,112},{112,128},... | collective-permute-start | bytes 1376264 | tf_op jit(solution)/shard_map/ppermute | solution.py:407
  36.6 7.7 %collective-permute-done.1.recv_ref = f32[28,8,512]{2,1,0:T(8,128)S(1)} collective-permute-done((f32[28,8,512]{2,1,0:T(8,128)S(1)}, f32[28,8,512]{2,1,0:T(8,128)S(1)}, u32[]{:S(2)}, u32[]{:S(2)}) %collective-permute-start.1) | collective-permute-done | bytes 458784 | tf_op jit(solution)/shard_map/ppermute | solution.py:407
  44.2 1.9 %collective-permute-start.2 = (f32[28,8,512]{2,1,0:T(8,128)S(1)}, f32[28,8,512]{2,1,0:T(8,128)S(1)}, u32[]{:S(2)}, u32[]{:S(2)}) collective-permute-start(f32[28,8,512]{2,1,0:T(8,128)S(1)} %collective-permute-done.1.recv_ref), channel_id=1, source_target_pairs={{0,8},{8,0},{16,24},{24,16},{32,40},{40,32},{48,56},{56,48},{64,72... | collective-permute-start | bytes 1376264 | tf_op jit(solution)/shard_map/ppermute | solution.py:408
  46.2 1.8 %collective-permute-done.2.swap_ref = f32[28,8,512]{2,1,0:T(8,128)S(1)} collective-permute-done((f32[28,8,512]{2,1,0:T(8,128)S(1)}, f32[28,8,512]{2,1,0:T(8,128)S(1)}, u32[]{:S(2)}, u32[]{:S(2)}) %collective-permute-start.2) | collective-permute-done | bytes 458784 | tf_op jit(solution)/shard_map/ppermute | solution.py:408
  47.9 0.3 source.1
  48.2 3.4 %collective-permute-start.3 = (f32[45,8,512]{2,1,0:T(8,128)S(1)}, f32[45,8,512]{2,1,0:T(8,128)S(1)}, u32[]{:S(2)}, u32[]{:S(2)}) collective-permute-start(f32[45,8,512]{2,1,0:T(8,128)S(1)} %get-tuple-element.20.own_ref), channel_id=1, source_target_pairs={{0,1},{1,2},{2,3},{3,4},{4,5},{5,6},{6,7},{9,8},{10,9},{11,10},{12... | collective-permute-start | bytes 2211848 | tf_op jit(solution)/shard_map/ppermute | solution.py:420
  51.6 11.2 %collective-permute-done.3.recv_ref = f32[45,8,512]{2,1,0:T(8,128)S(1)} collective-permute-done((f32[45,8,512]{2,1,0:T(8,128)S(1)}, f32[45,8,512]{2,1,0:T(8,128)S(1)}, u32[]{:S(2)}, u32[]{:S(2)}) %collective-permute-start.3) | collective-permute-done | bytes 737312 | tf_op jit(solution)/shard_map/ppermute | solution.py:420
  62.8 1.9 %collective-permute-start.4 = (f32[45,8,512]{2,1,0:T(8,128)S(1)}, f32[45,8,512]{2,1,0:T(8,128)S(1)}, u32[]{:S(2)}, u32[]{:S(2)}) collective-permute-start(f32[45,8,512]{2,1,0:T(8,128)S(1)} %collective-permute-done.3.recv_ref), channel_id=1, source_target_pairs={{0,8},{8,0},{16,24},{24,16},{32,40},{40,32},{48,56},{56,48},{64,72... | collective-permute-start | bytes 2211848 | tf_op jit(solution)/shard_map/ppermute | solution.py:421
  64.7 2.2 %collective-permute-done.4.swap_ref = f32[45,8,512]{2,1,0:T(8,128)S(1)} collective-permute-done((f32[45,8,512]{2,1,0:T(8,128)S(1)}, f32[45,8,512]{2,1,0:T(8,128)S(1)}, u32[]{:S(2)}, u32[]{:S(2)}) %collective-permute-start.4) | collective-permute-done | bytes 737312 | tf_op jit(solution)/shard_map/ppermute | solution.py:421
  66.9 0.0 copy-done.3
  66.9 8.3 %solve.1 = (f32[4,8,512]{2,1,0:T(8,128)}, f32[3,4,8,512]{3,2,1,0:T(8,128)}, f32[512,128]{1,0:T(8,128)S(1)}) custom-call(s32[1]{0:T(128)} %bitcast.2.core_ref, f32[45,8,512]{2,1,0:T(8,128)S(1)} %get-tuple-element.20.own_ref, f32[6,8,512]{2,1,0:T(8,128)S(1)} %get-tuple-element.21.face_ref, f32[45,8,512]{2,1,0:T(8,128)S(1)} %collective-permute-done.3.recv_ref, ...), custom_call_target="tpu_custom_call" | custom-call | tf_op jit(solution)/shard_map/solve/pallas_call | solution.py:335
  75.2 0.0 copy-start.6
  75.2 0.0 copy-start.7
  75.2 18.2 %all_to_all.11 = f32[32,16,128]{2,1,0:T(8,128)S(1)} all-to-all(f32[32,16,128]{2,1,0:T(8,128)S(1)} %bitcast.16), channel_id=1, replica_groups={{0,16,32,48,64,80,96,112,128,144,160,176,192,208,224,240,256,272,288,30..., dimensions={0} | all-to-all | bytes 524288 | tf_op jit(solution)/shard_map/all_to_all | solution.py:367
  93.4 0.6 gather.1
  94.1 1.7 %fusion.6 = f32[64,4,64]{2,1,0:T(4,128)S(1)} fusion(f32[64,4,128]{2,1,0:T(4,128)S(1)} %gather.1, f32[64,64,128]{2,1,0:T(8,128)S(1)} %copy-done), kind=kOutput, calls=%fused_computation.8 | convolution fusion | flops 12582912 | bytes 2293760 | tf_op jit(solution)/shard_map/bkc,bpc->bkp/dot_general | solution.py:456
  95.8 0.0 copy-done.6
  95.8 0.0 copy-done.7
  95.9 0.1 fusion
  96.0 0.6 copy.13
  (1 shorter events, 0.0 us)
Async XLA Ops:
  0.6 1.7 %copy-start = (f32[64,64,128]{2,1,0:T(8,128)S(1)}, f32[64,64,128]{2,1,0:T(8,128)}, u32[]{:S(2)}) copy-start(f32[64,64,128]{2,1,0:T(8,128)} %param.6) | copy-start | bytes 6291460
  0.6 3.3 %copy-start.5 = (s32[64]{0:T(128)S(1)}, s32[64]{0:T(128)}, u32[]{:S(2)}) copy-start(s32[64]{0:T(128)} %tile_ref.1) | copy-start | bytes 772
  0.7 3.3 %copy-start.4 = (s32[64,1]{0,1:T(1,128)S(1)}, s32[64,1]{0,1:T(1,128)}, u32[]{:S(2)}) copy-start(s32[64,1]{0,1:T(1,128)} %param.9) | copy-start | bytes 772
  0.7 27.9 %copy-start.1 = (f32[3,4,8,512]{3,2,1,0:T(8,128)S(1)}, f32[3,4,8,512]{3,2,1,0:T(8,128)}, u32[]{:S(2)}) copy-start(f32[3,4,8,512]{3,2,1,0:T(8,128)} %fluid_ref.1) | copy-start | bytes 589828
  29.0 0.7 copy-start.2
  29.7 4.1 %collective-permute-start = (f32[44,8,512]{2,1,0:T(8,128)S(1)}, f32[44,8,512]{2,1,0:T(8,128)S(1)}, u32[]{:S(2)}, u32[]{:S(2)}) collective-permute-start(f32[44,8,512]{2,1,0:T(8,128)S(1)} %get-tuple-element.17.own_ref), channel_id=1, source_target_pairs={{0,8},{8,0},{16,24},{24,16},{32,40},{40,32},{48,56},{56,48},{64,72... | collective-permute-start | bytes 2162696 | tf_op jit(solution)/shard_map/ppermute | solution.py:393
  31.6 35.3 %copy-start.3 = (f32[128,256]{1,0:T(8,128)S(1)}, f32[128,256]{1,0:T(8,128)}, u32[]{:S(2)}) copy-start(f32[128,256]{1,0:T(8,128)} %copy-done.2) | copy-start | bytes 393220
  33.9 10.4 %collective-permute-start.1 = (f32[28,8,512]{2,1,0:T(8,128)S(1)}, f32[28,8,512]{2,1,0:T(8,128)S(1)}, u32[]{:S(2)}, u32[]{:S(2)}) collective-permute-start(f32[28,8,512]{2,1,0:T(8,128)S(1)} %get-tuple-element.19), channel_id=1, source_target_pairs={{0,16},{16,32},{32,48},{48,64},{64,80},{80,96},{96,112},{112,128},... | collective-permute-start | bytes 1376264 | tf_op jit(solution)/shard_map/ppermute | solution.py:407
  44.2 3.7 %collective-permute-start.2 = (f32[28,8,512]{2,1,0:T(8,128)S(1)}, f32[28,8,512]{2,1,0:T(8,128)S(1)}, u32[]{:S(2)}, u32[]{:S(2)}) collective-permute-start(f32[28,8,512]{2,1,0:T(8,128)S(1)} %collective-permute-done.1.recv_ref), channel_id=1, source_target_pairs={{0,8},{8,0},{16,24},{24,16},{32,40},{40,32},{48,56},{56,48},{64,72... | collective-permute-start | bytes 1376264 | tf_op jit(solution)/shard_map/ppermute | solution.py:408
  48.2 14.6 %collective-permute-start.3 = (f32[45,8,512]{2,1,0:T(8,128)S(1)}, f32[45,8,512]{2,1,0:T(8,128)S(1)}, u32[]{:S(2)}, u32[]{:S(2)}) collective-permute-start(f32[45,8,512]{2,1,0:T(8,128)S(1)} %get-tuple-element.20.own_ref), channel_id=1, source_target_pairs={{0,1},{1,2},{2,3},{3,4},{4,5},{5,6},{6,7},{9,8},{10,9},{11,10},{12... | collective-permute-start | bytes 2211848 | tf_op jit(solution)/shard_map/ppermute | solution.py:420
  62.8 4.1 %collective-permute-start.4 = (f32[45,8,512]{2,1,0:T(8,128)S(1)}, f32[45,8,512]{2,1,0:T(8,128)S(1)}, u32[]{:S(2)}, u32[]{:S(2)}) collective-permute-start(f32[45,8,512]{2,1,0:T(8,128)S(1)} %collective-permute-done.3.recv_ref), channel_id=1, source_target_pairs={{0,8},{8,0},{16,24},{24,16},{32,40},{40,32},{48,56},{56,48},{64,72... | collective-permute-start | bytes 2211848 | tf_op jit(solution)/shard_map/ppermute | solution.py:421
  75.2 20.6 %copy-start.6 = (f32[64,3,64]{2,0,1:T(8,128)S(1)}, f32[64,3,64]{2,0,1:T(8,128)}, u32[]{:S(2)}) copy-start(f32[64,3,64]{2,0,1:T(8,128)} %param.8) | copy-start | bytes 147460
  75.2 20.6 %copy-start.7 = (f32[64,64]{1,0:T(8,128)S(1)}, f32[64,64]{1,0:T(8,128)}, u32[]{:S(2)}) copy-start(f32[64,64]{1,0:T(8,128)} %param.7) | copy-start | bytes 49156

commit v3 on v2

--- a/solution.py
+++ b/solution.py
@@ -67,14 +67,22 @@
     send_ref[pl.ds(4 * SLOTS, chips, stride=KEYS), :] = keys
 
 
-def spread_kernel(recv_ref, fluid_ref, out_ref, pick_ref):
-    chips = recv_ref.shape[0] // KEYS
-    tiles = recv_ref[pl.ds(4 * SLOTS, chips, stride=KEYS), :].astype(jnp.int32)
+def picking(tiles, pick_ref):
+    chips = tiles.shape[0]
+    tiles = tiles.astype(jnp.int32)
     rows = (tiles >> 5) * 32 + (tiles & 3) * 8 + ((tiles >> 2) & 7)
     cells = iota((chips, XS * 32), 1)
     for j in range(SLOTS):
         mine = rows[:, j : j + 1] + (j // 2) * 128
         pick_ref[pl.ds(j * chips, chips), :] = (cells == mine).astype(f32)
+
+
+def spread_kernel(recv_ref, fluid_ref, out_ref, pick_ref):
+    chips = recv_ref.shape[0] // KEYS
+    tiles = recv_ref[pl.ds(4 * SLOTS, chips, stride=KEYS), :]
+    picking(tiles, pick_ref)
+    for q in range(chips // CZ):
+        out_ref[4 * XS + 3 * CX, :, q * CELLS : (q + 1) * CELLS] = tiles[q * CZ : (q + 1) * CZ]
     pick = pick_ref[...].astype(jnp.bfloat16)
     for k in range(4):
         sums = jnp.concatenate(
@@ -90,11 +98,40 @@
                 out_ref[k * XS + x, :, q * 128 : (q + 1) * 128] = total[
                     x * 32 + q * 8 : x * 32 + q * 8 + 8, :
                 ]
-    out_ref[4 * XS :] = fluid_ref[...].reshape(3 * CX, CZ, NY)
-
-
-def fields_kernel(core_ref, own_ref, other_ref, field_ref, aux_ref, send_ref):
+    out_ref[4 * XS : 4 * XS + 3 * CX] = fluid_ref[...].reshape(3 * CX, CZ, NY)
+
+
+ROWS_S = XE - 2
+MSG_X = DEPTH + (DEPTH - 1) + 3
+PACK_V = (((1, 0), (5, 6)), ((2, 0), (4, 5)), ((3, 0), (6, 4)))
+PACK_S = (((1, 0), (3, 5)), ((2, 0), (4, 4), (5, 6)))
+MSG_Z = 2 * XS + 2 * (len(PACK_V) + len(PACK_S)) + 3
+FACES_Z = MSG_Z - 3
+
+
+def place(x, start, to, count):
+    line = iota(x.shape, 0)
+    shift = (to - start) % CZ
+    moved = pltpu.roll(x, shift, 0) if shift else x
+    return jnp.where((line >= to) & (line < to + count), moved, 0.0)
+
+
+def packed_rows():
+    tile = 2 * XS
+    for plan, reach in ((PACK_V, DEPTH), (PACK_S, DEPTH - 1)):
+        for side in range(2):
+            for group in plan:
+                yield tile, reach, [
+                    (DEPTH - d if side == 0 else DEPTH + XS - 1 + d, line, reach - d)
+                    for d, line in group
+                ]
+                tile += 1
+
+
+def fields_kernel(core_ref, own_ref, other_ref, field_ref, aux_ref, send_ref, vx, vz):
     core = core_ref[0]
+    z = iota((CZ, NY), 0)
+    aux_ref[4 * XS] = own_ref[4 * XS + 3 * CX]
     for x in range(XS):
         sums = [own_ref[k * XS + x] + other_ref[k * XS + x] for k in range(4)]
         mine = core == x // CX
@@ -111,47 +148,116 @@
         provisional = [(fluid[a] + growth * sums[1 + a]) * scale for a in range(3)]
         field_ref[x] = void
         for a in range(3):
-            field_ref[(1 + a) * XS + x] = void * provisional[a]
             aux_ref[a * XS + x] = provisional[a]
         aux_ref[3 * XS + x] = growth
-    for f in range(4):
-        send_ref[f * DEPTH : (f + 1) * DEPTH] = field_ref[pl.ds(f * XS + 1 - core, DEPTH)]
-
-
-ROWS_S = XE - 2
-
-
-def source_kernel(core_ref, field_ref, recv_ref, swap_ref, send_ref, face_ref):
+        vx[x] = void * provisional[0]
+        vz[x] = void * provisional[1]
+        along_z = vz[x]
+        along_y = void * provisional[2]
+        field_ref[XS + x] = -0.5 * (
+            jnp.where(z == CZ - 1, 0.0, pltpu.roll(along_z, CZ - 1, 0))
+            - jnp.where(z == 0, 0.0, pltpu.roll(along_z, 1, 0))
+            + next_y(along_y)
+            - prev_y(along_y)
+        )
+    for x in range(XS):
+        if x == 0:
+            along_x = vx[1]
+        elif x == XS - 1:
+            along_x = -vx[XS - 2]
+        else:
+            along_x = vx[x + 1] - vx[x - 1]
+        field_ref[XS + x] = field_ref[XS + x] - 0.5 * along_x
+        field_ref[2 * XS + 2, x : x + 1, :] = vz[x, 0:1, :]
+        field_ref[2 * XS + 3, x : x + 1, :] = vz[x, CZ - 1 : CZ, :]
+    field_ref[2 * XS] = vx[0]
+    field_ref[2 * XS + 1] = vx[XS - 1]
+
+    def fill(where):
+        for d in range(1, DEPTH + 1):
+            send_ref[d - 1] = field_ref[where(d)]
+        for d in range(1, DEPTH):
+            send_ref[DEPTH + d - 1] = field_ref[XS + where(d)]
+        send_ref[2 * DEPTH - 1] = vx[where(1)]
+        for f in range(2):
+            tile = 2 * DEPTH + f
+            send_ref[tile] = jnp.zeros((CZ, NY), f32)
+            for d in range(1, DEPTH):
+                x = where(d)
+                send_ref[tile, d - 1 : d, :] = field_ref[2 * XS + 2 + f, x : x + 1, :]
+
+    @pl.when(core == 0)
+    def _():
+        fill(lambda d: XS - d)
+
+    @pl.when(core != 0)
+    def _():
+        fill(lambda d: d - 1)
+
+
+def source_kernel(core_ref, field_ref, recv_ref, swap_ref, send_ref, face_ref, v, s):
     core = core_ref[0]
-    first = core == 0
-
-    def row(f, r):
-        if r < DEPTH:
-            return jnp.where(first, recv_ref[f * DEPTH + r], swap_ref[f * DEPTH + r])
-        if r < DEPTH + XS:
-            return field_ref[f * XS + r - DEPTH]
-        i = f * DEPTH + r - DEPTH - XS
-        return jnp.where(first, swap_ref[i], recv_ref[i])
-
-    for r in range(XE):
-        send_ref[r] = row(0, r)
-    face_ref[...] = jnp.zeros_like(face_ref)
-    send_ref[XE + ROWS_S :] = jnp.zeros((3, CZ, NY), f32)
-    z = iota((CZ, NY), 0)
-    for i in range(ROWS_S):
-        r = i + 1
-        along_x = row(1, r + 1) - row(1, r - 1)
-        vz = row(2, r)
-        along_z = jnp.where(z == CZ - 1, 0.0, pltpu.roll(vz, CZ - 1, 0)) - jnp.where(
-            z == 0, 0.0, pltpu.roll(vz, 1, 0)
-        )
-        vy = row(3, r)
-        along_y = next_y(vy) - prev_y(vy)
-        send_ref[XE + i] = -0.5 * (along_x + along_z + along_y)
-        low, high = vz[0:1], vz[CZ - 1 : CZ]
-        face_ref[i // 8, i % 8 : i % 8 + 1, :] = low
-        face_ref[3 + i // 8, i % 8 : i % 8 + 1, :] = high
-        send_ref[XE + ROWS_S + i // 8, i % 8 : i % 8 + 1, :] = jnp.where(first, high, low)
+
+    def bring(low, high):
+        for d in range(1, DEPTH + 1):
+            v[DEPTH - d] = low[d - 1]
+            v[DEPTH + XS - 1 + d] = high[d - 1]
+        for x in range(XS):
+            v[DEPTH + x] = field_ref[x]
+            s[DEPTH + x] = field_ref[XS + x]
+        for d in range(1, DEPTH):
+            s[DEPTH - d] = low[DEPTH + d - 1]
+            s[DEPTH + XS - 1 + d] = high[DEPTH + d - 1]
+        edge = 2 * DEPTH - 1
+        s[DEPTH - 1] = s[DEPTH - 1] - 0.5 * field_ref[2 * XS]
+        s[DEPTH] = s[DEPTH] + 0.5 * low[edge]
+        s[DEPTH + XS - 1] = s[DEPTH + XS - 1] - 0.5 * high[edge]
+        s[DEPTH + XS] = s[DEPTH + XS] + 0.5 * field_ref[2 * XS + 1]
+        for f in range(2):
+            face_ref[3 * f + 2] = jnp.zeros((CZ, NY), f32)
+            for i in range(ROWS_S):
+                r = i + 1
+                if r < DEPTH:
+                    d = DEPTH - r
+                    value = low[2 * DEPTH + f, d - 1 : d, :]
+                elif r < DEPTH + XS:
+                    x = r - DEPTH
+                    value = field_ref[2 * XS + 2 + f, x : x + 1, :]
+                else:
+                    d = r - DEPTH - XS + 1
+                    value = high[2 * DEPTH + f, d - 1 : d, :]
+                face_ref[3 * f + i // 8, i % 8 : i % 8 + 1, :] = value
+
+    @pl.when(core == 0)
+    def _():
+        bring(recv_ref, swap_ref)
+
+    @pl.when(core != 0)
+    def _():
+        bring(swap_ref, recv_ref)
+
+    for x in range(XS):
+        send_ref[x] = v[DEPTH + x]
+        send_ref[XS + x] = s[DEPTH + x]
+
+    def fill(up):
+        for tile, reach, rows in packed_rows():
+            ref = v if reach == DEPTH else s
+            total = None
+            for r, line, count in rows:
+                part = place(ref[r], CZ - count if up else 0, line, count)
+                total = part if total is None else total + part
+            send_ref[tile] = total
+        for t in range(3):
+            send_ref[FACES_Z + t] = face_ref[(3 if up else 0) + t]
+
+    @pl.when(core == 0)
+    def _():
+        fill(True)
+
+    @pl.when(core != 0)
+    def _():
+        fill(False)
 
 
 ZE = 3 * CZ
@@ -160,9 +266,9 @@
 
 
 def solve_kernel(
-    core_ref, own_ref, face_ref, recv_ref, swap_ref, aux_ref, pick_ref,
+    core_ref, v_ref, s_ref, face_ref, recv_ref, swap_ref, aux_ref,
     pressure_ref, next_ref, send_ref,
-    v, s, xp, xm, zp, zm, yp, ym, pa, pb, faces, coupled, keep,
+    v, s, xp, xm, zp, zm, yp, ym, pa, pb, faces, coupled, keep, pick_ref,
 ):
     core = core_ref[0]
     lane = iota((CZ, CELLS), 1)
@@ -175,24 +281,32 @@
         return slice(q * CELLS, (q + 1) * CELLS)
 
     def bring(low, high):
-        def body(r, _):
-            for q in range(Q):
-                v[at(r, q)] = low[r, :, lanes(q)]
-                v[at(r, q, CZ)] = own_ref[r, :, lanes(q)]
-                v[at(r, q, 2 * CZ)] = high[r, :, lanes(q)]
-                s[at(r, q)] = low[XE + r, :, lanes(q)]
-                s[at(r, q, CZ)] = own_ref[XE + r, :, lanes(q)]
-                s[at(r, q, 2 * CZ)] = high[XE + r, :, lanes(q)]
-            return 0
-
-        lax.fori_loop(0, ROWS_S, body, 0, unroll=2)
-        for r in range(ROWS_S, XE):
-            for q in range(Q):
-                v[at(r, q)] = low[r, :, lanes(q)]
-                v[at(r, q, CZ)] = own_ref[r, :, lanes(q)]
-                v[at(r, q, 2 * CZ)] = high[r, :, lanes(q)]
-        tail = XE + ROWS_S
-        for f, (ref, base) in enumerate(((face_ref, 0), (face_ref, 3), (low, tail), (high, tail))):
+        none = jnp.zeros((CZ, CELLS), f32)
+        for q in range(Q):
+            for r in (0, XE - 1):
+                v[at(r, q)] = none
+                v[at(r, q, 2 * CZ)] = none
+            for r in (1, XE - 2):
+                s[at(r - 1, q)] = none
+                s[at(r - 1, q, 2 * CZ)] = none
+            for r in range(XE):
+                v[at(r, q, CZ)] = v_ref[r, :, lanes(q)]
+            for i in range(ROWS_S):
+                s[at(i, q, CZ)] = s_ref[i + 1, :, lanes(q)]
+            for x in range(XS):
+                v[at(DEPTH + x, q)] = low[x, :, lanes(q)]
+                v[at(DEPTH + x, q, 2 * CZ)] = high[x, :, lanes(q)]
+                s[at(DEPTH + x - 1, q)] = low[XS + x, :, lanes(q)]
+                s[at(DEPTH + x - 1, q, 2 * CZ)] = high[XS + x, :, lanes(q)]
+            for tile, reach, rows in packed_rows():
+                a, b = low[tile, :, lanes(q)], high[tile, :, lanes(q)]
+                for r, line, count in rows:
+                    ref, i = (v, r) if reach == DEPTH else (s, r - 1)
+                    ref[at(i, q)] = place(a, line, CZ - count, count)
+                    ref[at(i, q, 2 * CZ)] = place(b, line, 0, count)
+        for f, (ref, base) in enumerate(
+            ((face_ref, 0), (face_ref, 3), (low, FACES_Z), (high, FACES_Z))
+        ):
             for t in range(3):
                 for q in range(Q):
                     faces[(f * Q + q) * 24 + t * 8 : (f * Q + q) * 24 + t * 8 + 8] = ref[
@@ -260,7 +374,8 @@
                 pa[here] = value
         return 0
 
-    lax.fori_loop(1, XE - 1, weights, 0)
+    for r in range(1, XE - 1):
+        weights(r, 0)
 
     def sweep(src, dst, reach):
         def body(r, _):
@@ -275,7 +390,8 @@
                     dst[here] = (s[at(r - 1, q, z)] + a) + (b + c)
             return 0
 
-        lax.fori_loop(DEPTH - reach, DEPTH + XS + reach, body, 0, unroll=2)
+        for r in range(DEPTH - reach, DEPTH + XS + reach):
+            body(r, 0)
 
     src, dst = pa, pb
     for k in range(1, SWEEPS):
@@ -307,8 +423,10 @@
     for a in range(3):
         next_ref[a] = keep[pl.ds(a * XS + core * CX, CX)]
 
+    chips = pick_ref.shape[0] // SLOTS
+    tiles = aux_ref[4 * XS]
+    picking(jnp.concatenate([tiles[:, lanes(q)] for q in range(chips // CZ)], axis=0), pick_ref)
     pick = pick_ref[...].astype(jnp.bfloat16)
-    chips = pick.shape[0] // SLOTS
     for k in range(4):
         total = jnp.zeros((pick.shape[0], CELLS), f32)
         for part in split3(coupled[:, lanes(k)]):
@@ -382,12 +500,13 @@
         name="pack",
     )
     recv = exchange(send.reshape(chips * KEYS, 1, CELLS)).reshape(chips * KEYS, CELLS)
-    part, pick = call(
+    (part,) = call(
         spread_kernel,
         [VMEM, VMEM],
-        [(arr(4 * XS + 3 * CX, CZ, NY), VMEM), (arr(SLOTS * chips, XS * 32), VMEM)],
+        [(arr(4 * XS + 3 * CX + 1, CZ, NY), VMEM)],
         recv,
         fluid_velocity,
+        scratch=[pltpu.VMEM((SLOTS * chips, XS * 32), f32)],
         name="spread",
     )
     other = lax.ppermute(part, "wide", swap)
@@ -395,22 +514,27 @@
         fields_kernel,
         [SMEM, VMEM, VMEM],
         [
-            (arr(4 * XS, CZ, NY), VMEM),
-            (arr(4 * XS, CZ, NY), VMEM),
-            (arr(4 * DEPTH, CZ, NY), VMEM),
+            (arr(2 * XS + 4, CZ, NY), VMEM),
+            (arr(4 * XS + 1, CZ, NY), VMEM),
+            (arr(MSG_X, CZ, NY), VMEM),
         ],
         core,
         part,
         other,
+        scratch=[pltpu.VMEM((XS, CZ, NY), f32)] * 2,
         name="fields",
     )
     recv_x = lax.ppermute(send_x, "wide", along_wide)
     swap_x = lax.ppermute(recv_x, "wide", swap)
-    rows_z = XE + ROWS_S + 3
-    send_z, faces = call(
+    send_z, faces, void, source = call(
         source_kernel,
         [SMEM, VMEM, VMEM, VMEM],
-        [(arr(rows_z, CZ, NY), VMEM), (arr(6, CZ, NY), VMEM)],
+        [
+            (arr(MSG_Z, CZ, NY), VMEM),
+            (arr(6, CZ, NY), VMEM),
+            (arr(XE, CZ, NY), VMEM),
+            (arr(XE - 1, CZ, NY), VMEM),
+        ],
         core,
         fields,
         recv_x,
@@ -429,17 +553,18 @@
             (arr(chips * 4 * SLOTS, CELLS), VMEM),
         ],
         core,
-        send_z,
+        void,
+        source,
         faces,
         recv_z,
         swap_z,
         aux,
-        pick,
         scratch=[region] * 10
         + [
             pltpu.VMEM((4 * Q * 24 + PAD, CELLS), f32),
             pltpu.VMEM((XS * 32, 4 * CELLS), f32),
             pltpu.VMEM((3 * XS, CZ, NY), f32),
+            pltpu.VMEM((SLOTS * chips, XS * 32), f32),
         ],
         name="solve",
         grant=20,

time: 97 us -> 88 us (0.907)
  waiting for transfers between devices: 24.9 us -> 19.5 us
  Pallas kernels: 11.8 us -> 8.77 us
    pallas_call x6, Pallas kernels: 11.8 us -> 8.77 us  [call(): pl.pallas_call(kernel, out_shape=[shape for shape, _ in outs], in_specs=i...]
    ppermute x1, waiting for transfers between devices: 11.2 us -> 8.37 us  [local(): recv_z = lax.ppermute(send_z, ('wide', 'narrow'), along_narrow)]
    ppermute x1, waiting for transfers between devices: 7.67 us -> 5.56 us  [local(): recv_x = lax.ppermute(send_x, 'wide', along_wide)]
where the time goes in v3:
time: 88 us; the launch traced here: 87.5 us
  blocking collectives  40.8 us (46%)
  waiting for transfers between devices  19.5 us (22%)
  starting transfers between devices  11.8 us (13%)
  Pallas kernels  8.77 us (10%)
  matrix products  3.41 us (4%)
  other arithmetic  1.25 us (1%)
  local copies, waits for them, and re-layouts  1.2 us (1%)
    all_to_all x2, blocking collectives, exchange(): lax.all_to_all(x, 'wide', split_axis=0, concat_axis=0, tiled=True, axis_i...  40.8 us
    pallas_call x6, Pallas kernels, call(): pl.pallas_call(kernel, out_shape=[shape for shape, _ in outs], in_specs=i...  8.77 us
    ppermute x1, waiting for transfers between devices, local(): recv_z = lax.ppermute(send_z, ('wide', 'narrow'), along_narrow)  8.37 us
    ppermute x1, waiting for transfers between devices, local(): recv_x = lax.ppermute(send_x, 'wide', along_wide)  5.56 us
    ppermute x1, starting transfers between devices, local(): recv_z = lax.ppermute(send_z, ('wide', 'narrow'), along_narrow)  3.38 us
    ppermute x1, starting transfers between devices, local(): recv_x = lax.ppermute(send_x, 'wide', along_wide)  2.7 us
    ppermute x1, waiting for transfers between devices, local(): other = lax.ppermute(part, 'wide', swap)  2.3 us
    ppermute x1, starting transfers between devices, local(): other = lax.ppermute(part, 'wide', swap)  1.92 us
  transfers between devices with their start and end apart: 5, of which 5 were waited for; matrix products, arithmetic and copies ran while one was open for 0% of the time, Pallas kernels for 0%

profile of v3, /device:TPU:264, one launch (start us, length us, event | category | flops | bytes accessed | tf_op | source)
XLA Modules:
  0.0 87.5 jit_solution(13982893851946003108)
XLA Ops:
  0.6 0.0 copy-start
  0.6 0.0 copy-start.3
  0.7 0.0 copy-start.2
  0.7 0.0 copy-start.1
  0.7 1.1 %copy_multiply_fusion = f32[64,3,64]{2,1,0:T(4,128)S(1)} fusion(f32[64,3,64]{2,0,1:T(8,128)} %param.8, f32[64,64]{1,0:T(8,128)} %param.7), kind=kLoop, calls=%fused_computation.6 | loop fusion | flops 12288 | bytes 114688 | tf_op jit(solution)/shard_map/mul | solution.py:490
  1.8 0.5 copy-done
  2.3 1.7 %fusion.1.sums_ref = f32[64,4,128]{2,1,0:T(4,128)S(1)} fusion(f32[64,64,128]{2,1,0:T(8,128)S(1)} %copy-done, f32[64,3,64]{2,1,0:T(4,128)S(1)} %copy_multiply_fusion, f32[64,1,64]{2,1,0:T(1,128)} %bitcast.18), kind=kOutput, calls=%fused_computation.2 | convolution fusion | flops 12599296 | bytes 2293760 | tf_op jit(solution)/shard_map/bkp,bpc->bkc/dot_general | solution.py:491
  4.0 0.0 copy-done.3
  4.0 0.0 copy-done.2
  4.0 1.9 %pack.1 = (f32[544,128]{1,0:T(8,128)S(1)}, s32[64]{0:T(128)S(1)}) custom-call(s32[64]{0:T(128)S(1)} %bitcast.17, s32[64]{0:T(128)S(1)} %copy-done.3, f32[64,4,128]{2,1,0:T(4,128)S(1)} %fusion.1.sums_ref), custom_call_target="tpu_custom_call" | custom-call | tf_op jit(solution)/shard_map/pack/pallas_call | solution.py:453
  5.9 22.6 %all_to_all.10 = f32[544,1,128]{2,1,0:T(1,128)S(1)} all-to-all(f32[544,1,128]{2,1,0:T(1,128)S(1)} %bitcast.15), channel_id=1, replica_groups={{0,16,32,48,64,80,96,112,128,144,160,176,192,208,224,240,256,272,288,30..., dimensions={0} | all-to-all | bytes 557056 | tf_op jit(solution)/shard_map/all_to_all | solution.py:485
  28.5 0.0 copy-done.1
  28.5 0.5 spread.1.own_ref
  29.0 1.9 %collective-permute-start = (f32[45,8,512]{2,1,0:T(8,128)S(1)}, f32[45,8,512]{2,1,0:T(8,128)}, u32[]{:S(2)}, u32[]{:S(2)}) collective-permute-start(f32[45,8,512]{2,1,0:T(8,128)S(1)} %spread.1.own_ref), channel_id=1, source_target_pairs={{0,8},{8,0},{16,24},{24,16},{32,40},{40,32},{48,56},{56,48},{64,72... | collective-permute-start | bytes 2211848 | tf_op jit(solution)/shard_map/ppermute | solution.py:512
  30.9 2.3 %collective-permute-done.other_ref = f32[45,8,512]{2,1,0:T(8,128)} collective-permute-done((f32[45,8,512]{2,1,0:T(8,128)S(1)}, f32[45,8,512]{2,1,0:T(8,128)}, u32[]{:S(2)}, u32[]{:S(2)}) %collective-permute-start) | collective-permute-done | bytes 737312 | tf_op jit(solution)/shard_map/ppermute | solution.py:512
  33.2 1.4 %fields.1 = (f32[20,8,512]{2,1,0:T(8,128)S(1)}, f32[33,8,512]{2,1,0:T(8,128)S(1)}, f32[16,8,512]{2,1,0:T(8,128)S(1)}) custom-call(s32[1]{0:T(128)} %bitcast.2.core_ref, f32[45,8,512]{2,1,0:T(8,128)S(1)} %spread.1.own_ref, f32[45,8,512]{2,1,0:T(8,128)} %collective-permute-done.other_ref), custom_call_target="tpu_custom_call" | custom-call | tf_op jit(solution)/shard_map/fields/pallas_call | solution.py:453
  34.6 2.7 %collective-permute-start.1 = (f32[16,8,512]{2,1,0:T(8,128)S(1)}, f32[16,8,512]{2,1,0:T(8,128)S(1)}, u32[]{:S(2)}, u32[]{:S(2)}) collective-permute-start(f32[16,8,512]{2,1,0:T(8,128)S(1)} %get-tuple-element.18), channel_id=1, source_target_pairs={{0,16},{16,32},{32,48},{48,64},{64,80},{80,96},{96,112},{112,128},... | collective-permute-start | bytes 786440 | tf_op jit(solution)/shard_map/ppermute | solution.py:527
  37.3 5.6 %collective-permute-done.1.recv_ref = f32[16,8,512]{2,1,0:T(8,128)S(1)} collective-permute-done((f32[16,8,512]{2,1,0:T(8,128)S(1)}, f32[16,8,512]{2,1,0:T(8,128)S(1)}, u32[]{:S(2)}, u32[]{:S(2)}) %collective-permute-start.1) | collective-permute-done | bytes 262176 | tf_op jit(solution)/shard_map/ppermute | solution.py:527
  42.9 1.9 %collective-permute-start.2 = (f32[16,8,512]{2,1,0:T(8,128)S(1)}, f32[16,8,512]{2,1,0:T(8,128)S(1)}, u32[]{:S(2)}, u32[]{:S(2)}) collective-permute-start(f32[16,8,512]{2,1,0:T(8,128)S(1)} %collective-permute-done.1.recv_ref), channel_id=1, source_target_pairs={{0,8},{8,0},{16,24},{24,16},{32,40},{40,32},{48,56},{56,48},{64,72... | collective-permute-start | bytes 786440 | tf_op jit(solution)/shard_map/ppermute | solution.py:528
  44.8 1.5 %collective-permute-done.2.swap_ref = f32[16,8,512]{2,1,0:T(8,128)S(1)} collective-permute-done((f32[16,8,512]{2,1,0:T(8,128)S(1)}, f32[16,8,512]{2,1,0:T(8,128)S(1)}, u32[]{:S(2)}, u32[]{:S(2)}) %collective-permute-start.2) | collective-permute-done | bytes 262176 | tf_op jit(solution)/shard_map/ppermute | solution.py:528
  46.3 0.1 source.1
  46.4 3.4 %collective-permute-start.3 = (f32[29,8,512]{2,1,0:T(8,128)S(1)}, f32[29,8,512]{2,1,0:T(8,128)S(1)}, u32[]{:S(2)}, u32[]{:S(2)}) collective-permute-start(f32[29,8,512]{2,1,0:T(8,128)S(1)} %get-tuple-element.22), channel_id=1, source_target_pairs={{0,1},{1,2},{2,3},{3,4},{4,5},{5,6},{6,7},{9,8},{10,9},{11,10},{12... | collective-permute-start | bytes 1425416 | tf_op jit(solution)/shard_map/ppermute | solution.py:544
  49.8 8.4 %collective-permute-done.3.recv_ref = f32[29,8,512]{2,1,0:T(8,128)S(1)} collective-permute-done((f32[29,8,512]{2,1,0:T(8,128)S(1)}, f32[29,8,512]{2,1,0:T(8,128)S(1)}, u32[]{:S(2)}, u32[]{:S(2)}) %collective-permute-start.3) | collective-permute-done | bytes 475168 | tf_op jit(solution)/shard_map/ppermute | solution.py:544
  58.2 1.9 %collective-permute-start.4 = (f32[29,8,512]{2,1,0:T(8,128)S(1)}, f32[29,8,512]{2,1,0:T(8,128)S(1)}, u32[]{:S(2)}, u32[]{:S(2)}) collective-permute-start(f32[29,8,512]{2,1,0:T(8,128)S(1)} %collective-permute-done.3.recv_ref), channel_id=1, source_target_pairs={{0,8},{8,0},{16,24},{24,16},{32,40},{40,32},{48,56},{56,48},{64,72... | collective-permute-start | bytes 1425416 | tf_op jit(solution)/shard_map/ppermute | solution.py:545
  60.1 1.8 %collective-permute-done.4.swap_ref = f32[29,8,512]{2,1,0:T(8,128)S(1)} collective-permute-done((f32[29,8,512]{2,1,0:T(8,128)S(1)}, f32[29,8,512]{2,1,0:T(8,128)S(1)}, u32[]{:S(2)}, u32[]{:S(2)}) %collective-permute-start.4) | collective-permute-done | bytes 475168 | tf_op jit(solution)/shard_map/ppermute | solution.py:545
  61.9 4.2 %solve.1 = (f32[4,8,512]{2,1,0:T(8,128)}, f32[3,4,8,512]{3,2,1,0:T(8,128)}, f32[512,128]{1,0:T(8,128)S(1)}) custom-call(s32[1]{0:T(128)} %bitcast.2.core_ref, f32[22,8,512]{2,1,0:T(8,128)S(1)} %get-tuple-element.19.v_ref, f32[21,8,512]{2,1,0:T(8,128)S(1)} %get-tuple-element.20.s_ref, f32[6,8,512]{2,1,0:T(8,128)S(1)} %get-tuple-element.21.face_ref, ...), custom_call_target="tpu_custom_call" | custom-call | tf_op jit(solution)/shard_map/solve/pallas_call | solution.py:453
  66.1 0.0 copy-start.4
  66.1 0.0 copy-start.5
  66.1 18.2 %all_to_all.11 = f32[32,16,128]{2,1,0:T(8,128)S(1)} all-to-all(f32[32,16,128]{2,1,0:T(8,128)S(1)} %bitcast.16), channel_id=1, replica_groups={{0,16,32,48,64,80,96,112,128,144,160,176,192,208,224,240,256,272,288,30..., dimensions={0} | all-to-all | bytes 524288 | tf_op jit(solution)/shard_map/all_to_all | solution.py:485
  84.3 0.6 gather.1
  85.0 1.7 %fusion.6 = f32[64,4,64]{2,1,0:T(4,128)S(1)} fusion(f32[64,4,128]{2,1,0:T(4,128)S(1)} %gather.1, f32[64,64,128]{2,1,0:T(8,128)S(1)} %copy-done), kind=kOutput, calls=%fused_computation.8 | convolution fusion | flops 12582912 | bytes 2293760 | tf_op jit(solution)/shard_map/bkc,bpc->bkp/dot_general | solution.py:581
  86.7 0.0 copy-done.4
  86.7 0.0 copy-done.5
  86.8 0.1 fusion
  86.9 0.6 copy.13
  (1 shorter events, 0.0 us)
Async XLA Ops:
  0.6 1.7 %copy-start = (f32[64,64,128]{2,1,0:T(8,128)S(1)}, f32[64,64,128]{2,1,0:T(8,128)}, u32[]{:S(2)}) copy-start(f32[64,64,128]{2,1,0:T(8,128)} %param.6) | copy-start | bytes 6291460
  0.6 3.3 %copy-start.3 = (s32[64]{0:T(128)S(1)}, s32[64]{0:T(128)}, u32[]{:S(2)}) copy-start(s32[64]{0:T(128)} %tile_ref.1) | copy-start | bytes 772
  0.7 3.3 %copy-start.2 = (s32[64,1]{0,1:T(1,128)S(1)}, s32[64,1]{0,1:T(1,128)}, u32[]{:S(2)}) copy-start(s32[64,1]{0,1:T(1,128)} %param.9) | copy-start | bytes 772
  0.7 27.9 %copy-start.1 = (f32[3,4,8,512]{3,2,1,0:T(8,128)S(1)}, f32[3,4,8,512]{3,2,1,0:T(8,128)}, u32[]{:S(2)}) copy-start(f32[3,4,8,512]{3,2,1,0:T(8,128)} %fluid_ref.1) | copy-start | bytes 589828
  29.0 4.2 %collective-permute-start = (f32[45,8,512]{2,1,0:T(8,128)S(1)}, f32[45,8,512]{2,1,0:T(8,128)}, u32[]{:S(2)}, u32[]{:S(2)}) collective-permute-start(f32[45,8,512]{2,1,0:T(8,128)S(1)} %spread.1.own_ref), channel_id=1, source_target_pairs={{0,8},{8,0},{16,24},{24,16},{32,40},{40,32},{48,56},{56,48},{64,72... | collective-permute-start | bytes 2211848 | tf_op jit(solution)/shard_map/ppermute | solution.py:512
  34.6 8.3 %collective-permute-start.1 = (f32[16,8,512]{2,1,0:T(8,128)S(1)}, f32[16,8,512]{2,1,0:T(8,128)S(1)}, u32[]{:S(2)}, u32[]{:S(2)}) collective-permute-start(f32[16,8,512]{2,1,0:T(8,128)S(1)} %get-tuple-element.18), channel_id=1, source_target_pairs={{0,16},{16,32},{32,48},{48,64},{64,80},{80,96},{96,112},{112,128},... | collective-permute-start | bytes 786440 | tf_op jit(solution)/shard_map/ppermute | solution.py:527
  42.9 3.4 %collective-permute-start.2 = (f32[16,8,512]{2,1,0:T(8,128)S(1)}, f32[16,8,512]{2,1,0:T(8,128)S(1)}, u32[]{:S(2)}, u32[]{:S(2)}) collective-permute-start(f32[16,8,512]{2,1,0:T(8,128)S(1)} %collective-permute-done.1.recv_ref), channel_id=1, source_target_pairs={{0,8},{8,0},{16,24},{24,16},{32,40},{40,32},{48,56},{56,48},{64,72... | collective-permute-start | bytes 786440 | tf_op jit(solution)/shard_map/ppermute | solution.py:528
  46.4 11.8 %collective-permute-start.3 = (f32[29,8,512]{2,1,0:T(8,128)S(1)}, f32[29,8,512]{2,1,0:T(8,128)S(1)}, u32[]{:S(2)}, u32[]{:S(2)}) collective-permute-start(f32[29,8,512]{2,1,0:T(8,128)S(1)} %get-tuple-element.22), channel_id=1, source_target_pairs={{0,1},{1,2},{2,3},{3,4},{4,5},{5,6},{6,7},{9,8},{10,9},{11,10},{12... | collective-permute-start | bytes 1425416 | tf_op jit(solution)/shard_map/ppermute | solution.py:544
  58.2 3.7 %collective-permute-start.4 = (f32[29,8,512]{2,1,0:T(8,128)S(1)}, f32[29,8,512]{2,1,0:T(8,128)S(1)}, u32[]{:S(2)}, u32[]{:S(2)}) collective-permute-start(f32[29,8,512]{2,1,0:T(8,128)S(1)} %collective-permute-done.3.recv_ref), channel_id=1, source_target_pairs={{0,8},{8,0},{16,24},{24,16},{32,40},{40,32},{48,56},{56,48},{64,72... | collective-permute-start | bytes 1425416 | tf_op jit(solution)/shard_map/ppermute | solution.py:545
  66.1 20.6 %copy-start.4 = (f32[64,3,64]{2,0,1:T(8,128)S(1)}, f32[64,3,64]{2,0,1:T(8,128)}, u32[]{:S(2)}) copy-start(f32[64,3,64]{2,0,1:T(8,128)} %param.8) | copy-start | bytes 147460
  66.1 20.6 %copy-start.5 = (f32[64,64]{1,0:T(8,128)S(1)}, f32[64,64]{1,0:T(8,128)}, u32[]{:S(2)}) copy-start(f32[64,64]{1,0:T(8,128)} %param.7) | copy-start | bytes 49156

commit v4 on v3

--- a/solution.py
+++ b/solution.py
@@ -16,9 +16,8 @@
 SLOTS = 4
 KEYS = 4 * SLOTS + 1
 
-high = lax.Precision.HIGH
 f32 = jnp.float32
-UNROLL = 8
+BLK = 64
 
 
 def iota(shape, dim):
@@ -41,30 +40,66 @@
     return jnp.where(iota(x.shape, x.ndim - 1) == NY - 1, 0.0, pltpu.roll(x, NY - 1, x.ndim - 1))
 
 
-def pack_kernel(brick_ref, tile_ref, sums_ref, send_ref, placed_ref, count_ref):
-    blocks = sums_ref.shape[0]
-    send_ref[...] = jnp.zeros_like(send_ref)
-
-    def clear(i, _):
-        count_ref[i] = 0
-        return 0
-
-    lax.fori_loop(0, count_ref.shape[0], clear, 0, unroll=8)
-    chips = count_ref.shape[0] // 2
-    spot = iota((chips, CELLS), 0) * CELLS + iota((chips, CELLS), 1)
-
-    def body(b, keys):
-        brick = brick_ref[b]
-        position = count_ref[brick]
-        count_ref[brick] = position + 1
-        chip = brick // 2
-        slot = (brick % 2) * 2 + position
-        placed_ref[b] = chip * SLOTS + slot
-        send_ref[pl.ds(chip * KEYS + slot * 4, 4), :] = sums_ref[b]
-        return jnp.where(spot == chip * CELLS + slot, tile_ref[b].astype(f32), keys)
-
-    keys = lax.fori_loop(0, blocks, body, jnp.zeros((chips, CELLS), f32), unroll=UNROLL)
-    send_ref[pl.ds(4 * SLOTS, chips, stride=KEYS), :] = keys
+def split2(x):
+    hi = x.astype(jnp.bfloat16).astype(f32)
+    return hi, (x - hi).astype(jnp.bfloat16).astype(f32)
+
+
+def block_products(left, kernel_ref, out, transposed):
+    dims = (((1,), (1 if transposed else 0,)), ((), ()))
+    hi, low = split2(left)
+    for g in range(left.shape[0] // 8):
+        rows = slice(8 * g, 8 * g + 8)
+        both = jnp.concatenate([hi[rows], low[rows]], axis=0).astype(jnp.bfloat16)
+        right = kernel_ref[2 * g : 2 * g + 2].reshape(2 * BLK, CELLS)
+        right_hi = right.astype(jnp.bfloat16)
+        right_low = (right - right_hi.astype(f32)).astype(jnp.bfloat16)
+        first = lax.dot_general(both, right_hi, dims, preferred_element_type=f32)
+        second = lax.dot_general(both, right_low, dims, preferred_element_type=f32)
+        out[rows, :] = first[0:8] + (first[8:16] + second[0:8])
+
+
+def slot_codes(brick):
+    blocks = brick.shape[1]
+    rows, lanes = iota((blocks, blocks), 0), iota((blocks, blocks), 1)
+    mine = jnp.broadcast_to(brick.astype(f32), (blocks, blocks))
+    other = jnp.sum(jnp.where(rows == lanes, mine, 0.0), axis=1, keepdims=True)
+    earlier = jnp.where((other == mine) & (rows < lanes), 1.0, 0.0)
+    position = jnp.sum(earlier, axis=0, keepdims=True).astype(jnp.int32)
+    return (2 * (brick & 1) + position), brick >> 1
+
+
+def pack_kernel(brick_ref, tile_ref, volume_ref, velocity_ref, kernel_ref, send_ref, left, sums):
+    blocks = volume_ref.shape[0]
+    chips = send_ref.shape[0] // KEYS
+    slots = chips * SLOTS
+    odd = (iota((blocks, BLK), 0) & 1) == 1
+    volume = volume_ref[...]
+    for k in range(4):
+        value = volume if k == 0 else volume * velocity_ref[k - 1]
+        left[pl.ds(k, blocks, stride=4), :] = jnp.concatenate(
+            [jnp.where(odd, 0.0, value), jnp.where(odd, value, 0.0)], axis=1
+        )
+    block_products(left[...], kernel_ref, sums, False)
+    slot, chip = slot_codes(brick_ref[...])
+    code = slot * chips + chip
+    match = iota((slots, blocks), 0) == jnp.broadcast_to(code, (slots, blocks))
+    move = match.astype(f32).astype(jnp.bfloat16)
+    for k in range(4):
+        total = jnp.zeros((slots, CELLS), f32)
+        for part in split3(sums[pl.ds(k, blocks, stride=4), :]):
+            total += jnp.dot(move, part, preferred_element_type=f32)
+        for j in range(SLOTS):
+            send_ref[pl.ds(j * 4 + k, chips, stride=KEYS), :] = total[
+                j * chips : (j + 1) * chips, :
+            ]
+    tile = jnp.broadcast_to(tile_ref[...].astype(f32), (slots, blocks))
+    keys = jnp.sum(jnp.where(match, tile, 0.0), axis=1, keepdims=True)
+    lane = iota((chips, CELLS), 1)
+    row = jnp.zeros((chips, CELLS), f32)
+    for j in range(SLOTS):
+        row = jnp.where(lane == j, keys[j * chips : (j + 1) * chips], row)
+    send_ref[pl.ds(4 * SLOTS, chips, stride=KEYS), :] = row
 
 
 def picking(tiles, pick_ref):
@@ -437,12 +472,29 @@
             ]
 
 
-def gather_kernel(placed_ref, back_ref, out_ref):
-    def body(b, _):
-        out_ref[b] = back_ref[pl.ds(placed_ref[b] * 4, 4), :]
-        return 0
-
-    lax.fori_loop(0, out_ref.shape[0], body, 0, unroll=UNROLL)
+def drag_kernel(brick_ref, volume_ref, velocity_ref, kernel_ref, back_ref, drag_ref, left, out):
+    blocks = volume_ref.shape[0]
+    slots = back_ref.shape[0] // 4
+    slot, chip = slot_codes(brick_ref[...])
+    code = chip * SLOTS + slot
+    match = iota((slots, blocks), 0) == jnp.broadcast_to(code, (slots, blocks))
+    move = match.astype(f32).astype(jnp.bfloat16)
+    for k in range(4):
+        total = jnp.zeros((blocks, CELLS), f32)
+        for part in split3(back_ref[pl.ds(k, slots, stride=4), :]):
+            total += lax.dot_general(
+                move, part, (((0,), (0,)), ((), ())), preferred_element_type=f32
+            )
+        left[pl.ds(k, blocks, stride=4), :] = total
+    block_products(left[...], kernel_ref, out, True)
+    odd = (iota((blocks, BLK), 0) & 1) == 1
+    sampled = []
+    for k in range(4):
+        value = out[pl.ds(k, blocks, stride=4), :]
+        sampled.append(jnp.where(odd, value[:, BLK:], value[:, :BLK]))
+    volume = volume_ref[...]
+    for k in range(3):
+        drag_ref[k] = volume * sampled[k] - (volume * velocity_ref[k]) * sampled[3]
 
 
 VMEM = pl.BlockSpec(memory_space=pltpu.VMEM)
@@ -487,16 +539,18 @@
         )
 
     core = (lax.axis_index("wide") % 2).astype(jnp.int32).reshape(1)
-    carried = jnp.concatenate([volume[:, None, :], volume[:, None, :] * velocity], axis=1)
-    own_sums = jnp.einsum("bkp,bpc->bkc", carried, kernel, precision=high)
-    send, placed = call(
+    brick = block_brick.reshape(1, blocks)
+    by_component = jnp.transpose(velocity, (1, 0, 2))
+    (send,) = call(
         pack_kernel,
-        [SMEM, SMEM, VMEM],
-        [(arr(chips * KEYS, CELLS), VMEM), (jax.ShapeDtypeStruct((blocks,), jnp.int32), SMEM)],
-        block_brick.reshape(blocks),
-        block_tile,
-        own_sums,
-        scratch=[pltpu.SMEM((n_wide,), jnp.int32)],
+        [VMEM] * 5,
+        [(arr(chips * KEYS, CELLS), VMEM)],
+        brick,
+        block_tile.reshape(1, blocks),
+        volume,
+        by_component,
+        kernel,
+        scratch=[pltpu.VMEM((4 * blocks, CELLS), f32)] * 2,
         name="pack",
     )
     recv = exchange(send.reshape(chips * KEYS, 1, CELLS)).reshape(chips * KEYS, CELLS)
@@ -567,19 +621,22 @@
             pltpu.VMEM((SLOTS * chips, XS * 32), f32),
         ],
         name="solve",
-        grant=20,
+        grant=16,
     )
     back = exchange(send_back.reshape(chips, 4 * SLOTS, CELLS)).reshape(chips * 4 * SLOTS, CELLS)
-    (block_fields,) = call(
-        gather_kernel,
-        [SMEM, VMEM],
-        [(arr(blocks, 4, CELLS), VMEM)],
-        placed,
+    (drag,) = call(
+        drag_kernel,
+        [VMEM] * 5,
+        [(arr(3, blocks, BLK), VMEM)],
+        brick,
+        volume,
+        by_component,
+        kernel,
         back,
-        name="gather",
+        scratch=[pltpu.VMEM((4 * blocks, CELLS), f32)] * 2,
+        name="drag",
     )
-    sampled = jnp.einsum("bkc,bpc->bkp", block_fields, kernel, precision=high)
-    particle_drag = volume[:, None, :] * sampled[:, :3] - carried[:, 1:] * sampled[:, 3:4]
+    particle_drag = jnp.transpose(drag, (1, 0, 2))
     return (particle_drag, pressure, fluid_next)
 
 

time: 88 us -> 86.2 us (0.980)
  matrix products: 3.41 us -> 0 us
  local copies, waits for them, and re-layouts: 1.2 us -> 4.57 us
  other arithmetic: 1.25 us -> 0 us
    unnamed x13 -> x20, local copies, waits for them, and re-layouts: 1.15 us -> 4.57 us
    dot_general x2 -> x0, matrix products: 3.41 us -> none  [the longest x1 1.73 us: local(): sampled = jnp.einsum('bkc,bpc->bkp', block_fields, kernel, precision=high)]
    mul x1 -> x0, other arithmetic: 1.13 us -> none  [local(): volume[:, None, :] * velocity]
where the time goes in v4:
time: 86.2 us; the launch traced here: 85.7 us
  blocking collectives  40.6 us (47%)
  waiting for transfers between devices  19.4 us (23%)
  starting transfers between devices  11.9 us (14%)
  Pallas kernels  8.42 us (10%)
  local copies, waits for them, and re-layouts  4.57 us (5%)
    all_to_all x2, blocking collectives, exchange(): lax.all_to_all(x, 'wide', split_axis=0, concat_axis=0, tiled=True, axis_i...  40.6 us
    pallas_call x6, Pallas kernels, call(): pl.pallas_call(kernel, out_shape=[shape for shape, _ in outs], in_specs=i...  8.42 us
    ppermute x1, waiting for transfers between devices, local(): recv_z = lax.ppermute(send_z, ('wide', 'narrow'), along_narrow)  8.38 us
    ppermute x1, waiting for transfers between devices, local(): recv_x = lax.ppermute(send_x, 'wide', along_wide)  5.56 us
    unnamed x20, local copies, waits for them, and re-layouts  4.57 us
    ppermute x1, starting transfers between devices, local(): recv_z = lax.ppermute(send_z, ('wide', 'narrow'), along_narrow)  3.37 us
    ppermute x1, starting transfers between devices, local(): recv_x = lax.ppermute(send_x, 'wide', along_wide)  2.83 us
    ppermute x1, waiting for transfers between devices, local(): other = lax.ppermute(part, 'wide', swap)  2.17 us
  transfers between devices with their start and end apart: 5, of which 5 were waited for; matrix products, arithmetic and copies ran while one was open for 0% of the time, Pallas kernels for 0%

profile of v4, /device:TPU:264, one launch (start us, length us, event | category | flops | bytes accessed | tf_op | source)
XLA Modules:
  0.0 85.7 jit_solution(6846773439030899087)
XLA Ops:
  0.6 0.0 copy-start
  0.6 1.6 %copy-done = f32[64,64,128]{2,1,0:T(8,128)S(1)} copy-done((f32[64,64,128]{2,1,0:T(8,128)S(1)}, f32[64,64,128]{2,1,0:T(8,128)}, u32[]{:S(2)}) %copy-start) | copy-done | bytes 2097176
  2.2 0.0 copy-start.2
  2.2 0.9 %copy-done.2 = f32[64,3,64]{2,0,1:T(8,128)S(1)} copy-done((f32[64,3,64]{2,0,1:T(8,128)S(1)}, f32[64,3,64]{2,0,1:T(8,128)}, u32[]{:S(2)}) %copy-start.2) | copy-done | bytes 49176
  3.1 0.0 copy-start.5
  3.1 0.8 copy-done.5
  3.9 0.0 copy-start.7
  3.9 0.7 copy-done.7
  4.5 0.0 copy-start.9
  4.5 0.7 copy-done.9
  5.2 0.0 copy-start.4
  5.2 1.0 %pack.1 = f32[544,128]{1,0:T(8,128)S(1)} custom-call(s32[1,64]{1,0:T(1,128)S(1)} %bitcast.17, s32[1,64]{1,0:T(1,128)S(1)} %bitcast.19, f32[64,64]{1,0:T(8,128)S(1)} %copy-done.5, f32[3,64,64]{2,1,0:T(8,128)S(1)} %bitcast.14, f32[64,64,128]{2,1,0:T(8,128)S(1)} %copy-done), custom_call_target="tpu_custom_call" | custom-call | tf_op jit(solution)/shard_map/pack/pallas_call | solution.py:505
  6.2 22.6 %all_to_all.10 = f32[544,1,128]{2,1,0:T(1,128)S(1)} all-to-all(f32[544,1,128]{2,1,0:T(1,128)S(1)} %bitcast.11), channel_id=1, replica_groups={{0,16,32,48,64,80,96,112,128,144,160,176,192,208,224,240,256,272,288,30..., dimensions={0} | all-to-all | bytes 557056 | tf_op jit(solution)/shard_map/all_to_all | solution.py:537
  28.7 0.0 copy-done.4
  28.7 0.5 spread.1.own_ref
  29.2 1.9 %collective-permute-start = (f32[45,8,512]{2,1,0:T(8,128)S(1)}, f32[45,8,512]{2,1,0:T(8,128)S(1)}, u32[]{:S(2)}, u32[]{:S(2)}) collective-permute-start(f32[45,8,512]{2,1,0:T(8,128)S(1)} %spread.1.own_ref), channel_id=1, source_target_pairs={{0,8},{8,0},{16,24},{24,16},{32,40},{40,32},{48,56},{56,48},{64,72... | collective-permute-start | bytes 2211848 | tf_op jit(solution)/shard_map/ppermute | solution.py:566
  31.2 2.2 %collective-permute-done.other_ref = f32[45,8,512]{2,1,0:T(8,128)S(1)} collective-permute-done((f32[45,8,512]{2,1,0:T(8,128)S(1)}, f32[45,8,512]{2,1,0:T(8,128)S(1)}, u32[]{:S(2)}, u32[]{:S(2)}) %collective-permute-start) | collective-permute-done | bytes 737312 | tf_op jit(solution)/shard_map/ppermute | solution.py:566
  33.3 0.3 fields.1
  33.6 0.0 copy-start.1
  33.6 0.0 copy-start.3
  33.6 0.0 copy-start.6
  33.6 0.0 copy-start.8
  33.6 2.8 %collective-permute-start.1 = (f32[16,8,512]{2,1,0:T(8,128)S(1)}, f32[16,8,512]{2,1,0:T(8,128)S(1)}, u32[]{:S(2)}, u32[]{:S(2)}) collective-permute-start(f32[16,8,512]{2,1,0:T(8,128)S(1)} %get-tuple-element.14), channel_id=1, source_target_pairs={{0,16},{16,32},{32,48},{48,64},{64,80},{80,96},{96,112},{112,128},... | collective-permute-start | bytes 786440 | tf_op jit(solution)/shard_map/ppermute | solution.py:581
  36.5 5.6 %collective-permute-done.1.recv_ref = f32[16,8,512]{2,1,0:T(8,128)S(1)} collective-permute-done((f32[16,8,512]{2,1,0:T(8,128)S(1)}, f32[16,8,512]{2,1,0:T(8,128)S(1)}, u32[]{:S(2)}, u32[]{:S(2)}) %collective-permute-start.1) | collective-permute-done | bytes 262176 | tf_op jit(solution)/shard_map/ppermute | solution.py:581
  42.0 1.9 %collective-permute-start.2 = (f32[16,8,512]{2,1,0:T(8,128)S(1)}, f32[16,8,512]{2,1,0:T(8,128)S(1)}, u32[]{:S(2)}, u32[]{:S(2)}) collective-permute-start(f32[16,8,512]{2,1,0:T(8,128)S(1)} %collective-permute-done.1.recv_ref), channel_id=1, source_target_pairs={{0,8},{8,0},{16,24},{24,16},{32,40},{40,32},{48,56},{56,48},{64,72... | collective-permute-start | bytes 786440 | tf_op jit(solution)/shard_map/ppermute | solution.py:582
  44.0 1.5 %collective-permute-done.2.swap_ref = f32[16,8,512]{2,1,0:T(8,128)S(1)} collective-permute-done((f32[16,8,512]{2,1,0:T(8,128)S(1)}, f32[16,8,512]{2,1,0:T(8,128)S(1)}, u32[]{:S(2)}, u32[]{:S(2)}) %collective-permute-start.2) | collective-permute-done | bytes 262176 | tf_op jit(solution)/shard_map/ppermute | solution.py:582
  45.5 0.1 source.1
  45.6 3.4 %collective-permute-start.3 = (f32[29,8,512]{2,1,0:T(8,128)S(1)}, f32[29,8,512]{2,1,0:T(8,128)S(1)}, u32[]{:S(2)}, u32[]{:S(2)}) collective-permute-start(f32[29,8,512]{2,1,0:T(8,128)S(1)} %get-tuple-element.18), channel_id=1, source_target_pairs={{0,1},{1,2},{2,3},{3,4},{4,5},{5,6},{6,7},{9,8},{10,9},{11,10},{12... | collective-permute-start | bytes 1425416 | tf_op jit(solution)/shard_map/ppermute | solution.py:598
  49.0 8.4 %collective-permute-done.3.recv_ref = f32[29,8,512]{2,1,0:T(8,128)S(1)} collective-permute-done((f32[29,8,512]{2,1,0:T(8,128)S(1)}, f32[29,8,512]{2,1,0:T(8,128)S(1)}, u32[]{:S(2)}, u32[]{:S(2)}) %collective-permute-start.3) | collective-permute-done | bytes 475168 | tf_op jit(solution)/shard_map/ppermute | solution.py:598
  57.3 1.9 %collective-permute-start.4 = (f32[29,8,512]{2,1,0:T(8,128)S(1)}, f32[29,8,512]{2,1,0:T(8,128)S(1)}, u32[]{:S(2)}, u32[]{:S(2)}) collective-permute-start(f32[29,8,512]{2,1,0:T(8,128)S(1)} %collective-permute-done.3.recv_ref), channel_id=1, source_target_pairs={{0,8},{8,0},{16,24},{24,16},{32,40},{40,32},{48,56},{56,48},{64,72... | collective-permute-start | bytes 1425416 | tf_op jit(solution)/shard_map/ppermute | solution.py:599
  59.3 1.8 %collective-permute-done.4.swap_ref = f32[29,8,512]{2,1,0:T(8,128)S(1)} collective-permute-done((f32[29,8,512]{2,1,0:T(8,128)S(1)}, f32[29,8,512]{2,1,0:T(8,128)S(1)}, u32[]{:S(2)}, u32[]{:S(2)}) %collective-permute-start.4) | collective-permute-done | bytes 475168 | tf_op jit(solution)/shard_map/ppermute | solution.py:599
  61.1 4.2 %solve.1 = (f32[4,8,512]{2,1,0:T(8,128)}, f32[3,4,8,512]{3,2,1,0:T(8,128)}, f32[512,128]{1,0:T(8,128)S(1)}) custom-call(s32[1]{0:T(128)} %bitcast.2.core_ref, f32[22,8,512]{2,1,0:T(8,128)S(1)} %get-tuple-element.15.v_ref, f32[21,8,512]{2,1,0:T(8,128)S(1)} %get-tuple-element.16.s_ref, f32[6,8,512]{2,1,0:T(8,128)S(1)} %get-tuple-element.17.face_ref, ...), custom_call_target="tpu_custom_call" | custom-call | tf_op jit(solution)/shard_map/solve/pallas_call | solution.py:505
  65.3 18.0 %all_to_all.11 = f32[32,16,128]{2,1,0:T(8,128)S(1)} all-to-all(f32[32,16,128]{2,1,0:T(8,128)S(1)} %bitcast.16), channel_id=1, replica_groups={{0,16,32,48,64,80,96,112,128,144,160,176,192,208,224,240,256,272,288,30..., dimensions={0} | all-to-all | bytes 524288 | tf_op jit(solution)/shard_map/all_to_all | solution.py:537
  83.3 0.0 copy-done.1
  83.3 0.0 copy-done.3
  83.3 0.0 copy-done.6
  83.4 0.0 copy-done.8
  83.4 2.4 %drag.1 = f32[3,64,64]{2,1,0:T(8,128)} custom-call(s32[1,64]{1,0:T(1,128)S(1)} %bitcast.18, f32[64,64]{1,0:T(8,128)S(1)} %copy-done.6, f32[3,64,64]{2,1,0:T(8,128)S(1)} %bitcast.15, f32[64,64,128]{2,1,0:T(8,128)S(1)} %copy-done.1, f32[512,128]{1,0:T(8,128)S(1)} %bitcast.13), custom_call_target="tpu_custom_call" | custom-call | tf_op jit(solution)/shard_map/drag/pallas_call | solution.py:505
Async XLA Ops:
  0.6 1.6 %copy-start = (f32[64,64,128]{2,1,0:T(8,128)S(1)}, f32[64,64,128]{2,1,0:T(8,128)}, u32[]{:S(2)}) copy-start(f32[64,64,128]{2,1,0:T(8,128)} %kernel_ref.3) | copy-start | bytes 6291460
  2.2 0.9 %copy-start.2 = (f32[64,3,64]{2,0,1:T(8,128)S(1)}, f32[64,3,64]{2,0,1:T(8,128)}, u32[]{:S(2)}) copy-start(f32[64,3,64]{2,0,1:T(8,128)} %param.8) | copy-start | bytes 147460
  3.1 0.8 copy-start.5
  3.9 0.7 copy-start.7
  4.5 0.7 copy-start.9
  5.2 23.6 %copy-start.4 = (f32[3,4,8,512]{3,2,1,0:T(8,128)S(1)}, f32[3,4,8,512]{3,2,1,0:T(8,128)}, u32[]{:S(2)}) copy-start(f32[3,4,8,512]{3,2,1,0:T(8,128)} %fluid_ref.1) | copy-start | bytes 589828
  29.2 4.1 %collective-permute-start = (f32[45,8,512]{2,1,0:T(8,128)S(1)}, f32[45,8,512]{2,1,0:T(8,128)S(1)}, u32[]{:S(2)}, u32[]{:S(2)}) collective-permute-start(f32[45,8,512]{2,1,0:T(8,128)S(1)} %spread.1.own_ref), channel_id=1, source_target_pairs={{0,8},{8,0},{16,24},{24,16},{32,40},{40,32},{48,56},{56,48},{64,72... | collective-permute-start | bytes 2211848 | tf_op jit(solution)/shard_map/ppermute | solution.py:566
  33.6 49.8 %copy-start.1 = (f32[64,64,128]{2,1,0:T(8,128)S(1)}, f32[64,64,128]{2,1,0:T(8,128)}, u32[]{:S(2)}) copy-start(f32[64,64,128]{2,1,0:T(8,128)} %kernel_ref.3) | copy-start | bytes 6291460
  33.6 49.7 %copy-start.3 = (f32[64,3,64]{2,0,1:T(8,128)S(1)}, f32[64,3,64]{2,0,1:T(8,128)}, u32[]{:S(2)}) copy-start(f32[64,3,64]{2,0,1:T(8,128)} %param.8) | copy-start | bytes 147460
  33.6 49.7 %copy-start.6 = (f32[64,64]{1,0:T(8,128)S(1)}, f32[64,64]{1,0:T(8,128)}, u32[]{:S(2)}) copy-start(f32[64,64]{1,0:T(8,128)} %volume_ref.3) | copy-start | bytes 49156
  33.6 49.7 %copy-start.8 = (s32[64,1]{0,1:T(1,128)S(1)}, s32[64,1]{0,1:T(1,128)}, u32[]{:S(2)}) copy-start(s32[64,1]{0,1:T(1,128)} %param.9) | copy-start | bytes 772
  33.6 8.4 %collective-permute-start.1 = (f32[16,8,512]{2,1,0:T(8,128)S(1)}, f32[16,8,512]{2,1,0:T(8,128)S(1)}, u32[]{:S(2)}, u32[]{:S(2)}) collective-permute-start(f32[16,8,512]{2,1,0:T(8,128)S(1)} %get-tuple-element.14), channel_id=1, source_target_pairs={{0,16},{16,32},{32,48},{48,64},{64,80},{80,96},{96,112},{112,128},... | collective-permute-start | bytes 786440 | tf_op jit(solution)/shard_map/ppermute | solution.py:581
  42.0 3.4 %collective-permute-start.2 = (f32[16,8,512]{2,1,0:T(8,128)S(1)}, f32[16,8,512]{2,1,0:T(8,128)S(1)}, u32[]{:S(2)}, u32[]{:S(2)}) collective-permute-start(f32[16,8,512]{2,1,0:T(8,128)S(1)} %collective-permute-done.1.recv_ref), channel_id=1, source_target_pairs={{0,8},{8,0},{16,24},{24,16},{32,40},{40,32},{48,56},{56,48},{64,72... | collective-permute-start | bytes 786440 | tf_op jit(solution)/shard_map/ppermute | solution.py:582
  45.6 11.8 %collective-permute-start.3 = (f32[29,8,512]{2,1,0:T(8,128)S(1)}, f32[29,8,512]{2,1,0:T(8,128)S(1)}, u32[]{:S(2)}, u32[]{:S(2)}) collective-permute-start(f32[29,8,512]{2,1,0:T(8,128)S(1)} %get-tuple-element.18), channel_id=1, source_target_pairs={{0,1},{1,2},{2,3},{3,4},{4,5},{5,6},{6,7},{9,8},{10,9},{11,10},{12... | collective-permute-start | bytes 1425416 | tf_op jit(solution)/shard_map/ppermute | solution.py:598
  57.3 3.7 %collective-permute-start.4 = (f32[29,8,512]{2,1,0:T(8,128)S(1)}, f32[29,8,512]{2,1,0:T(8,128)S(1)}, u32[]{:S(2)}, u32[]{:S(2)}) collective-permute-start(f32[29,8,512]{2,1,0:T(8,128)S(1)} %collective-permute-done.3.recv_ref), channel_id=1, source_target_pairs={{0,8},{8,0},{16,24},{24,16},{32,40},{40,32},{48,56},{56,48},{64,72... | collective-permute-start | bytes 1425416 | tf_op jit(solution)/shard_map/ppermute | solution.py:599

commit v5 on v4

--- a/solution.py
+++ b/solution.py
@@ -45,10 +45,12 @@
     return hi, (x - hi).astype(jnp.bfloat16).astype(f32)
 
 
-def block_products(left, kernel_ref, out, transposed):
+def block_products(left, kernel_ref, out, transposed, ready=None):
     dims = (((1,), (1 if transposed else 0,)), ((), ()))
     hi, low = split2(left)
     for g in range(left.shape[0] // 8):
+        if ready is not None:
+            ready(g)
         rows = slice(8 * g, 8 * g + 8)
         both = jnp.concatenate([hi[rows], low[rows]], axis=0).astype(jnp.bfloat16)
         right = kernel_ref[2 * g : 2 * g + 2].reshape(2 * BLK, CELLS)
@@ -69,10 +71,56 @@
     return (2 * (brick & 1) + position), brick >> 1
 
 
-def pack_kernel(brick_ref, tile_ref, volume_ref, velocity_ref, kernel_ref, send_ref, left, sums):
+PIECES = 4
+
+
+def pack_kernel(
+    brick_hbm, tile_hbm, volume_hbm, velocity_hbm, kernel_hbm,
+    send_ref,
+    brick_ref, tile_ref, volume_ref, velocity_ref, kernel_ref, left, sums, sem,
+):
     blocks = volume_ref.shape[0]
     chips = send_ref.shape[0] // KEYS
     slots = chips * SLOTS
+    piece = blocks // PIECES
+    small = [
+        pltpu.make_async_copy(src, dst, sem.at[i])
+        for i, (src, dst) in enumerate(
+            (
+                (volume_hbm, volume_ref),
+                (velocity_hbm, velocity_ref),
+                (brick_hbm, brick_ref),
+                (tile_hbm, tile_ref),
+            )
+        )
+    ]
+    large = [
+        pltpu.make_async_copy(
+            kernel_hbm.at[pl.ds(i * piece, piece)],
+            kernel_ref.at[pl.ds(i * piece, piece)],
+            sem.at[len(small) + i],
+        )
+        for i in range(PIECES)
+    ]
+    for copy in small + large:
+        copy.start()
+
+    def ready(g):
+        if (2 * g) % piece == 0:
+            large[2 * g // piece].wait()
+
+    for copy in small:
+        copy.wait()
+    slot, chip = slot_codes(brick_ref[...])
+    code = slot * chips + chip
+    match = iota((slots, blocks), 0) == jnp.broadcast_to(code, (slots, blocks))
+    tile = jnp.broadcast_to(tile_ref[...].astype(f32), (slots, blocks))
+    keys = jnp.sum(jnp.where(match, tile, 0.0), axis=1, keepdims=True)
+    lane = iota((chips, CELLS), 1)
+    row = jnp.zeros((chips, CELLS), f32)
+    for j in range(SLOTS):
+        row = jnp.where(lane == j, keys[j * chips : (j + 1) * chips], row)
+    send_ref[pl.ds(4 * SLOTS, chips, stride=KEYS), :] = row
     odd = (iota((blocks, BLK), 0) & 1) == 1
     volume = volume_ref[...]
     for k in range(4):
@@ -80,10 +128,7 @@
         left[pl.ds(k, blocks, stride=4), :] = jnp.concatenate(
             [jnp.where(odd, 0.0, value), jnp.where(odd, value, 0.0)], axis=1
         )
-    block_products(left[...], kernel_ref, sums, False)
-    slot, chip = slot_codes(brick_ref[...])
-    code = slot * chips + chip
-    match = iota((slots, blocks), 0) == jnp.broadcast_to(code, (slots, blocks))
+    block_products(left[...], kernel_ref, sums, False, ready)
     move = match.astype(f32).astype(jnp.bfloat16)
     for k in range(4):
         total = jnp.zeros((slots, CELLS), f32)
@@ -93,13 +138,6 @@
             send_ref[pl.ds(j * 4 + k, chips, stride=KEYS), :] = total[
                 j * chips : (j + 1) * chips, :
             ]
-    tile = jnp.broadcast_to(tile_ref[...].astype(f32), (slots, blocks))
-    keys = jnp.sum(jnp.where(match, tile, 0.0), axis=1, keepdims=True)
-    lane = iota((chips, CELLS), 1)
-    row = jnp.zeros((chips, CELLS), f32)
-    for j in range(SLOTS):
-        row = jnp.where(lane == j, keys[j * chips : (j + 1) * chips], row)
-    send_ref[pl.ds(4 * SLOTS, chips, stride=KEYS), :] = row
 
 
 def picking(tiles, pick_ref):
@@ -303,7 +341,7 @@
 def solve_kernel(
     core_ref, v_ref, s_ref, face_ref, recv_ref, swap_ref, aux_ref,
     pressure_ref, next_ref, send_ref,
-    v, s, xp, xm, zp, zm, yp, ym, pa, pb, faces, coupled, keep, pick_ref,
+    v, s, xp, xm, zp, zm, yp, ym, pa, pb, faces, coupled, keep, pick_ref, press, sem,
 ):
     core = core_ref[0]
     lane = iota((CZ, CELLS), 1)
@@ -435,7 +473,9 @@
 
     for i in range(CX):
         for q in range(Q):
-            pressure_ref[i, :, lanes(q)] = src[at(DEPTH + core * CX + i, q, CZ)]
+            press[i, :, lanes(q)] = src[at(DEPTH + core * CX + i, q, CZ)]
+    copies = [pltpu.make_async_copy(press, pressure_ref, sem.at[3])]
+    copies[0].start()
     for x in range(XS):
         r = DEPTH + x
         p = [src[at(r, q, CZ)] for q in range(Q)]
@@ -456,7 +496,10 @@
                 keep[a * XS + x, :, lanes(q)] = value
             coupled[put, lanes(3)] = growth
     for a in range(3):
-        next_ref[a] = keep[pl.ds(a * XS + core * CX, CX)]
+        copies.append(
+            pltpu.make_async_copy(keep.at[pl.ds(a * XS + core * CX, CX)], next_ref.at[a], sem.at[a])
+        )
+        copies[-1].start()
 
     chips = pick_ref.shape[0] // SLOTS
     tiles = aux_ref[4 * XS]
@@ -470,6 +513,8 @@
             send_ref[pl.ds(j * 4 + k, chips, stride=4 * SLOTS), :] = total[
                 j * chips : (j + 1) * chips, :
             ]
+    for copy in copies:
+        copy.wait()
 
 
 def drag_kernel(brick_ref, volume_ref, velocity_ref, kernel_ref, back_ref, drag_ref, left, out):
@@ -499,6 +544,7 @@
 
 VMEM = pl.BlockSpec(memory_space=pltpu.VMEM)
 SMEM = pl.BlockSpec(memory_space=pltpu.SMEM)
+HBM = pl.BlockSpec(memory_space=pltpu.HBM)
 
 
 def call(kernel, ins, outs, *args, scratch=(), name=None, grant=4):
@@ -543,14 +589,24 @@
     by_component = jnp.transpose(velocity, (1, 0, 2))
     (send,) = call(
         pack_kernel,
-        [VMEM] * 5,
+        [HBM] * 5,
         [(arr(chips * KEYS, CELLS), VMEM)],
         brick,
         block_tile.reshape(1, blocks),
         volume,
         by_component,
         kernel,
-        scratch=[pltpu.VMEM((4 * blocks, CELLS), f32)] * 2,
+        scratch=[
+            pltpu.VMEM((1, blocks), jnp.int32),
+            pltpu.VMEM((1, blocks), jnp.int32),
+            pltpu.VMEM((blocks, BLK), f32),
+            pltpu.VMEM((3, blocks, BLK), f32),
+            pltpu.VMEM((blocks, BLK, CELLS), f32),
+            pltpu.VMEM((4 * blocks, CELLS), f32),
+            pltpu.VMEM((4 * blocks, CELLS), f32),
+            pltpu.SemaphoreType.DMA((4 + PIECES,)),
+        ],
+        grant=60,
         name="pack",
     )
     recv = exchange(send.reshape(chips * KEYS, 1, CELLS)).reshape(chips * KEYS, CELLS)
@@ -602,8 +658,8 @@
         solve_kernel,
         [SMEM] + [VMEM] * 6,
         [
-            (arr(CX, CZ, NY), VMEM),
-            (arr(3, CX, CZ, NY), VMEM),
+            (arr(CX, CZ, NY), HBM),
+            (arr(3, CX, CZ, NY), HBM),
             (arr(chips * 4 * SLOTS, CELLS), VMEM),
         ],
         core,
@@ -619,6 +675,8 @@
             pltpu.VMEM((XS * 32, 4 * CELLS), f32),
             pltpu.VMEM((3 * XS, CZ, NY), f32),
             pltpu.VMEM((SLOTS * chips, XS * 32), f32),
+            pltpu.VMEM((CX, CZ, NY), f32),
+            pltpu.SemaphoreType.DMA((4,)),
         ],
         name="solve",
         grant=16,

time: 86.2 us -> 84.1 us (0.976)
  local copies, waits for them, and re-layouts: 4.57 us -> 0.03 us
  Pallas kernels: 8.42 us -> 10.7 us
    unnamed x20 -> x10, local copies, waits for them, and re-layouts: 4.57 us -> 0.03 us
    pallas_call x6, Pallas kernels: 8.42 us -> 10.7 us  [call(): pl.pallas_call(kernel, out_shape=[shape for shape, _ in outs], in_specs=i...]
where the time goes in v5:
time: 84.1 us; the launch traced here: 83.7 us
  blocking collectives  40.9 us (49%)
  waiting for transfers between devices  19.4 us (23%)
  starting transfers between devices  11.9 us (14%)
  Pallas kernels  10.7 us (13%)
    all_to_all x2, blocking collectives, exchange(): lax.all_to_all(x, 'wide', split_axis=0, concat_axis=0, tiled=True, axis_i...  40.9 us
    pallas_call x6, Pallas kernels, call(): pl.pallas_call(kernel, out_shape=[shape for shape, _ in outs], in_specs=i...  10.7 us
    ppermute x1, waiting for transfers between devices, local(): recv_z = lax.ppermute(send_z, ('wide', 'narrow'), along_narrow)  8.37 us
    ppermute x1, waiting for transfers between devices, local(): recv_x = lax.ppermute(send_x, 'wide', along_wide)  5.56 us
    ppermute x1, starting transfers between devices, local(): recv_z = lax.ppermute(send_z, ('wide', 'narrow'), along_narrow)  3.38 us
    ppermute x1, starting transfers between devices, local(): recv_x = lax.ppermute(send_x, 'wide', along_wide)  2.83 us
    ppermute x1, waiting for transfers between devices, local(): other = lax.ppermute(part, 'wide', swap)  2.17 us
    ppermute x1, starting transfers between devices, local(): other = lax.ppermute(part, 'wide', swap)  1.92 us
  transfers between devices with their start and end apart: 5, of which 5 were waited for; matrix products, arithmetic and copies ran while one was open for 0% of the time, Pallas kernels for 0%

profile of v5, /device:TPU:264, one launch (start us, length us, event | category | flops | bytes accessed | tf_op | source)
XLA Modules:
  0.0 83.7 jit_solution(11263228940980565444)
XLA Ops:
  0.6 0.0 copy-start.2
  0.6 3.2 %pack.1 = f32[544,128]{1,0:T(8,128)} custom-call(s32[1,64]{1,0:T(1,128)} %bitcast.16, s32[1,64]{1,0:T(1,128)} %bitcast.20, f32[64,64]{1,0:T(8,128)} %volume_ref.1, f32[3,64,64]{2,1,0:T(8,128)} %bitcast.13, f32[64,64,128]{2,1,0:T(8,128)} %kernel_ref.1), custom_call_target="tpu_custom_call" | custom-call | tf_op jit(solution)/shard_map/pack/pallas_call | solution.py:551
  3.9 22.8 %all_to_all.10 = f32[544,1,128]{2,1,0:T(1,128)S(1)} all-to-all(f32[544,1,128]{2,1,0:T(1,128)} %bitcast.18), channel_id=1, replica_groups={{0,16,32,48,64,80,96,112,128,144,160,176,192,208,224,240,256,272,288,30..., dimensions={0} | all-to-all | bytes 557056 | tf_op jit(solution)/shard_map/all_to_all | solution.py:583
  26.7 0.0 copy-done.2
  26.7 0.5 spread.1.own_ref
  27.1 1.9 %collective-permute-start = (f32[45,8,512]{2,1,0:T(8,128)S(1)}, f32[45,8,512]{2,1,0:T(8,128)S(1)}, u32[]{:S(2)}, u32[]{:S(2)}) collective-permute-start(f32[45,8,512]{2,1,0:T(8,128)S(1)} %spread.1.own_ref), channel_id=1, source_target_pairs={{0,8},{8,0},{16,24},{24,16},{32,40},{40,32},{48,56},{56,48},{64,72... | collective-permute-start | bytes 2211848 | tf_op jit(solution)/shard_map/ppermute | solution.py:622
  29.1 2.2 %collective-permute-done.other_ref = f32[45,8,512]{2,1,0:T(8,128)S(1)} collective-permute-done((f32[45,8,512]{2,1,0:T(8,128)S(1)}, f32[45,8,512]{2,1,0:T(8,128)S(1)}, u32[]{:S(2)}, u32[]{:S(2)}) %collective-permute-start) | collective-permute-done | bytes 737312 | tf_op jit(solution)/shard_map/ppermute | solution.py:622
  31.2 0.3 fields.1
  31.5 0.0 copy-start
  31.5 0.0 copy-start.1
  31.5 0.0 copy-start.3
  31.5 0.0 copy-start.4
  31.6 2.8 %collective-permute-start.1 = (f32[16,8,512]{2,1,0:T(8,128)S(1)}, f32[16,8,512]{2,1,0:T(8,128)S(1)}, u32[]{:S(2)}, u32[]{:S(2)}) collective-permute-start(f32[16,8,512]{2,1,0:T(8,128)S(1)} %get-tuple-element.14), channel_id=1, source_target_pairs={{0,16},{16,32},{32,48},{48,64},{64,80},{80,96},{96,112},{112,128},... | collective-permute-start | bytes 786440 | tf_op jit(solution)/shard_map/ppermute | solution.py:637
  34.4 5.6 %collective-permute-done.1.recv_ref = f32[16,8,512]{2,1,0:T(8,128)S(1)} collective-permute-done((f32[16,8,512]{2,1,0:T(8,128)S(1)}, f32[16,8,512]{2,1,0:T(8,128)S(1)}, u32[]{:S(2)}, u32[]{:S(2)}) %collective-permute-start.1) | collective-permute-done | bytes 262176 | tf_op jit(solution)/shard_map/ppermute | solution.py:637
  40.0 1.9 %collective-permute-start.2 = (f32[16,8,512]{2,1,0:T(8,128)S(1)}, f32[16,8,512]{2,1,0:T(8,128)S(1)}, u32[]{:S(2)}, u32[]{:S(2)}) collective-permute-start(f32[16,8,512]{2,1,0:T(8,128)S(1)} %collective-permute-done.1.recv_ref), channel_id=1, source_target_pairs={{0,8},{8,0},{16,24},{24,16},{32,40},{40,32},{48,56},{56,48},{64,72... | collective-permute-start | bytes 786440 | tf_op jit(solution)/shard_map/ppermute | solution.py:638
  41.9 1.5 %collective-permute-done.2.swap_ref = f32[16,8,512]{2,1,0:T(8,128)S(1)} collective-permute-done((f32[16,8,512]{2,1,0:T(8,128)S(1)}, f32[16,8,512]{2,1,0:T(8,128)S(1)}, u32[]{:S(2)}, u32[]{:S(2)}) %collective-permute-start.2) | collective-permute-done | bytes 262176 | tf_op jit(solution)/shard_map/ppermute | solution.py:638
  43.4 0.1 source.1
  43.5 3.4 %collective-permute-start.3 = (f32[29,8,512]{2,1,0:T(8,128)S(1)}, f32[29,8,512]{2,1,0:T(8,128)S(1)}, u32[]{:S(2)}, u32[]{:S(2)}) collective-permute-start(f32[29,8,512]{2,1,0:T(8,128)S(1)} %get-tuple-element.18), channel_id=1, source_target_pairs={{0,1},{1,2},{2,3},{3,4},{4,5},{5,6},{6,7},{9,8},{10,9},{11,10},{12... | collective-permute-start | bytes 1425416 | tf_op jit(solution)/shard_map/ppermute | solution.py:654
  46.9 8.4 %collective-permute-done.3.recv_ref = f32[29,8,512]{2,1,0:T(8,128)S(1)} collective-permute-done((f32[29,8,512]{2,1,0:T(8,128)S(1)}, f32[29,8,512]{2,1,0:T(8,128)S(1)}, u32[]{:S(2)}, u32[]{:S(2)}) %collective-permute-start.3) | collective-permute-done | bytes 475168 | tf_op jit(solution)/shard_map/ppermute | solution.py:654
  55.3 1.9 %collective-permute-start.4 = (f32[29,8,512]{2,1,0:T(8,128)S(1)}, f32[29,8,512]{2,1,0:T(8,128)S(1)}, u32[]{:S(2)}, u32[]{:S(2)}) collective-permute-start(f32[29,8,512]{2,1,0:T(8,128)S(1)} %collective-permute-done.3.recv_ref), channel_id=1, source_target_pairs={{0,8},{8,0},{16,24},{24,16},{32,40},{40,32},{48,56},{56,48},{64,72... | collective-permute-start | bytes 1425416 | tf_op jit(solution)/shard_map/ppermute | solution.py:655
  57.2 1.8 %collective-permute-done.4.swap_ref = f32[29,8,512]{2,1,0:T(8,128)S(1)} collective-permute-done((f32[29,8,512]{2,1,0:T(8,128)S(1)}, f32[29,8,512]{2,1,0:T(8,128)S(1)}, u32[]{:S(2)}, u32[]{:S(2)}) %collective-permute-start.4) | collective-permute-done | bytes 475168 | tf_op jit(solution)/shard_map/ppermute | solution.py:655
  59.0 4.3 %solve.1 = (f32[4,8,512]{2,1,0:T(8,128)}, f32[3,4,8,512]{3,2,1,0:T(8,128)}, f32[512,128]{1,0:T(8,128)S(1)}) custom-call(s32[1]{0:T(128)} %bitcast.2.core_ref, f32[22,8,512]{2,1,0:T(8,128)S(1)} %get-tuple-element.15.v_ref, f32[21,8,512]{2,1,0:T(8,128)S(1)} %get-tuple-element.16.s_ref, f32[6,8,512]{2,1,0:T(8,128)S(1)} %get-tuple-element.17.face_ref, ...), custom_call_target="tpu_custom_call" | custom-call | tf_op jit(solution)/shard_map/solve/pallas_call | solution.py:551
  63.3 18.1 %all_to_all.11 = f32[32,16,128]{2,1,0:T(8,128)S(1)} all-to-all(f32[32,16,128]{2,1,0:T(8,128)S(1)} %bitcast.15), channel_id=1, replica_groups={{0,16,32,48,64,80,96,112,128,144,160,176,192,208,224,240,256,272,288,30..., dimensions={0} | all-to-all | bytes 524288 | tf_op jit(solution)/shard_map/all_to_all | solution.py:583
  81.3 0.0 copy-done
  81.3 0.0 copy-done.1
  81.3 0.0 copy-done.3
  81.3 0.0 copy-done.4
  81.3 2.4 %drag.1 = f32[3,64,64]{2,1,0:T(8,128)} custom-call(s32[1,64]{1,0:T(1,128)S(1)} %bitcast.17, f32[64,64]{1,0:T(8,128)S(1)} %copy-done.3, f32[3,64,64]{2,1,0:T(8,128)S(1)} %bitcast.14, f32[64,64,128]{2,1,0:T(8,128)S(1)} %copy-done, f32[512,128]{1,0:T(8,128)S(1)} %bitcast.12), custom_call_target="tpu_custom_call" | custom-call | tf_op jit(solution)/shard_map/drag/pallas_call | solution.py:551
Async XLA Ops:
  0.6 26.0 %copy-start.2 = (f32[3,4,8,512]{3,2,1,0:T(8,128)S(1)}, f32[3,4,8,512]{3,2,1,0:T(8,128)}, u32[]{:S(2)}) copy-start(f32[3,4,8,512]{3,2,1,0:T(8,128)} %fluid_ref.1) | copy-start | bytes 589828
  27.1 4.1 %collective-permute-start = (f32[45,8,512]{2,1,0:T(8,128)S(1)}, f32[45,8,512]{2,1,0:T(8,128)S(1)}, u32[]{:S(2)}, u32[]{:S(2)}) collective-permute-start(f32[45,8,512]{2,1,0:T(8,128)S(1)} %spread.1.own_ref), channel_id=1, source_target_pairs={{0,8},{8,0},{16,24},{24,16},{32,40},{40,32},{48,56},{56,48},{64,72... | collective-permute-start | bytes 2211848 | tf_op jit(solution)/shard_map/ppermute | solution.py:622
  31.5 49.8 %copy-start = (f32[64,64,128]{2,1,0:T(8,128)S(1)}, f32[64,64,128]{2,1,0:T(8,128)}, u32[]{:S(2)}) copy-start(f32[64,64,128]{2,1,0:T(8,128)} %kernel_ref.1) | copy-start | bytes 6291460
  31.5 49.8 %copy-start.1 = (f32[64,3,64]{2,0,1:T(8,128)S(1)}, f32[64,3,64]{2,0,1:T(8,128)}, u32[]{:S(2)}) copy-start(f32[64,3,64]{2,0,1:T(8,128)} %param.8) | copy-start | bytes 147460
  31.5 49.8 %copy-start.3 = (f32[64,64]{1,0:T(8,128)S(1)}, f32[64,64]{1,0:T(8,128)}, u32[]{:S(2)}) copy-start(f32[64,64]{1,0:T(8,128)} %volume_ref.1) | copy-start | bytes 49156
  31.5 49.8 %copy-start.4 = (s32[64,1]{0,1:T(1,128)S(1)}, s32[64,1]{0,1:T(1,128)}, u32[]{:S(2)}) copy-start(s32[64,1]{0,1:T(1,128)} %param.9) | copy-start | bytes 772
  31.6 8.4 %collective-permute-start.1 = (f32[16,8,512]{2,1,0:T(8,128)S(1)}, f32[16,8,512]{2,1,0:T(8,128)S(1)}, u32[]{:S(2)}, u32[]{:S(2)}) collective-permute-start(f32[16,8,512]{2,1,0:T(8,128)S(1)} %get-tuple-element.14), channel_id=1, source_target_pairs={{0,16},{16,32},{32,48},{48,64},{64,80},{80,96},{96,112},{112,128},... | collective-permute-start | bytes 786440 | tf_op jit(solution)/shard_map/ppermute | solution.py:637
  40.0 3.4 %collective-permute-start.2 = (f32[16,8,512]{2,1,0:T(8,128)S(1)}, f32[16,8,512]{2,1,0:T(8,128)S(1)}, u32[]{:S(2)}, u32[]{:S(2)}) collective-permute-start(f32[16,8,512]{2,1,0:T(8,128)S(1)} %collective-permute-done.1.recv_ref), channel_id=1, source_target_pairs={{0,8},{8,0},{16,24},{24,16},{32,40},{40,32},{48,56},{56,48},{64,72... | collective-permute-start | bytes 786440 | tf_op jit(solution)/shard_map/ppermute | solution.py:638
  43.5 11.8 %collective-permute-start.3 = (f32[29,8,512]{2,1,0:T(8,128)S(1)}, f32[29,8,512]{2,1,0:T(8,128)S(1)}, u32[]{:S(2)}, u32[]{:S(2)}) collective-permute-start(f32[29,8,512]{2,1,0:T(8,128)S(1)} %get-tuple-element.18), channel_id=1, source_target_pairs={{0,1},{1,2},{2,3},{3,4},{4,5},{5,6},{6,7},{9,8},{10,9},{11,10},{12... | collective-permute-start | bytes 1425416 | tf_op jit(solution)/shard_map/ppermute | solution.py:654
  55.3 3.7 %collective-permute-start.4 = (f32[29,8,512]{2,1,0:T(8,128)S(1)}, f32[29,8,512]{2,1,0:T(8,128)S(1)}, u32[]{:S(2)}, u32[]{:S(2)}) collective-permute-start(f32[29,8,512]{2,1,0:T(8,128)S(1)} %collective-permute-done.3.recv_ref), channel_id=1, source_target_pairs={{0,8},{8,0},{16,24},{24,16},{32,40},{40,32},{48,56},{56,48},{64,72... | collective-permute-start | bytes 1425416 | tf_op jit(solution)/shard_map/ppermute | solution.py:655

commit v6 on v5

--- a/solution.py
+++ b/solution.py
@@ -178,8 +178,9 @@
 MSG_X = DEPTH + (DEPTH - 1) + 3
 PACK_V = (((1, 0), (5, 6)), ((2, 0), (4, 5)), ((3, 0), (6, 4)))
 PACK_S = (((1, 0), (3, 5)), ((2, 0), (4, 4), (5, 6)))
-MSG_Z = 2 * XS + 2 * (len(PACK_V) + len(PACK_S)) + 3
-FACES_Z = MSG_Z - 3
+HALF = 2 * CX + len(PACK_V) + len(PACK_S) + 2
+FACES_Z = HALF - 2
+LINES = ROWS_S // 2
 
 
 def place(x, start, to, count):
@@ -190,15 +191,11 @@
 
 
 def packed_rows():
-    tile = 2 * XS
+    tile = 2 * CX
     for plan, reach in ((PACK_V, DEPTH), (PACK_S, DEPTH - 1)):
-        for side in range(2):
-            for group in plan:
-                yield tile, reach, [
-                    (DEPTH - d if side == 0 else DEPTH + XS - 1 + d, line, reach - d)
-                    for d, line in group
-                ]
-                tile += 1
+        for group in plan:
+            yield tile, reach, [(d, line, reach - d) for d, line in group]
+            tile += 1
 
 
 def fields_kernel(core_ref, own_ref, other_ref, field_ref, aux_ref, send_ref, vx, vz):
@@ -268,8 +265,64 @@
         fill(lambda d: d - 1)
 
 
-def source_kernel(core_ref, field_ref, recv_ref, swap_ref, send_ref, face_ref, v, s):
+EDGE = 2 * DEPTH - 1
+
+
+def half_kernel(core_ref, field_ref, recv_ref, up_ref, down_ref):
     core = core_ref[0]
+
+    def fill(half):
+        def source(d):
+            value = recv_ref[DEPTH + d - 1]
+            if d == 1:
+                value = value + (0.5 if half else -0.5) * field_ref[2 * XS + half]
+            return value
+
+        for i in range(CX):
+            x = half * CX + i
+            value = field_ref[XS + x]
+            if x == 0:
+                value = value + 0.5 * recv_ref[EDGE]
+            if x == XS - 1:
+                value = value - 0.5 * recv_ref[EDGE]
+            for ref in (up_ref, down_ref):
+                ref[i] = field_ref[x]
+                ref[CX + i] = value
+        for tile, reach, rows in packed_rows():
+            up = down = None
+            for d, line, count in rows:
+                value = recv_ref[d - 1] if reach == DEPTH else source(d)
+                one, two = place(value, CZ - count, line, count), place(value, 0, line, count)
+                up, down = (one, two) if up is None else (up + one, down + two)
+            up_ref[tile] = up
+            down_ref[tile] = down
+        for f, ref in enumerate((down_ref, up_ref)):
+            ref[FACES_Z + 1] = jnp.zeros((CZ, NY), f32)
+            for line in range(LINES):
+                r = 1 + half * LINES + line
+                if DEPTH <= r < DEPTH + XS:
+                    x = r - DEPTH
+                    value = field_ref[2 * XS + 2 + f, x : x + 1, :]
+                else:
+                    d = r - DEPTH - XS + 1 if half else DEPTH - r
+                    value = recv_ref[2 * DEPTH + f, d - 1 : d, :]
+                ref[FACES_Z + line // 8, line % 8 : line % 8 + 1, :] = value
+
+    @pl.when(core == 0)
+    def _():
+        fill(0)
+
+    @pl.when(core != 0)
+    def _():
+        fill(1)
+
+
+def source_kernel(
+    core_ref, field_ref, recv_ref, swap_ref, low_ref, high_ref, send_ref, face_ref, v, s
+):
+    core = core_ref[0]
+    send_ref[0:HALF] = low_ref[...]
+    send_ref[HALF:] = high_ref[...]
 
     def bring(low, high):
         for d in range(1, DEPTH + 1):
@@ -309,29 +362,6 @@
     def _():
         bring(swap_ref, recv_ref)
 
-    for x in range(XS):
-        send_ref[x] = v[DEPTH + x]
-        send_ref[XS + x] = s[DEPTH + x]
-
-    def fill(up):
-        for tile, reach, rows in packed_rows():
-            ref = v if reach == DEPTH else s
-            total = None
-            for r, line, count in rows:
-                part = place(ref[r], CZ - count if up else 0, line, count)
-                total = part if total is None else total + part
-            send_ref[tile] = total
-        for t in range(3):
-            send_ref[FACES_Z + t] = face_ref[(3 if up else 0) + t]
-
-    @pl.when(core == 0)
-    def _():
-        fill(True)
-
-    @pl.when(core != 0)
-    def _():
-        fill(False)
-
 
 ZE = 3 * CZ
 Q = NY // CELLS
@@ -353,7 +383,7 @@
     def lanes(q):
         return slice(q * CELLS, (q + 1) * CELLS)
 
-    def bring(low, high):
+    def bring(*halves):
         none = jnp.zeros((CZ, CELLS), f32)
         for q in range(Q):
             for r in (0, XE - 1):
@@ -366,25 +396,30 @@
                 v[at(r, q, CZ)] = v_ref[r, :, lanes(q)]
             for i in range(ROWS_S):
                 s[at(i, q, CZ)] = s_ref[i + 1, :, lanes(q)]
-            for x in range(XS):
-                v[at(DEPTH + x, q)] = low[x, :, lanes(q)]
-                v[at(DEPTH + x, q, 2 * CZ)] = high[x, :, lanes(q)]
-                s[at(DEPTH + x - 1, q)] = low[XS + x, :, lanes(q)]
-                s[at(DEPTH + x - 1, q, 2 * CZ)] = high[XS + x, :, lanes(q)]
-            for tile, reach, rows in packed_rows():
-                a, b = low[tile, :, lanes(q)], high[tile, :, lanes(q)]
-                for r, line, count in rows:
-                    ref, i = (v, r) if reach == DEPTH else (s, r - 1)
-                    ref[at(i, q)] = place(a, line, CZ - count, count)
-                    ref[at(i, q, 2 * CZ)] = place(b, line, 0, count)
-        for f, (ref, base) in enumerate(
-            ((face_ref, 0), (face_ref, 3), (low, FACES_Z), (high, FACES_Z))
-        ):
-            for t in range(3):
-                for q in range(Q):
-                    faces[(f * Q + q) * 24 + t * 8 : (f * Q + q) * 24 + t * 8 + 8] = ref[
-                        base + t, :, lanes(q)
-                    ]
+            for half, ref in enumerate(halves):
+                for i in range(CX):
+                    r = DEPTH + half * CX + i
+                    v[at(r, q)] = ref[i, :, lanes(q)]
+                    v[at(r, q, 2 * CZ)] = ref[HALF + i, :, lanes(q)]
+                    s[at(r - 1, q)] = ref[CX + i, :, lanes(q)]
+                    s[at(r - 1, q, 2 * CZ)] = ref[HALF + CX + i, :, lanes(q)]
+                for tile, reach, rows in packed_rows():
+                    a, b = ref[tile, :, lanes(q)], ref[HALF + tile, :, lanes(q)]
+                    for d, line, count in rows:
+                        r = DEPTH + XS - 1 + d if half else DEPTH - d
+                        to, i = (v, r) if reach == DEPTH else (s, r - 1)
+                        to[at(i, q)] = place(a, line, CZ - count, count)
+                        to[at(i, q, 2 * CZ)] = place(b, line, 0, count)
+        for q in range(Q):
+            for f in range(2):
+                for t in range(3):
+                    base = (f * Q + q) * 24 + t * 8
+                    faces[base : base + 8] = face_ref[3 * f + t, :, lanes(q)]
+                for half, ref in enumerate(halves):
+                    base = ((2 + f) * Q + q) * 24 + half * LINES
+                    tile = f * HALF + FACES_Z
+                    faces[base : base + 8] = ref[tile, :, lanes(q)]
+                    faces[base + 8 : base + LINES] = ref[tile + 1, 0 : LINES - 8, lanes(q)]
 
     @pl.when(core == 0)
     def _():
@@ -401,7 +436,7 @@
         downs = [down[0]] + [jnp.where(lane == 0, down[q - 1], down[q]) for q in range(1, Q)]
         return ups, downs
 
-    def weights(r, _):
+    def weights(r):
         i = r - 1
 
         def face(f, q):
@@ -448,11 +483,12 @@
         return 0
 
     for r in range(1, XE - 1):
-        weights(r, 0)
+        weights(r)
 
     def sweep(src, dst, reach):
-        def body(r, _):
-            for z in range(0, ZE, CZ):
+        def body(r):
+            ends = (DEPTH - reach, DEPTH + XS + reach - 1)
+            for z in (CZ,) if r in ends else range(0, ZE, CZ):
                 p = [src[at(r, q, z)] for q in range(Q)]
                 ups, downs = shifted(p)
                 for q in range(Q):
@@ -464,7 +500,7 @@
             return 0
 
         for r in range(DEPTH - reach, DEPTH + XS + reach):
-            body(r, 0)
+            body(r)
 
     src, dst = pa, pb
     for k in range(1, SWEEPS):
@@ -547,14 +583,13 @@
 HBM = pl.BlockSpec(memory_space=pltpu.HBM)
 
 
-def call(kernel, ins, outs, *args, scratch=(), name=None, grant=4):
+def call(kernel, ins, outs, *args, scratch=(), grant=4):
     return pl.pallas_call(
         kernel,
         out_shape=[shape for shape, _ in outs],
         in_specs=ins,
         out_specs=[spec for _, spec in outs],
         scratch_shapes=scratch,
-        name=name,
         compiler_params=pltpu.CompilerParams(vmem_limit_bytes=grant * 1024 * 1024),
     )(*args)
 
@@ -570,13 +605,8 @@
     along_wide = [(w, w + 2) for w in range(0, n_wide - 2, 2)] + [
         (w, w - 2) for w in range(3, n_wide, 2)
     ]
-    along_narrow = [
-        (w * n_narrow + n, w * n_narrow + t)
-        for w in range(n_wide)
-        for n in range(n_narrow)
-        for t in (n + 1 - 2 * (w % 2),)
-        if 0 <= t < n_narrow
-    ]
+    upward = [(n, n + 1) for n in range(n_narrow - 1)]
+    downward = [(t, n) for n, t in upward]
     groups = [list(range(c, n_wide, 2)) for c in range(2)]
 
     def exchange(x):
@@ -607,7 +637,6 @@
             pltpu.SemaphoreType.DMA((4 + PIECES,)),
         ],
         grant=60,
-        name="pack",
     )
     recv = exchange(send.reshape(chips * KEYS, 1, CELLS)).reshape(chips * KEYS, CELLS)
     (part,) = call(
@@ -617,7 +646,6 @@
         recv,
         fluid_velocity,
         scratch=[pltpu.VMEM((SLOTS * chips, XS * 32), f32)],
-        name="spread",
     )
     other = lax.ppermute(part, "wide", swap)
     fields, aux, send_x = call(
@@ -632,15 +660,19 @@
         part,
         other,
         scratch=[pltpu.VMEM((XS, CZ, NY), f32)] * 2,
-        name="fields",
     )
     recv_x = lax.ppermute(send_x, "wide", along_wide)
+    send_up, send_down = call(
+        half_kernel, [SMEM, VMEM, VMEM], [(arr(HALF, CZ, NY), VMEM)] * 2, core, fields, recv_x
+    )
+    from_low = lax.ppermute(send_up, "narrow", upward)
+    from_high = lax.ppermute(send_down, "narrow", downward)
     swap_x = lax.ppermute(recv_x, "wide", swap)
-    send_z, faces, void, source = call(
+    recv_z, faces, void, source = call(
         source_kernel,
-        [SMEM, VMEM, VMEM, VMEM],
+        [SMEM] + [VMEM] * 5,
         [
-            (arr(MSG_Z, CZ, NY), VMEM),
+            (arr(2 * HALF, CZ, NY), VMEM),
             (arr(6, CZ, NY), VMEM),
             (arr(XE, CZ, NY), VMEM),
             (arr(XE - 1, CZ, NY), VMEM),
@@ -649,9 +681,9 @@
         fields,
         recv_x,
         swap_x,
-        name="source",
+        from_low,
+        from_high,
     )
-    recv_z = lax.ppermute(send_z, ("wide", "narrow"), along_narrow)
     swap_z = lax.ppermute(recv_z, "wide", swap)
     region = pltpu.VMEM((XE * Q * ZE + 2 * PAD, CELLS), f32)
     pressure, fluid_next, send_back = call(
@@ -678,7 +710,6 @@
             pltpu.VMEM((CX, CZ, NY), f32),
             pltpu.SemaphoreType.DMA((4,)),
         ],
-        name="solve",
         grant=16,
     )
     back = exchange(send_back.reshape(chips, 4 * SLOTS, CELLS)).reshape(chips * 4 * SLOTS, CELLS)
@@ -692,7 +723,6 @@
         kernel,
         back,
         scratch=[pltpu.VMEM((4 * blocks, CELLS), f32)] * 2,
-        name="drag",
     )
     particle_drag = jnp.transpose(drag, (1, 0, 2))
     return (particle_drag, pressure, fluid_next)

time: 84.1 us -> 87.4 us (1.039)
  the two profiles are of different devices: /device:TPU:264 before, /device:TPU:200 now
where the time goes in v6:
time: 87.4 us; the launch traced here: 87.1 us
  blocking collectives  40.8 us (47%)
  waiting for transfers between devices  18.8 us (22%)
  starting transfers between devices  16 us (18%)
  Pallas kernels  10.6 us (12%)
    all_to_all x2, blocking collectives, exchange(): lax.all_to_all(x, 'wide', split_axis=0, concat_axis=0, tiled=True, axis_i...  40.8 us
    pallas_call x7, Pallas kernels, call(): pl.pallas_call(kernel, out_shape=[shape for shape, _ in outs], in_specs=i...  10.6 us
    ppermute x1, waiting for transfers between devices, local(): recv_x = lax.ppermute(send_x, 'wide', along_wide)  5.55 us
    ppermute x1, waiting for transfers between devices, local(): from_high = lax.ppermute(send_down, 'narrow', downward)  5.51 us
    ppermute x1, starting transfers between devices, local(): from_low = lax.ppermute(send_up, 'narrow', upward)  5.49 us
    ppermute x1, waiting for transfers between devices, local(): from_low = lax.ppermute(send_up, 'narrow', upward)  3.75 us
    ppermute x1, starting transfers between devices, local(): recv_x = lax.ppermute(send_x, 'wide', along_wide)  2.71 us
    ppermute x1, waiting for transfers between devices, local(): other = lax.ppermute(part, 'wide', swap)  2.17 us
  transfers between devices with their start and end apart: 6, of which 5 were waited for; matrix products, arithmetic and copies ran while one was open for 0% of the time, Pallas kernels for 0%

profile of v6, /device:TPU:200, one launch (start us, length us, event | category | flops | bytes accessed | tf_op | source)
XLA Modules:
  0.0 87.1 jit_solution(10645228377593878209)
XLA Ops:
  0.6 0.0 copy-start.2
  0.6 3.2 %shard_map.85 = f32[544,128]{1,0:T(8,128)} custom-call(s32[1,64]{1,0:T(1,128)} %bitcast.16, s32[1,64]{1,0:T(1,128)} %bitcast.20, f32[64,64]{1,0:T(8,128)} %volume_ref.1, f32[3,64,64]{2,1,0:T(8,128)} %bitcast.13, f32[64,64,128]{2,1,0:T(8,128)} %kernel_ref.1), custom_call_target="tpu_custom_call" | custom-call | tf_op jit(solution)/shard_map/pallas_call | solution.py:587
  3.9 22.8 %all_to_all.10 = f32[544,1,128]{2,1,0:T(1,128)S(1)} all-to-all(f32[544,1,128]{2,1,0:T(1,128)} %bitcast.18), channel_id=1, replica_groups={{0,16,32,48,64,80,96,112,128,144,160,176,192,208,224,240,256,272,288,30..., dimensions={0} | all-to-all | bytes 557056 | tf_op jit(solution)/shard_map/all_to_all | solution.py:613
  26.7 0.0 copy-done.2
  26.7 0.5 shard_map.86.own_ref
  27.1 1.9 %collective-permute-start = (f32[45,8,512]{2,1,0:T(8,128)S(1)}, f32[45,8,512]{2,1,0:T(8,128)S(1)}, u32[]{:S(2)}, u32[]{:S(2)}) collective-permute-start(f32[45,8,512]{2,1,0:T(8,128)S(1)} %shard_map.86.own_ref), channel_id=1, source_target_pairs={{0,8},{8,0},{16,24},{24,16},{32,40},{40,32},{48,56},{56,48},{64,72... | collective-permute-start | bytes 2211848 | tf_op jit(solution)/shard_map/ppermute | solution.py:650
  29.1 2.2 %collective-permute-done.other_ref = f32[45,8,512]{2,1,0:T(8,128)S(1)} collective-permute-done((f32[45,8,512]{2,1,0:T(8,128)S(1)}, f32[45,8,512]{2,1,0:T(8,128)S(1)}, u32[]{:S(2)}, u32[]{:S(2)}) %collective-permute-start) | collective-permute-done | bytes 737312 | tf_op jit(solution)/shard_map/ppermute | solution.py:650
  31.2 0.3 shard_map.87
  31.5 2.7 %collective-permute-start.1 = (f32[16,8,512]{2,1,0:T(8,128)S(1)}, f32[16,8,512]{2,1,0:T(8,128)S(1)}, u32[]{:S(2)}, u32[]{:S(2)}) collective-permute-start(f32[16,8,512]{2,1,0:T(8,128)S(1)} %get-tuple-element.16), channel_id=1, source_target_pairs={{0,16},{16,32},{32,48},{48,64},{64,80},{80,96},{96,112},{112,128},... | collective-permute-start | bytes 786440 | tf_op jit(solution)/shard_map/ppermute | solution.py:664
  34.2 5.6 %collective-permute-done.1.recv_ref = f32[16,8,512]{2,1,0:T(8,128)S(1)} collective-permute-done((f32[16,8,512]{2,1,0:T(8,128)S(1)}, f32[16,8,512]{2,1,0:T(8,128)S(1)}, u32[]{:S(2)}, u32[]{:S(2)}) %collective-permute-start.1) | collective-permute-done | bytes 262176 | tf_op jit(solution)/shard_map/ppermute | solution.py:664
  39.8 1.9 %collective-permute-start.2 = (f32[16,8,512]{2,1,0:T(8,128)S(1)}, f32[16,8,512]{2,1,0:T(8,128)S(1)}, u32[]{:S(2)}, u32[]{:S(2)}) collective-permute-start(f32[16,8,512]{2,1,0:T(8,128)S(1)} %collective-permute-done.1.recv_ref), channel_id=1, source_target_pairs={{0,8},{8,0},{16,24},{24,16},{32,40},{40,32},{48,56},{56,48},{64,72... | collective-permute-start | bytes 786440 | tf_op jit(solution)/shard_map/ppermute | solution.py:670
  41.7 0.1 shard_map.88
  41.8 5.5 %collective-permute-start.3 = (f32[15,8,512]{2,1,0:T(8,128)S(1)}, f32[15,8,512]{2,1,0:T(8,128)S(1)}, u32[]{:S(2)}, u32[]{:S(2)}) collective-permute-start(f32[15,8,512]{2,1,0:T(8,128)S(1)} %get-tuple-element.17), channel_id=1, source_target_pairs={{0,1},{1,2},{2,3},{3,4},{4,5},{5,6},{6,7},{8,9},{9,10},{10,11},{11... | collective-permute-start | bytes 737288 | tf_op jit(solution)/shard_map/ppermute | solution.py:668
  47.3 0.0 copy-start
  47.3 0.0 copy-start.1
  47.3 0.0 copy-start.3
  47.3 0.0 copy-start.4
  47.3 2.1 %collective-permute-start.4 = (f32[15,8,512]{2,1,0:T(8,128)S(1)}, f32[15,8,512]{2,1,0:T(8,128)S(1)}, u32[]{:S(2)}, u32[]{:S(2)}) collective-permute-start(f32[15,8,512]{2,1,0:T(8,128)S(1)} %get-tuple-element.18), channel_id=1, source_target_pairs={{1,0},{2,1},{3,2},{4,3},{5,4},{6,5},{7,6},{9,8},{10,9},{11,10},{12... | collective-permute-start | bytes 737288 | tf_op jit(solution)/shard_map/ppermute | solution.py:669
  49.4 3.7 %collective-permute-done.3.low_ref = f32[15,8,512]{2,1,0:T(8,128)S(1)} collective-permute-done((f32[15,8,512]{2,1,0:T(8,128)S(1)}, f32[15,8,512]{2,1,0:T(8,128)S(1)}, u32[]{:S(2)}, u32[]{:S(2)}) %collective-permute-start.3) | collective-permute-done | bytes 245792 | tf_op jit(solution)/shard_map/ppermute | solution.py:668
  53.1 5.5 %collective-permute-done.4.high_ref = f32[15,8,512]{2,1,0:T(8,128)S(1)} collective-permute-done((f32[15,8,512]{2,1,0:T(8,128)S(1)}, f32[15,8,512]{2,1,0:T(8,128)S(1)}, u32[]{:S(2)}, u32[]{:S(2)}) %collective-permute-start.4) | collective-permute-done | bytes 245792 | tf_op jit(solution)/shard_map/ppermute | solution.py:669
  58.6 0.0 collective-permute-done.2.swap_ref
  58.6 0.1 shard_map.89
  58.7 1.9 %collective-permute-start.5 = (f32[30,8,512]{2,1,0:T(8,128)S(1)}, f32[30,8,512]{2,1,0:T(8,128)S(1)}, u32[]{:S(2)}, u32[]{:S(2)}) collective-permute-start(f32[30,8,512]{2,1,0:T(8,128)S(1)} %get-tuple-element.22.recv_ref), channel_id=1, source_target_pairs={{0,8},{8,0},{16,24},{24,16},{32,40},{40,32},{48,56},{56,48},{64,72... | collective-permute-start | bytes 1474568 | tf_op jit(solution)/shard_map/ppermute | solution.py:687
  60.7 1.8 %collective-permute-done.5.swap_ref = f32[30,8,512]{2,1,0:T(8,128)S(1)} collective-permute-done((f32[30,8,512]{2,1,0:T(8,128)S(1)}, f32[30,8,512]{2,1,0:T(8,128)S(1)}, u32[]{:S(2)}, u32[]{:S(2)}) %collective-permute-start.5) | collective-permute-done | bytes 491552 | tf_op jit(solution)/shard_map/ppermute | solution.py:687
  62.5 4.1 %shard_map.90 = (f32[4,8,512]{2,1,0:T(8,128)}, f32[3,4,8,512]{3,2,1,0:T(8,128)}, f32[512,128]{1,0:T(8,128)S(1)}) custom-call(s32[1]{0:T(128)} %bitcast.2.core_ref, f32[22,8,512]{2,1,0:T(8,128)S(1)} %get-tuple-element.19.v_ref, f32[21,8,512]{2,1,0:T(8,128)S(1)} %get-tuple-element.20.s_ref, f32[6,8,512]{2,1,0:T(8,128)S(1)} %get-tuple-element.21.face_ref, ...), custom_call_target="tpu_custom_call" | custom-call | tf_op jit(solution)/shard_map/pallas_call | solution.py:587
  66.6 18.1 %all_to_all.11 = f32[32,16,128]{2,1,0:T(8,128)S(1)} all-to-all(f32[32,16,128]{2,1,0:T(8,128)S(1)} %bitcast.15), channel_id=1, replica_groups={{0,16,32,48,64,80,96,112,128,144,160,176,192,208,224,240,256,272,288,30..., dimensions={0} | all-to-all | bytes 524288 | tf_op jit(solution)/shard_map/all_to_all | solution.py:613
  84.7 0.0 copy-done
  84.7 0.0 copy-done.1
  84.7 0.0 copy-done.3
  84.7 0.0 copy-done.4
  84.7 2.4 %shard_map.91 = f32[3,64,64]{2,1,0:T(8,128)} custom-call(s32[1,64]{1,0:T(1,128)S(1)} %bitcast.17, f32[64,64]{1,0:T(8,128)S(1)} %copy-done.3, f32[3,64,64]{2,1,0:T(8,128)S(1)} %bitcast.14, f32[64,64,128]{2,1,0:T(8,128)S(1)} %copy-done, f32[512,128]{1,0:T(8,128)S(1)} %bitcast.12), custom_call_target="tpu_custom_call" | custom-call | tf_op jit(solution)/shard_map/pallas_call | solution.py:587
Async XLA Ops:
  0.6 26.0 %copy-start.2 = (f32[3,4,8,512]{3,2,1,0:T(8,128)S(1)}, f32[3,4,8,512]{3,2,1,0:T(8,128)}, u32[]{:S(2)}) copy-start(f32[3,4,8,512]{3,2,1,0:T(8,128)} %fluid_ref.1) | copy-start | bytes 589828
  27.1 4.1 %collective-permute-start = (f32[45,8,512]{2,1,0:T(8,128)S(1)}, f32[45,8,512]{2,1,0:T(8,128)S(1)}, u32[]{:S(2)}, u32[]{:S(2)}) collective-permute-start(f32[45,8,512]{2,1,0:T(8,128)S(1)} %shard_map.86.own_ref), channel_id=1, source_target_pairs={{0,8},{8,0},{16,24},{24,16},{32,40},{40,32},{48,56},{56,48},{64,72... | collective-permute-start | bytes 2211848 | tf_op jit(solution)/shard_map/ppermute | solution.py:650
  31.5 8.3 %collective-permute-start.1 = (f32[16,8,512]{2,1,0:T(8,128)S(1)}, f32[16,8,512]{2,1,0:T(8,128)S(1)}, u32[]{:S(2)}, u32[]{:S(2)}) collective-permute-start(f32[16,8,512]{2,1,0:T(8,128)S(1)} %get-tuple-element.16), channel_id=1, source_target_pairs={{0,16},{16,32},{32,48},{48,64},{64,80},{80,96},{96,112},{112,128},... | collective-permute-start | bytes 786440 | tf_op jit(solution)/shard_map/ppermute | solution.py:664
  39.8 18.8 %collective-permute-start.2 = (f32[16,8,512]{2,1,0:T(8,128)S(1)}, f32[16,8,512]{2,1,0:T(8,128)S(1)}, u32[]{:S(2)}, u32[]{:S(2)}) collective-permute-start(f32[16,8,512]{2,1,0:T(8,128)S(1)} %collective-permute-done.1.recv_ref), channel_id=1, source_target_pairs={{0,8},{8,0},{16,24},{24,16},{32,40},{40,32},{48,56},{56,48},{64,72... | collective-permute-start | bytes 786440 | tf_op jit(solution)/shard_map/ppermute | solution.py:670
  41.8 11.4 %collective-permute-start.3 = (f32[15,8,512]{2,1,0:T(8,128)S(1)}, f32[15,8,512]{2,1,0:T(8,128)S(1)}, u32[]{:S(2)}, u32[]{:S(2)}) collective-permute-start(f32[15,8,512]{2,1,0:T(8,128)S(1)} %get-tuple-element.17), channel_id=1, source_target_pairs={{0,1},{1,2},{2,3},{3,4},{4,5},{5,6},{6,7},{8,9},{9,10},{10,11},{11... | collective-permute-start | bytes 737288 | tf_op jit(solution)/shard_map/ppermute | solution.py:668
  47.3 37.4 %copy-start = (f32[64,64,128]{2,1,0:T(8,128)S(1)}, f32[64,64,128]{2,1,0:T(8,128)}, u32[]{:S(2)}) copy-start(f32[64,64,128]{2,1,0:T(8,128)} %kernel_ref.1) | copy-start | bytes 6291460
  47.3 37.4 %copy-start.1 = (f32[64,3,64]{2,0,1:T(8,128)S(1)}, f32[64,3,64]{2,0,1:T(8,128)}, u32[]{:S(2)}) copy-start(f32[64,3,64]{2,0,1:T(8,128)} %param.8) | copy-start | bytes 147460
  47.3 37.4 %copy-start.3 = (f32[64,64]{1,0:T(8,128)S(1)}, f32[64,64]{1,0:T(8,128)}, u32[]{:S(2)}) copy-start(f32[64,64]{1,0:T(8,128)} %volume_ref.1) | copy-start | bytes 49156
  47.3 37.4 %copy-start.4 = (s32[64,1]{0,1:T(1,128)S(1)}, s32[64,1]{0,1:T(1,128)}, u32[]{:S(2)}) copy-start(s32[64,1]{0,1:T(1,128)} %param.9) | copy-start | bytes 772
  47.3 11.3 %collective-permute-start.4 = (f32[15,8,512]{2,1,0:T(8,128)S(1)}, f32[15,8,512]{2,1,0:T(8,128)S(1)}, u32[]{:S(2)}, u32[]{:S(2)}) collective-permute-start(f32[15,8,512]{2,1,0:T(8,128)S(1)} %get-tuple-element.18), channel_id=1, source_target_pairs={{1,0},{2,1},{3,2},{4,3},{5,4},{6,5},{7,6},{9,8},{10,9},{11,10},{12... | collective-permute-start | bytes 737288 | tf_op jit(solution)/shard_map/ppermute | solution.py:669
  58.7 3.8 %collective-permute-start.5 = (f32[30,8,512]{2,1,0:T(8,128)S(1)}, f32[30,8,512]{2,1,0:T(8,128)S(1)}, u32[]{:S(2)}, u32[]{:S(2)}) collective-permute-start(f32[30,8,512]{2,1,0:T(8,128)S(1)} %get-tuple-element.22.recv_ref), channel_id=1, source_target_pairs={{0,8},{8,0},{16,24},{24,16},{32,40},{40,32},{48,56},{56,48},{64,72... | collective-permute-start | bytes 1474568 | tf_op jit(solution)/shard_map/ppermute | solution.py:687
